TPU v7x, 256 devices: a whole 4x4x8 slice. The times are simulated.
256 devices in a mesh: ctx: 8 (over z), head: 32 (over y, x, core).
Axes of the slice: x: 4, y: 4, z: 8, core: 2. Of those that a mesh axis runs over, the one named last changes fastest.
Arguments:
- hidden: float32 [2048, 2304], P(('ctx', 'head')), may hold values from -40 to 40
- w_query: float32 [2304, 6144], P(None, 'head'), may hold values from -0.125 to 0.125
- w_down: float32 [2304, 576], replicated, may hold values from -0.125 to 0.125
- latent_gain: float32 [512], replicated, may hold values from 0.25 to 1.75
- w_key_up: float32 [512, 4096], P(None, 'head'), may hold values from -0.25 to 0.25
- w_value_up: float32 [512, 4096], P(None, 'head'), may hold values from -0.25 to 0.25
- w_out: float32 [4096, 2304], P('head'), may hold values from -0.09375 to 0.09375
Outputs:
- output: float32 [2048, 2304], P(('ctx', 'head'))
All inputs are finite; a program needn't handle non-finite values.
Results may differ from a plain program's by a relative error of at most 0.0003.
Values sent between devices are 32-bit elements; how exact they have to be, the bound alone decides.
No kernel may reach another device: no remote copies, remote signals or barrier semaphores. Data moves between devices by JAX's collectives and lax.ppermute only.
A program may use at most 64 MiB of HBM per device.

v0:
```python
import jax
import jax.numpy as jnp
from jax import lax
from jax.sharding import PartitionSpec as P

EXACT = lax.Precision.HIGHEST
EPSILON = 1e-06
FLOOR = -1e30


def in_order(pieces, dim):
    pieces = jnp.moveaxis(pieces, 0, dim)
    shape = pieces.shape
    return pieces.reshape(*shape[:dim], shape[dim] * shape[dim + 1], *shape[dim + 2 :])


def copy_for_each(array, axis):
    copies = jnp.broadcast_to(array, (lax.axis_size(axis), *array.shape))
    return lax.all_to_all(copies, axis, split_axis=0, concat_axis=0, tiled=True)


def gather_directly(array, axis, dim):
    return in_order(copy_for_each(array, axis), dim)


def in_blocks(array, dim, size):
    shape = array.shape
    pieces = array.reshape(*shape[:dim], size, shape[dim] // size, *shape[dim + 1 :])
    return jnp.moveaxis(pieces, dim, 0)


def summed_on_arrival(array, axis, dim):
    pieces = in_blocks(array, dim, lax.axis_size(axis))
    arrived = lax.all_to_all(pieces, axis, split_axis=0, concat_axis=0, tiled=True)
    return arrived.sum(axis=0)


def matmul(left, right):
    return jnp.dot(left, right, precision=EXACT, preferred_element_type=jnp.float32)


def on_device(hidden, w_query, w_down, latent_gain, w_key_up, w_value_up, w_out):
    rank = w_key_up.shape[0]
    nope = w_key_up.shape[1]
    down_part = matmul(hidden, w_down)
    raw_latent = down_part[:, :rank]
    meansq = jnp.mean(raw_latent * raw_latent, axis=-1, keepdims=True)
    own_latent = jnp.concatenate(
        [raw_latent * lax.rsqrt(meansq + EPSILON) * latent_gain, down_part[:, rank:]], axis=1
    )
    latent_block = gather_directly(own_latent, "head", 0)
    queries = matmul(lax.all_gather(hidden, "head", axis=0, tiled=True), w_query)
    row_count = queries.shape[0]
    score_scale = queries.shape[1] ** (-0.5)
    query_pos = lax.axis_index("ctx") * row_count + jnp.arange(row_count, dtype=jnp.int32)
    latent_part = latent_block[:, :rank]
    projected = jnp.concatenate(
        [matmul(latent_part, w_key_up), latent_block[:, rank:], matmul(latent_part, w_value_up)],
        axis=1,
    )
    shared_end = nope + latent_block.shape[1] - rank
    portion = lax.all_gather(projected, "ctx", axis=0, tiled=True)
    key_own = portion[:, :nope]
    maxima = jnp.full((row_count,), FLOOR, jnp.float32)
    scores = (
        matmul(queries[:, :nope], key_own.T)
        + matmul(queries[:, nope:], portion[:, nope:shared_end].T)
    ) * score_scale
    key_pos = jnp.arange(key_own.shape[0], dtype=jnp.int32)
    causal = query_pos[:, None] >= key_pos[None, :]
    scores = jnp.where(causal, scores, FLOOR)
    new_max = jnp.maximum(maxima, jnp.max(scores, axis=1))
    weights = jnp.where(causal, jnp.exp(scores - new_max[:, None]), 0.0)
    attended = matmul(weights, portion[:, shared_end:]) / jnp.sum(weights, axis=1)[:, None]
    return summed_on_arrival(matmul(attended, w_out), "head", 0)


def solution(mesh):
    placed = (
        P(("ctx", "head"), None),
        P(None, "head"),
        P(),
        P(),
        P(None, "head"),
        P(None, "head"),
        P("head", None),
    )
    return jax.shard_map(
        on_device, mesh=mesh, in_specs=placed, out_specs=P(("ctx", "head"), None), check_vma=False
    )
```

profile of v0, /device:TPU:1, one launch (start us, length us, event | category | flops | bytes accessed | tf_op | source)
XLA Modules:
  0.0 167.0 jit_solution(1022464244086564012)
XLA Ops:
  6.5 0.0 copy-start
  6.5 0.7 all-gather.3.cloned.1.call-update
  7.3 0.0 all-gather.5.cloned.1.call-start
  7.3 6.9 %fusion.21 = f32[8,576]{1,0:T(8,128)S(1)} fusion(f32[8,2304]{1,0:T(8,128)} %param.7, f32[2304,576]{0,1:T(8,128)} %param.9), kind=kOutput, calls=%fused_computation.32 | convolution fusion | flops 127401984 | bytes 5400576 | tf_op jit(solution)/shard_map/dot_general | solution.py:39
  14.2 0.1 multiply_reduce_fusion
  14.3 0.0 copy-done.5
  14.4 0.1 multiply_multiply_fusion
  14.5 22.0 %all_to_all.10 = f32[32,8,576]{2,1,0:T(8,128)S(1)} all-to-all(f32[32,8,576]{2,1,0:T(8,128)S(1)} %broadcast_in_dim.19), channel_id=1, replica_groups=mesh['ctx'=8,'head'=32] {'head'}, dimensions={0} | all-to-all | bytes 1179648 | tf_op jit(solution)/shard_map/all_to_all | solution.py:19
  36.5 0.1 copy.10
  36.6 0.6 fusion.12
  37.2 0.6 fusion.14
  37.8 0.8 pad_maximum_fusion
  38.6 0.0 all-gather.5.cloned.1.call-update
  38.6 26.6 %all-gather.3.cloned.1.call-done = f32[256,2304]{1,0:T(8,128)} async-done(((f32[8,2304]{1,0:T(8,128)}), f32[256,2304]{1,0:T(8,128)}) %all-gather.3.cloned.1.call-update) | async-done | bytes 2359312 | tf_op jit(solution)/shard_map/all_gather | solution.py:52
  65.3 4.1 %fusion.20 = f32[256,192]{0,1:T(8,128)S(1)} fusion(f32[256,2304]{1,0:T(8,128)} %all-gather.3.cloned.1.call-done, f32[2304,192]{0,1:T(8,128)S(1)} %copy-done), kind=kOutput, calls=%fused_computation.31 | convolution fusion | flops 1358954496 | bytes 4325376 | tf_op jit(solution)/shard_map/dot_general | solution.py:39
  69.4 36.0 %all-gather.5.cloned.1.call-done = f32[2048,320]{0,1:T(8,128)} async-done(((f32[256,320]{0,1:T(8,128)}), f32[2048,320]{0,1:T(8,128)}) %all-gather.5.cloned.1.call-update) | async-done | bytes 2621456 | tf_op jit(solution)/shard_map/all_gather | solution.py:62
  105.5 3.2 %fusion.6 = f32[256,2048]{1,0:T(8,128)S(1)} fusion(f32[2048,320]{0,1:T(8,128)} %all-gather.5.cloned.1.call-done, f32[256,192]{0,1:T(8,128)S(1)} %fusion.20), kind=kOutput, calls=%fused_computation.10 | convolution fusion | flops 805306368 | bytes 3276800 | tf_op jit(solution)/shard_map/dot_general | solution.py:39
  108.7 2.3 %fusion.19 = (f32[256]{0:T(256)S(1)}, f32[256,2048]{1,0:T(8,128)S(1)}) fusion(f32[256,2048]{1,0:T(8,128)S(1)} %fusion.6, f32[2048,320]{0,1:T(8,128)S(1)} %copy-done.2, f32[256,192]{0,1:T(8,128)S(1)} %fusion.20, s32[256]{0:T(256)S(1)} %iota_add_fusion), kind=kOutput, calls=%fused_computation.30 | convolution fusion | flops 405274368 | bytes 4786176 | tf_op jit(solution)/shard_map/dot_general | solution.py:39
  111.0 0.6 fusion.2
  111.6 0.0 copy-start.1
  111.7 2.2 %fusion.4 = f32[256,128]{1,0:T(8,128)S(1)} fusion(f32[256,2048]{1,0:T(8,128)S(1)} %get-tuple-element.6, f32[2048,320]{0,1:T(8,128)S(1)} %copy-done.2, f32[256]{0:T(256)S(1)} %broadcast_maximum_fusion, s32[256]{0:T(256)S(1)} %iota_add_fusion, f32[256]{0:T(256)S(1)} %fusion.2), kind=kOutput, calls=%fused_computation.8 | convolution fusion | flops 806912000 | bytes 3279872 | tf_op jit(solution)/shard_map/dot_general | solution.py:39
  113.9 2.0 %convolution_bitcast_fusion = f32[32,8,2304]{2,1,0:T(8,128)S(1)} fusion(f32[256,128]{1,0:T(8,128)S(1)} %fusion.4, f32[128,2304]{1,0:T(8,128)S(1)} %copy-done.1), kind=kOutput, calls=%fused_computation | convolution fusion | flops 905969664 | bytes 3670016 | tf_op jit(solution)/shard_map/dot_general | solution.py:39
  115.9 41.8 %all_to_all.11 = f32[32,8,2304]{2,1,0:T(8,128)} all-to-all(f32[32,8,2304]{2,1,0:T(8,128)S(1)} %convolution_bitcast_fusion), channel_id=1, replica_groups=mesh['ctx'=8,'head'=32] {'head'}, dimensions={0} | all-to-all | bytes 4718592 | tf_op jit(solution)/shard_map/all_to_all | solution.py:34
  157.7 2.4 %reduce_sum.29 = f32[8,2304]{1,0:T(8,128)} reduce(f32[32,8,2304]{2,1,0:T(8,128)} %all_to_all.11, f32[]{:T(128)} %constant.5.clone.1), dimensions={0}, to_apply=%region_3.4 | reduce | flops 571392 | bytes 2433028 | tf_op jit(solution)/shard_map/reduce_sum | solution.py:35
  (17 shorter events, 0.1 us)
Async XLA Ops:
  6.5 58.8 %copy-start = (f32[2304,192]{0,1:T(8,128)S(1)}, f32[2304,192]{0,1:T(8,128)}, u32[]{:S(2)}) copy-start(f32[2304,192]{0,1:T(8,128)} %param.8) | copy-start | bytes 5308420
  6.5 58.8 %all-gather.3.cloned.1.call-start = ((), (), s32[]{:S(2)}) async-start(), calls=%async_computation.2 | async-start | bytes 2433024 | tf_op jit(solution)/shard_map/all_gather | solution.py:52
  7.3 7.1 %copy-start.5 = (f32[512]{0:T(512)S(1)}, f32[512]{0:T(512)}, u32[]{:S(2)}) copy-start(f32[512]{0:T(512)} %param.10) | copy-start | bytes 6148
  7.3 98.2 %all-gather.5.cloned.1.call-start = ((), (), s32[]{:S(2)}) async-start(), calls=%async_computation.3 | async-start | bytes 2949120 | tf_op jit(solution)/shard_map/all_gather | solution.py:62
  14.2 22.4 %copy-start.3 = (f32[512,128]{1,0:T(8,128)S(1)}, f32[512,128]{1,0:T(8,128)}, u32[]{:S(2)}) copy-start(f32[512,128]{1,0:T(8,128)} %param.12) | copy-start | bytes 786436
  14.2 23.1 %copy-start.4 = (f32[512,128]{1,0:T(8,128)S(1)}, f32[512,128]{1,0:T(8,128)}, u32[]{:S(2)}) copy-start(f32[512,128]{1,0:T(8,128)} %param.11) | copy-start | bytes 786436
  105.5 3.2 %copy-start.2 = (f32[2048,320]{0,1:T(8,128)S(1)}, f32[2048,320]{0,1:T(8,128)}, u32[]{:S(2)}) copy-start(f32[2048,320]{0,1:T(8,128)} %all-gather.5.cloned.1.call-done) | copy-start | bytes 7864324
  111.6 2.2 %copy-start.1 = (f32[128,2304]{1,0:T(8,128)S(1)}, f32[128,2304]{1,0:T(8,128)}, u32[]{:S(2)}) copy-start(f32[128,2304]{1,0:T(8,128)} %param.13) | copy-start | bytes 3538948
Sparse Core Ops, SparseCore 0:
  9.9 55.3 all-gather.2
  67.1 38.3 all-gather.4
where the time goes:
time: 167 us
  blocking collectives  63.9 us (38%)
  waiting for transfers between devices  63.4 us (38%)
  matrix products  21.9 us (13%)
  between operations  13.5 us (8%)
  other arithmetic  4.02 us (2%)
    all_to_all x1, blocking collectives, summed_on_arrival(): lax.all_to_all(pieces, axis, split_axis=0, concat_axis=0, tiled=True)  41.8 us
    all_gather x1, waiting for transfers between devices, on_device(): portion = lax.all_gather(projected, 'ctx', axis=0, tiled=True)  36 us
    all_gather x1, waiting for transfers between devices, on_device(): lax.all_gather(hidden, 'head', axis=0, tiled=True)  26.6 us
    all_to_all x1, blocking collectives, copy_for_each(): return lax.all_to_all(copies, axis, split_axis=0, concat_axis=0, tiled=True)  22 us
    dot_general x8, matrix products, matmul(): jnp.dot(left, right, precision=EXACT, preferred_element_type=jnp.float32)  21.9 us
  transfers between devices with their start and end apart: 2, of which 2 were waited for; matrix products, arithmetic and copies ran while one was open for 8% of the time, Pallas kernels for 0%

commit v1 on v0

v1 whole, which is shorter than its diff:
```python
import functools

import jax
import jax.numpy as jnp
from jax import lax
from jax.experimental import pallas as pl
from jax.experimental.pallas import tpu as pltpu
from jax.sharding import PartitionSpec as P

EXACT = lax.Precision.HIGHEST
EPSILON = 1e-06
FLOOR = -1e30
VMEM = pltpu.VMEM


def dot_nn(left, right):
    return lax.dot_general(
        left, right, (((1,), (0,)), ((), ())), precision=EXACT, preferred_element_type=jnp.float32
    )


def dot_nt(left, right):
    return lax.dot_general(
        left, right, (((1,), (1,)), ((), ())), precision=EXACT, preferred_element_type=jnp.float32
    )


def call(kernel, out_shape, *operands, name):
    return pl.pallas_call(
        kernel,
        out_shape=jax.ShapeDtypeStruct(out_shape, jnp.float32),
        in_specs=[pl.BlockSpec(memory_space=VMEM)] * len(operands),
        out_specs=pl.BlockSpec(memory_space=VMEM),
        compiler_params=pltpu.CompilerParams(vmem_limit_bytes=48 << 20),
        name=name,
    )(*operands)


def latent_kernel(x_ref, down_ref, gain_ref, out_ref):
    rank = gain_ref.shape[1]
    down = dot_nt(x_ref[...], down_ref[...])
    raw = down[:, :rank]
    meansq = jnp.mean(raw * raw, axis=-1, keepdims=True)
    out_ref[:, :rank] = raw * lax.rsqrt(meansq + EPSILON) * gain_ref[...]
    out_ref[:, rank:] = down[:, rank:]


def query_kernel(x_ref, own_ref, other_ref, out_ref):
    out_ref[0] = dot_nt(x_ref[...], own_ref[...])
    out_ref[1] = dot_nt(x_ref[...], other_ref[...])


def token_offset(index, cls, rows, half):
    within = lax.rem(index, half)
    return (within // rows * 2 + cls) * rows + lax.rem(within, rows)


def attend_kernel(rows, scale, blocks, pieces, fresh, place_ref, *refs):
    query_ref, key_ref, value_ref, far_key_ref, far_value_ref = refs[:5]
    latent_refs = refs[5 : 5 + len(pieces)]
    out_ref = refs[-1]
    ctx, core = place_ref[0], place_ref[1]
    rank = key_ref.shape[0]
    nope = key_ref.shape[1]
    vdim = value_ref.shape[1]
    count = query_ref.shape[1]
    half = count // 2
    latent = jnp.concatenate([ref[...] for ref in latent_refs], axis=0)
    keys = latent.shape[0]

    row = lax.broadcasted_iota(jnp.int32, (count, 1), 0)
    row_cls = jnp.where(row < half, core, 1 - core)
    q_pos = ctx * count + token_offset(row, row_cls, rows, half)
    column = lax.broadcasted_iota(jnp.int32, (1, keys), 1)
    block = jnp.zeros((1, keys), jnp.int32)
    start = 0
    for (step, first), ref in zip(pieces, latent_refs):
        source = lax.rem(ctx - step + blocks, blocks)
        inside = (column >= start) & (column < start + ref.shape[0])
        block = jnp.where(inside, source, block)
        start += ref.shape[0]
    k_pos = block * count + token_offset(column, core, rows, half)
    causal = q_pos >= k_pos

    compressed = latent[:, :rank]
    key_shared = latent[:, rank:]
    for head, (up_k, up_v) in enumerate(((key_ref, value_ref), (far_key_ref, far_value_ref))):
        key = dot_nn(compressed, up_k[...])
        value = dot_nn(compressed, up_v[...])
        query = query_ref[head]
        scores = (dot_nt(query[:, :nope], key) + dot_nt(query[:, nope:], key_shared)) * scale
        scores = jnp.where(causal, scores, FLOOR)
        top = jnp.max(scores, axis=1, keepdims=True)
        if not fresh:
            state_ref = refs[5 + len(pieces)]
            before = state_ref[head, :, vdim : vdim + 1]
            top = jnp.maximum(top, before)
        weight = jnp.where(causal, jnp.exp(scores - top), 0.0)
        total = jnp.sum(weight, axis=1, keepdims=True)
        acc = dot_nn(weight, value)
        if not fresh:
            fade = jnp.exp(before - top)
            total = total + state_ref[head, :, vdim + 64 : vdim + 65] * fade
            acc = acc + state_ref[head, :, :vdim] * fade
        out_ref[head, :, :vdim] = acc
        out_ref[head, :, vdim : vdim + 64] = jnp.broadcast_to(top, (count, 64))
        out_ref[head, :, vdim + 64 :] = jnp.broadcast_to(total, (count, 64))


def share_kernel(state_ref, arrived_ref, out_w_ref, far_out_ref, out_ref):
    vdim = out_w_ref.shape[0]
    half = arrived_ref.shape[1]
    attended = []
    for head in range(2):
        mine = state_ref[head, :half]
        other = arrived_ref[1 - head]
        m0, m1 = mine[:, vdim : vdim + 1], other[:, vdim : vdim + 1]
        top = jnp.maximum(m0, m1)
        f0, f1 = jnp.exp(m0 - top), jnp.exp(m1 - top)
        total = mine[:, vdim + 64 : vdim + 65] * f0 + other[:, vdim + 64 : vdim + 65] * f1
        attended.append((mine[:, :vdim] * f0 + other[:, :vdim] * f1) / total)
    out_ref[...] = dot_nn(attended[0], out_w_ref[...]) + dot_nn(attended[1], far_out_ref[...])


def partner(array):
    size = lax.axis_size("head")
    return lax.ppermute(array, "head", [(h, h ^ 1) for h in range(size)])


def from_behind(array, step):
    size = lax.axis_size("ctx")
    return lax.ppermute(array, "ctx", [(c, (c + step) % size) for c in range(size)])


def exchange(pieces):
    size = lax.axis_size("head")
    groups = [list(range(core, size, 2)) for core in range(2)]
    return lax.all_to_all(
        pieces, "head", split_axis=0, concat_axis=0, tiled=True, axis_index_groups=groups
    )


def on_device(hidden, w_query, w_down, latent_gain, w_key_up, w_value_up, w_out):
    rows = hidden.shape[0]
    blocks = lax.axis_size("ctx")
    places = lax.axis_size("head") // 2
    scale = w_query.shape[1] ** (-0.5)
    place = jnp.stack([lax.axis_index("ctx"), lax.axis_index("head") & 1]).astype(jnp.int32)

    copies = jnp.broadcast_to(hidden[None], (places, *hidden.shape))
    mine = exchange(copies).reshape(places * rows, hidden.shape[1])
    far_query = partner(w_query)
    far_key = partner(w_key_up)
    far_value = partner(w_value_up)
    far_out = partner(w_out)

    width = w_down.shape[1]
    latent = call(
        latent_kernel, (places * rows, width), mine, w_down.T, latent_gain[None], name="latent"
    )
    ring = {step: from_behind(latent, step) for step in (1, -1, 2, -2)}
    half = latent.shape[0] // 2

    q_mine = call(
        query_kernel,
        (2, places * rows, w_query.shape[1]),
        mine,
        w_query.T,
        far_query.T,
        name="query",
    )
    q_other = partner(q_mine)
    queries = jnp.concatenate([q_mine, q_other[::-1]], axis=1)

    def attend(pieces, latents, state):
        kernel = functools.partial(attend_kernel, rows, scale, blocks, pieces, state is None)
        operands = [queries, w_key_up, w_value_up, far_key, far_value, *latents]
        if state is not None:
            operands.append(state)
        return pl.pallas_call(
            kernel,
            out_shape=jax.ShapeDtypeStruct(
                (2, queries.shape[1], 2 * w_value_up.shape[1]), jnp.float32
            ),
            in_specs=[pl.BlockSpec(memory_space=pltpu.SMEM)]
            + [pl.BlockSpec(memory_space=VMEM)] * len(operands),
            out_specs=pl.BlockSpec(memory_space=VMEM),
            compiler_params=pltpu.CompilerParams(vmem_limit_bytes=48 << 20),
            name="attend",
        )(place, *operands)

    state = attend([(0, 0)], [latent], None)
    state = attend([(k, 0) for k in ring], list(ring.values()), state)
    relay = [
        from_behind(ring[2], 1),
        from_behind(ring[-2], -1),
        from_behind(ring[2][:half], 2),
        from_behind(ring[-2][half:], -2),
    ]
    state = attend([(3, 0), (-3, 0), (4, 0), (4, half)], relay, state)

    arrived = partner(state[:, places * rows :])
    shares = call(
        share_kernel,
        (places * rows, w_out.shape[1]),
        state,
        arrived,
        w_out,
        far_out,
        name="share",
    )
    return exchange(shares.reshape(places, rows, shares.shape[1])).sum(axis=0)


def solution(mesh):
    placed = (
        P(("ctx", "head"), None),
        P(None, "head"),
        P(),
        P(),
        P(None, "head"),
        P(None, "head"),
        P("head", None),
    )
    return jax.shard_map(
        on_device, mesh=mesh, in_specs=placed, out_specs=P(("ctx", "head"), None), check_vma=False
    )
```

time: 167 us -> 122 us (0.73)
  blocking collectives: 63.9 us -> 20.9 us
  waiting for transfers between devices: 63.4 us -> 25.8 us
  Pallas kernels: 0 us -> 34 us
  starting transfers between devices: 0.04 us -> 33.7 us
  matrix products: 21.9 us -> 0 us
  between operations: 13.5 us -> 0.15 us
  local copies, waits for them, and re-layouts: 0.19 us -> 5.12 us
  other arithmetic: 4.02 us -> 1.75 us
    all_gather x2 -> x0, waiting for transfers between devices: 62.7 us -> none  [the longest x1 36 us: on_device(): portion = lax.all_gather(projected, 'ctx', axis=0, tiled=True)]
    all_to_all x2 -> x1, blocking collectives: 63.9 us -> 20.9 us  [exchange(): lax.all_to_all(pieces, 'head', split_axis=0, concat_axis=0, tiled=True, a...]
    pallas_call x0 -> x6, Pallas kernels: none -> 34 us  [the longest x3 17.2 us: attend(): pl.pallas_call(kernel, out_shape=jax.ShapeDtypeStruct((2, queries.shape[1...]
    ppermute x0 -> x14, starting transfers between devices: none -> 28.5 us  [the longest x6 15.8 us: partner(): return lax.ppermute(array, 'head', [(h, h ^ 1) for h in range(size)])]
    dot_general x8 -> x0, matrix products: 21.9 us -> none  [matmul(): jnp.dot(left, right, precision=EXACT, preferred_element_type=jnp.float32)]
    all_to_all x0 -> x1, waiting for transfers between devices: none -> 19 us  [exchange(): lax.all_to_all(pieces, 'head', split_axis=0, concat_axis=0, tiled=True, a...]
    ppermute x0 -> x14, waiting for transfers between devices: none -> 6.82 us  [the longest x8 5.65 us: from_behind(): lax.ppermute(array, 'ctx', [(c, (c + step) % size) for c in range(size)])]
    all_to_all x0 -> x1, starting transfers between devices: none -> 5.15 us  [exchange(): lax.all_to_all(pieces, 'head', split_axis=0, concat_axis=0, tiled=True, a...]
  transfers between devices with their start and end apart: 2 -> 15, of which waited for: 2 -> 4; matrix products, arithmetic and copies ran while one was open for 8% -> 4% of each run, Pallas kernels for 0% -> 25%
where the time goes in v1:
time: 122 us; the launch traced here: 121 us
  Pallas kernels  34 us (28%)
  starting transfers between devices  33.7 us (28%)
  waiting for transfers between devices  25.8 us (21%)
  blocking collectives  20.9 us (17%)
  local copies, waits for them, and re-layouts  5.12 us (4%)
  other arithmetic  1.75 us (1%)
    all_to_all x1, blocking collectives, exchange(): lax.all_to_all(pieces, 'head', split_axis=0, concat_axis=0, tiled=True, a...  20.9 us
    all_to_all x1, waiting for transfers between devices, exchange(): lax.all_to_all(pieces, 'head', split_axis=0, concat_axis=0, tiled=True, a...  19 us
    pallas_call x3, Pallas kernels, attend(): pl.pallas_call(kernel, out_shape=jax.ShapeDtypeStruct((2, queries.shape[1...  17.2 us
    pallas_call x3, Pallas kernels, call(): pl.pallas_call(kernel, out_shape=jax.ShapeDtypeStruct(out_shape, jnp.floa...  16.8 us
    ppermute x6, starting transfers between devices, partner(): return lax.ppermute(array, 'head', [(h, h ^ 1) for h in range(size)])  15.8 us
    ppermute x8, starting transfers between devices, from_behind(): lax.ppermute(array, 'ctx', [(c, (c + step) % size) for c in range(size)])  12.7 us
    ppermute x8, waiting for transfers between devices, from_behind(): lax.ppermute(array, 'ctx', [(c, (c + step) % size) for c in range(size)])  5.65 us
    all_to_all x1, starting transfers between devices, exchange(): lax.all_to_all(pieces, 'head', split_axis=0, concat_axis=0, tiled=True, a...  5.15 us
  transfers between devices with their start and end apart: 15, of which 4 were waited for; matrix products, arithmetic and copies ran while one was open for 4% of the time, Pallas kernels for 25%

profile of v1, /device:TPU:1, one launch (start us, length us, event | category | flops | bytes accessed | tf_op | source)
XLA Modules:
  0.0 121.4 jit_solution(12219457962420662667)
XLA Ops:
  0.0 3.2 %collective-permute-start = (f32[2304,192]{0,1:T(8,128)}, f32[2304,192]{0,1:T(8,128)}, u32[]{:S(2)}, u32[]{:S(2)}) collective-permute-start(f32[2304,192]{0,1:T(8,128)} %param.8), channel_id=1, source_target_pairs={{0,1},{1,0},{2,3},{3,2},{4,5},{5,4},{6,7},{7,6},{8,9},{9,8},{10,11... | collective-permute-start | bytes 5308424 | tf_op jit(solution)/shard_map/ppermute | solution.py:127
  3.2 2.0 %broadcast_in_dim.4 = f32[16,8,2304]{2,1,0:T(8,128)} broadcast(f32[8,2304]{1,0:T(8,128)} %param.7), dimensions={1,2} | broadcast | bytes 1253376 | tf_op jit(solution)/shard_map/broadcast_in_dim | solution.py:150
  5.2 5.2 %all-to-all-start = ((f32[16,8,2304]{2,1,0:T(8,128)}), f32[16,8,2304]{2,1,0:T(8,128)S(1)}, u32[]{:S(2)}, u32[]{:S(2)}) async-start(f32[16,8,2304]{2,1,0:T(8,128)} %broadcast_in_dim.4), calls=%async_computation | async-start | bytes 2359296 | tf_op jit(solution)/shard_map/all_to_all | solution.py:138
  11.3 19.0 %all-to-all-done = f32[16,8,2304]{2,1,0:T(8,128)S(1)} async-done(((f32[16,8,2304]{2,1,0:T(8,128)}), f32[16,8,2304]{2,1,0:T(8,128)S(1)}, u32[]{:S(2)}, u32[]{:S(2)}) %all-to-all-start) | async-done | bytes 1179680 | tf_op jit(solution)/shard_map/all_to_all | solution.py:138
  30.3 8.1 %latent.1.refs_5_ = f32[128,576]{1,0:T(8,128)S(1)} custom-call(f32[128,2304]{1,0:T(8,128)S(1)} %bitcast.8, f32[576,2304]{1,0:T(8,128)} %bitcast.13, f32[1,512]{1,0:T(1,128)S(1)} %bitcast.12), custom_call_target="tpu_custom_call" | custom-call | tf_op jit(solution)/shard_map/latent/pallas_call | solution.py:29
  38.5 3.1 %collective-permute-start.4 = (f32[128,576]{1,0:T(8,128)S(1)}, f32[128,576]{1,0:T(8,128)S(1)}, u32[]{:S(2)}, u32[]{:S(2)}) collective-permute-start(f32[128,576]{1,0:T(8,128)S(1)} %latent.1.refs_5_), channel_id=1, source_target_pairs={{0,64},{32,96},{64,128},{96,160},{128,192},{160,224},{192,0},{224,... | collective-permute-start | bytes 884744 | tf_op jit(solution)/shard_map/ppermute | solution.py:132
  41.5 3.1 %collective-permute-start.6 = (f32[128,576]{1,0:T(8,128)S(1)}, f32[128,576]{1,0:T(8,128)S(1)}, u32[]{:S(2)}, u32[]{:S(2)}) collective-permute-start(f32[128,576]{1,0:T(8,128)S(1)} %latent.1.refs_5_), channel_id=1, source_target_pairs={{0,192},{32,224},{64,0},{96,32},{128,64},{160,96},{192,128},{224,1... | collective-permute-start | bytes 884744 | tf_op jit(solution)/shard_map/ppermute | solution.py:132
  44.7 0.7 collective-permute-start.10
  45.4 1.9 %collective-permute-start.11 = (f32[128,576]{1,0:T(8,128)S(1)}, f32[128,576]{1,0:T(8,128)}, u32[]{:S(2)}, u32[]{:S(2)}) collective-permute-start(f32[128,576]{1,0:T(8,128)S(1)} %latent.1.refs_5_), channel_id=1, source_target_pairs={{0,224},{32,0},{64,32},{96,64},{128,96},{160,128},{192,160},{224,1... | collective-permute-start | bytes 884744 | tf_op jit(solution)/shard_map/ppermute | solution.py:132
  47.4 4.9 %query.1 = f32[2,128,192]{2,1,0:T(8,128)S(1)} custom-call(f32[128,2304]{1,0:T(8,128)S(1)} %bitcast.9, f32[192,2304]{1,0:T(8,128)S(1)} %bitcast.11, f32[192,2304]{1,0:T(8,128)} %bitcast.4.other_ref), custom_call_target="tpu_custom_call" | custom-call | tf_op jit(solution)/shard_map/query/pallas_call | solution.py:29
  52.3 1.3 %collective-permute-done.4.refs_7_ = f32[128,576]{1,0:T(8,128)S(1)} collective-permute-done((f32[128,576]{1,0:T(8,128)S(1)}, f32[128,576]{1,0:T(8,128)S(1)}, u32[]{:S(2)}, u32[]{:S(2)}) %collective-permute-start.4) | collective-permute-done | bytes 294944 | tf_op jit(solution)/shard_map/ppermute | solution.py:132
  53.6 7.9 %collective-permute-start.1 = (f32[2,128,192]{2,1,0:T(8,128)S(1)}, f32[2,128,192]{2,1,0:T(8,128)}, u32[]{:S(2)}, u32[]{:S(2)}) collective-permute-start(f32[2,128,192]{2,1,0:T(8,128)S(1)} %query.1), channel_id=1, source_target_pairs={{0,1},{1,0},{2,3},{3,2},{4,5},{5,4},{6,7},{7,6},{8,9},{9,8},{10,11... | collective-permute-start | bytes 589832 | tf_op jit(solution)/shard_map/ppermute | solution.py:127
  61.5 4.4 %collective-permute-done.10.refs_5_ = f32[128,576]{1,0:T(8,128)S(1)} collective-permute-done((f32[128,576]{1,0:T(8,128)S(1)}, f32[128,576]{1,0:T(8,128)S(1)}, u32[]{:S(2)}, u32[]{:S(2)}) %collective-permute-start.10) | collective-permute-done | bytes 294944 | tf_op jit(solution)/shard_map/ppermute | solution.py:132
  65.8 0.7 copy-done.3
  67.7 3.4 %collective-permute-start.9 = (f32[64,576]{1,0:T(8,128)S(1)}, f32[64,576]{1,0:T(8,128)S(1)}, u32[]{:S(2)}, u32[]{:S(2)}) collective-permute-start(f32[64,576]{1,0:T(8,128)S(1)} %slice.13), channel_id=1, source_target_pairs={{0,192},{32,224},{64,0},{96,32},{128,64},{160,96},{192,128},{224,1... | collective-permute-start | bytes 442376 | tf_op jit(solution)/shard_map/ppermute | solution.py:132
  71.2 1.7 %rev.3 = f32[2,128,192]{2,1,0:T(8,128)} reverse(f32[2,128,192]{2,1,0:T(8,128)} %collective-permute-done.1), dimensions={0} | reverse | bytes 393216 | tf_op jit(solution)/shard_map/rev | solution.py:173
  72.9 1.0 pad_maximum_fusion.refs_0_
  73.9 2.9 %attend.3.refs_9_ = f32[2,256,256]{2,1,0:T(8,128)S(1)} custom-call(s32[2]{0:T(128)S(1)} %pad_add_fusion.place_ref, f32[2,256,192]{2,1,0:T(8,128)S(1)} %pad_maximum_fusion.refs_0_, f32[512,128]{1,0:T(8,128)S(1)} %copy-done, f32[512,128]{1,0:T(8,128)S(1)} %copy-done.1, f32[512,128]{1,0:T(8,128)S(1)} %collective-permute-done.2.refs_3_, ...), custom_call_target="tpu_custom_call" | custom-call | tf_op jit(solution)/shard_map/attend/pallas_call | solution.py:180
  76.7 8.0 %attend.4.refs_9_ = f32[2,256,256]{2,1,0:T(8,128)S(1)} custom-call(s32[2]{0:T(128)S(1)} %pad_add_fusion.place_ref, f32[2,256,192]{2,1,0:T(8,128)S(1)} %pad_maximum_fusion.refs_0_, f32[512,128]{1,0:T(8,128)S(1)} %copy-done, f32[512,128]{1,0:T(8,128)S(1)} %copy-done.1, f32[512,128]{1,0:T(8,128)S(1)} %collective-permute-done.2.refs_3_, ...), custom_call_target="tpu_custom_call" | custom-call | tf_op jit(solution)/shard_map/attend/pallas_call | solution.py:180
  84.8 6.3 %attend.5.state_ref = f32[2,256,256]{2,1,0:T(8,128)S(1)} custom-call(s32[2]{0:T(128)S(1)} %pad_add_fusion.place_ref, f32[2,256,192]{2,1,0:T(8,128)S(1)} %pad_maximum_fusion.refs_0_, f32[512,128]{1,0:T(8,128)S(1)} %copy-done, f32[512,128]{1,0:T(8,128)S(1)} %copy-done.1, f32[512,128]{1,0:T(8,128)S(1)} %collective-permute-done.2.refs_3_, ...), custom_call_target="tpu_custom_call" | custom-call | tf_op jit(solution)/shard_map/attend/pallas_call | solution.py:180
  91.2 3.7 %collective-permute-start.12 = (f32[2,128,256]{2,1,0:T(8,128)S(1)}, f32[2,128,256]{2,1,0:T(8,128)S(1)}, u32[]{:S(2)}, u32[]{:S(2)}) collective-permute-start(f32[2,128,256]{2,1,0:T(8,128)S(1)} %slice.14), channel_id=1, source_target_pairs={{0,1},{1,0},{2,3},{3,2},{4,5},{5,4},{6,7},{7,6},{8,9},{9,8},{10,11... | collective-permute-start | bytes 786440 | tf_op jit(solution)/shard_map/ppermute | solution.py:127
  94.9 1.2 collective-permute-done.12.arrived_ref
  96.1 3.7 %share.1 = f32[128,2304]{1,0:T(8,128)S(1)} custom-call(f32[2,256,256]{2,1,0:T(8,128)S(1)} %attend.5.state_ref, f32[2,128,256]{2,1,0:T(8,128)S(1)} %collective-permute-done.12.arrived_ref, f32[128,2304]{1,0:T(8,128)} %out_w_ref.1, f32[128,2304]{1,0:T(8,128)} %collective-permute-done.13.far_out_ref), custom_call_target="tpu_custom_call" | custom-call | tf_op jit(solution)/shard_map/share/pallas_call | solution.py:29
  99.9 20.9 %all_to_all.10 = f32[16,8,2304]{2,1,0:T(8,128)S(1)} all-to-all(f32[16,8,2304]{2,1,0:T(8,128)S(1)} %bitcast.10), channel_id=1, replica_groups={{0,2,4,6,8,10,12,14,16,18,20,22,24,26,28,30},{1,3,5,7,9,11,13,15,17,19,..., dimensions={0} | all-to-all | bytes 2359296 | tf_op jit(solution)/shard_map/all_to_all | solution.py:138
  (33 shorter events, 2.9 us)
Async XLA Ops:
  0.0 45.4 %collective-permute-start = (f32[2304,192]{0,1:T(8,128)}, f32[2304,192]{0,1:T(8,128)}, u32[]{:S(2)}, u32[]{:S(2)}) collective-permute-start(f32[2304,192]{0,1:T(8,128)} %param.8), channel_id=1, source_target_pairs={{0,1},{1,0},{2,3},{3,2},{4,5},{5,4},{6,7},{7,6},{8,9},{9,8},{10,11... | collective-permute-start | bytes 5308424 | tf_op jit(solution)/shard_map/ppermute | solution.py:127
  5.2 5.5 %copy-start = (f32[512,128]{1,0:T(8,128)S(1)}, f32[512,128]{1,0:T(8,128)}, u32[]{:S(2)}) copy-start(f32[512,128]{1,0:T(8,128)} %refs_1_.5) | copy-start | bytes 786436
  5.2 5.8 %copy-start.1 = (f32[512,128]{1,0:T(8,128)S(1)}, f32[512,128]{1,0:T(8,128)}, u32[]{:S(2)}) copy-start(f32[512,128]{1,0:T(8,128)} %refs_2_.5) | copy-start | bytes 786436
  5.2 25.1 %copy-start.5 = (f32[512]{0:T(512)S(1)}, f32[512]{0:T(512)}, u32[]{:S(2)}) copy-start(f32[512]{0:T(512)} %param.10) | copy-start | bytes 6148
  5.2 25.1 %all-to-all-start = ((f32[16,8,2304]{2,1,0:T(8,128)}), f32[16,8,2304]{2,1,0:T(8,128)S(1)}, u32[]{:S(2)}, u32[]{:S(2)}) async-start(f32[16,8,2304]{2,1,0:T(8,128)} %broadcast_in_dim.4), calls=%async_computation | async-start | bytes 2359296 | tf_op jit(solution)/shard_map/all_to_all | solution.py:138
  10.4 84.5 %collective-permute-start.13 = (f32[128,2304]{1,0:T(8,128)}, f32[128,2304]{1,0:T(8,128)}, u32[]{:S(2)}, u32[]{:S(2)}) collective-permute-start(f32[128,2304]{1,0:T(8,128)} %out_w_ref.1), channel_id=1, source_target_pairs={{0,1},{1,0},{2,3},{3,2},{4,5},{5,4},{6,7},{7,6},{8,9},{9,8},{10,11... | collective-permute-start | bytes 3538952 | tf_op jit(solution)/shard_map/ppermute | solution.py:127
  10.8 30.8 %collective-permute-start.2 = (f32[512,128]{1,0:T(8,128)S(1)}, f32[512,128]{1,0:T(8,128)S(1)}, u32[]{:S(2)}, u32[]{:S(2)}) collective-permute-start(f32[512,128]{1,0:T(8,128)S(1)} %copy-done), channel_id=1, source_target_pairs={{0,1},{1,0},{2,3},{3,2},{4,5},{5,4},{6,7},{7,6},{8,9},{9,8},{10,11... | collective-permute-start | bytes 786440 | tf_op jit(solution)/shard_map/ppermute | solution.py:127
  11.0 33.7 %collective-permute-start.3 = (f32[512,128]{1,0:T(8,128)S(1)}, f32[512,128]{1,0:T(8,128)S(1)}, u32[]{:S(2)}, u32[]{:S(2)}) collective-permute-start(f32[512,128]{1,0:T(8,128)S(1)} %copy-done.1), channel_id=1, source_target_pairs={{0,1},{1,0},{2,3},{3,2},{4,5},{5,4},{6,7},{7,6},{8,9},{9,8},{10,11... | collective-permute-start | bytes 786440 | tf_op jit(solution)/shard_map/ppermute | solution.py:127
  30.3 17.0 %copy-start.2 = (f32[2304,192]{0,1:T(8,128)S(1)}, f32[2304,192]{0,1:T(8,128)}, u32[]{:S(2)}) copy-start(f32[2304,192]{0,1:T(8,128)} %param.8) | copy-start | bytes 5308420
  38.5 15.1 %collective-permute-start.4 = (f32[128,576]{1,0:T(8,128)S(1)}, f32[128,576]{1,0:T(8,128)S(1)}, u32[]{:S(2)}, u32[]{:S(2)}) collective-permute-start(f32[128,576]{1,0:T(8,128)S(1)} %latent.1.refs_5_), channel_id=1, source_target_pairs={{0,64},{32,96},{64,128},{96,160},{128,192},{160,224},{192,0},{224,... | collective-permute-start | bytes 884744 | tf_op jit(solution)/shard_map/ppermute | solution.py:132
  41.5 19.9 %collective-permute-start.6 = (f32[128,576]{1,0:T(8,128)S(1)}, f32[128,576]{1,0:T(8,128)S(1)}, u32[]{:S(2)}, u32[]{:S(2)}) collective-permute-start(f32[128,576]{1,0:T(8,128)S(1)} %latent.1.refs_5_), channel_id=1, source_target_pairs={{0,192},{32,224},{64,0},{96,32},{128,64},{160,96},{192,128},{224,1... | collective-permute-start | bytes 884744 | tf_op jit(solution)/shard_map/ppermute | solution.py:132
  44.7 21.2 %collective-permute-start.10 = (f32[128,576]{1,0:T(8,128)S(1)}, f32[128,576]{1,0:T(8,128)S(1)}, u32[]{:S(2)}, u32[]{:S(2)}) collective-permute-start(f32[128,576]{1,0:T(8,128)S(1)} %latent.1.refs_5_), channel_id=1, source_target_pairs={{0,32},{32,64},{64,96},{96,128},{128,160},{160,192},{192,224},{224... | collective-permute-start | bytes 884744 | tf_op jit(solution)/shard_map/ppermute | solution.py:132
  45.4 22.1 %collective-permute-start.11 = (f32[128,576]{1,0:T(8,128)S(1)}, f32[128,576]{1,0:T(8,128)}, u32[]{:S(2)}, u32[]{:S(2)}) collective-permute-start(f32[128,576]{1,0:T(8,128)S(1)} %latent.1.refs_5_), channel_id=1, source_target_pairs={{0,224},{32,0},{64,32},{96,64},{128,96},{160,128},{192,160},{224,1... | collective-permute-start | bytes 884744 | tf_op jit(solution)/shard_map/ppermute | solution.py:132
  53.6 14.2 %collective-permute-start.1 = (f32[2,128,192]{2,1,0:T(8,128)S(1)}, f32[2,128,192]{2,1,0:T(8,128)}, u32[]{:S(2)}, u32[]{:S(2)}) collective-permute-start(f32[2,128,192]{2,1,0:T(8,128)S(1)} %query.1), channel_id=1, source_target_pairs={{0,1},{1,0},{2,3},{3,2},{4,5},{5,4},{6,7},{7,6},{8,9},{9,8},{10,11... | collective-permute-start | bytes 589832 | tf_op jit(solution)/shard_map/ppermute | solution.py:127
  61.5 23.3 %collective-permute-start.5 = (f32[128,576]{1,0:T(8,128)S(1)}, f32[128,576]{1,0:T(8,128)S(1)}, u32[]{:S(2)}, u32[]{:S(2)}) collective-permute-start(f32[128,576]{1,0:T(8,128)S(1)} %collective-permute-done.4.refs_7_), channel_id=1, source_target_pairs={{0,32},{32,64},{64,96},{96,128},{128,160},{160,192},{192,224},{224... | collective-permute-start | bytes 884744 | tf_op jit(solution)/shard_map/ppermute | solution.py:132
  65.8 0.7 copy-start.3
  66.6 18.2 %collective-permute-start.7 = (f32[128,576]{1,0:T(8,128)S(1)}, f32[128,576]{1,0:T(8,128)S(1)}, u32[]{:S(2)}, u32[]{:S(2)}) collective-permute-start(f32[128,576]{1,0:T(8,128)S(1)} %collective-permute-done.6.refs_8_), channel_id=1, source_target_pairs={{0,224},{32,0},{64,32},{96,64},{128,96},{160,128},{192,160},{224,1... | collective-permute-start | bytes 884744 | tf_op jit(solution)/shard_map/ppermute | solution.py:132
  67.5 17.3 %collective-permute-start.8 = (f32[64,576]{1,0:T(8,128)}, f32[64,576]{1,0:T(8,128)S(1)}, u32[]{:S(2)}, u32[]{:S(2)}) collective-permute-start(f32[64,576]{1,0:T(8,128)} %slice.12), channel_id=1, source_target_pairs={{0,64},{32,96},{64,128},{96,160},{128,192},{160,224},{192,0},{224,... | collective-permute-start | bytes 442376 | tf_op jit(solution)/shard_map/ppermute | solution.py:132
  67.7 17.1 %collective-permute-start.9 = (f32[64,576]{1,0:T(8,128)S(1)}, f32[64,576]{1,0:T(8,128)S(1)}, u32[]{:S(2)}, u32[]{:S(2)}) collective-permute-start(f32[64,576]{1,0:T(8,128)S(1)} %slice.13), channel_id=1, source_target_pairs={{0,192},{32,224},{64,0},{96,32},{128,64},{160,96},{192,128},{224,1... | collective-permute-start | bytes 442376 | tf_op jit(solution)/shard_map/ppermute | solution.py:132
  73.9 2.9 %copy-start.4 = (f32[128,576]{1,0:T(8,128)S(1)}, f32[128,576]{1,0:T(8,128)}, u32[]{:S(2)}) copy-start(f32[128,576]{1,0:T(8,128)} %copy-done.3) | copy-start | bytes 884740
  91.2 4.9 %collective-permute-start.12 = (f32[2,128,256]{2,1,0:T(8,128)S(1)}, f32[2,128,256]{2,1,0:T(8,128)S(1)}, u32[]{:S(2)}, u32[]{:S(2)}) collective-permute-start(f32[2,128,256]{2,1,0:T(8,128)S(1)} %slice.14), channel_id=1, source_target_pairs={{0,1},{1,0},{2,3},{3,2},{4,5},{5,4},{6,7},{7,6},{8,9},{9,8},{10,11... | collective-permute-start | bytes 786440 | tf_op jit(solution)/shard_map/ppermute | solution.py:127

commit v2 on v0

v2 whole, which is shorter than its diff:
```python
import functools

import jax
import jax.numpy as jnp
from jax import lax
from jax.experimental import pallas as pl
from jax.experimental.pallas import tpu as pltpu
from jax.sharding import PartitionSpec as P

EPSILON = 1e-06
FLOOR = -1e30
RING = (1, -1)
FAR = (2, 3, 4, 5, 6)
F32 = jnp.float32
BF16 = jnp.bfloat16
VMEM = pltpu.VMEM
LIMIT = 24 << 20


def nn(left, right):
    return lax.dot_general(left, right, (((1,), (0,)), ((), ())), preferred_element_type=F32)


def nt(left, right):
    return lax.dot_general(left, right, (((1,), (1,)), ((), ())), preferred_element_type=F32)


def split(array, count):
    parts = []
    for _ in range(count - 1):
        part = array.astype(BF16)
        parts.append(part)
        array = array - part.astype(F32)
    parts.append(array.astype(BF16))
    return parts


def six(left, right, dot):
    high, middle, low = left
    rows = high.shape[0]
    by_high = dot(jnp.concatenate([high, middle, low], axis=0), right[0])
    by_middle = dot(jnp.concatenate([high, middle], axis=0), right[1])
    by_low = dot(high, right[2])
    return by_high[:rows] + (
        (by_high[rows : 2 * rows] + by_middle[:rows])
        + (by_high[2 * rows :] + by_middle[rows:] + by_low)
    )


def three(left, right, dot):
    high, low = left[:2]
    rows = high.shape[0]
    by_high = dot(jnp.concatenate([high, low], axis=0), right[0])
    return by_high[:rows] + (by_high[rows:] + dot(high, right[1]))


def call(kernel, outs, operands, name, place=None):
    first = [] if place is None else [place]
    return pl.pallas_call(
        kernel,
        out_shape=outs,
        in_specs=[pl.BlockSpec(memory_space=pltpu.SMEM)] * len(first)
        + [pl.BlockSpec(memory_space=VMEM)] * len(operands),
        out_specs=jax.tree.map(lambda _: pl.BlockSpec(memory_space=VMEM), outs),
        compiler_params=pltpu.CompilerParams(vmem_limit_bytes=LIMIT),
        name=name,
    )(*first, *operands)


def shape(*dims, dtype=F32):
    return jax.ShapeDtypeStruct(dims, dtype)


def split_kernel(count, *refs):
    sources, outs = refs[:-1], refs[-1]
    start = 0
    for ref in sources:
        stop = start + ref.shape[0]
        for part, value in enumerate(split(ref[...], count)):
            outs[part, start:stop] = value
        start = stop


def normed(down, gain, out_ref):
    rank = gain.shape[1]
    raw = down[:, :rank]
    meansq = jnp.mean(raw * raw, axis=-1, keepdims=True)
    out_ref[:, :rank] = raw * lax.rsqrt(meansq + EPSILON) * gain
    out_ref[:, rank:] = down[:, rank:]


def own_kernel(x_ref, down_ref, gain_ref, out_ref):
    rows = x_ref.shape[0]
    x = jnp.concatenate([part.astype(F32) for part in split(x_ref[...], 3)], axis=0).astype(BF16)
    high, middle, low = (nt(down_ref[part], x) for part in range(3))
    total = high[:, :rows] + (
        (high[:, rows : 2 * rows] + middle[:, :rows])
        + (high[:, 2 * rows :] + middle[:, rows : 2 * rows] + low[:, :rows])
    )
    normed(total.T, gain_ref[...], out_ref)


def latent_kernel(x_ref, down_ref, gain_ref, out_ref):
    down = six(split(x_ref[...], 3), [down_ref[part] for part in range(3)], nt)
    normed(down, gain_ref[...], out_ref)


def query_kernel(x_ref, own_ref, other_ref, out_ref):
    x = split(x_ref[...], 3)
    out_ref[0] = six(x, split(own_ref[...], 3), nt)
    out_ref[1] = six(x, split(other_ref[...], 3), nt)


def block_offset(place, row, cls, rows):
    return (place * 2 + cls) * rows + row


def attend_kernel(rows, scale, blocks, place_ref, *refs):
    mine_ref, theirs_ref, key_ref, value_ref = refs[:4]
    near_refs, far_ref = refs[4:-3], refs[-3]
    out_refs = refs[-2:]
    ctx, core = place_ref[0], place_ref[1]
    rank = key_ref.shape[1]
    heads = mine_ref.shape[0]
    half = mine_ref.shape[1]
    nope = key_ref.shape[2] // heads
    vdim = value_ref.shape[2] // heads
    count = 2 * half

    row = lax.broadcasted_iota(jnp.int32, (count, 1), 0)
    row_cls = jnp.where(row < half, core, 1 - core)
    within = lax.rem(row, half)
    q_pos = ctx * count + block_offset(within // rows, lax.rem(within, rows), row_cls, rows)

    latent = jnp.concatenate([ref[...] for ref in near_refs] + [far_ref[...]], axis=0)
    column = lax.broadcasted_iota(jnp.int32, (1, latent.shape[0]), 1)
    far_column = column - half * len(near_refs)
    step = FAR[0] + lax.rem(far_column // rows, len(FAR))
    within = far_column // (rows * len(FAR)) * rows + lax.rem(column, rows)
    for number, behind in enumerate((0, *RING)):
        inside = column // half == number
        step = jnp.where(inside, behind, step)
        within = jnp.where(inside, column - number * half, within)
    block = lax.rem(ctx - step + blocks, blocks)
    k_pos = block * count + block_offset(within // rows, lax.rem(within, rows), core, rows)
    causal = q_pos >= k_pos

    compressed = split(latent[:, :rank], 3)
    keys = six(compressed, [key_ref[part] for part in range(3)], nn)
    values = three(compressed, [value_ref[part] for part in range(2)], nn)
    for head in range(heads):
        key = jnp.concatenate([keys[:, head * nope : (head + 1) * nope], latent[:, rank:]], axis=1)
        query = jnp.concatenate([mine_ref[head], theirs_ref[heads - 1 - head]], axis=0)
        scores = jnp.where(causal, six(split(query, 3), split(key, 3), nt) * scale, FLOOR)
        top = jnp.max(scores, axis=1, keepdims=True)
        weight = jnp.where(causal, jnp.exp(scores - top), 0.0)
        total = jnp.sum(weight, axis=1, keepdims=True)
        value = split(values[:, head * vdim : (head + 1) * vdim], 2)
        acc = three(split(weight, 2), value, nn)
        for number, out_ref in enumerate(out_refs):
            chosen = slice(number * half, (number + 1) * half)
            out_ref[head, :, :vdim] = acc[chosen]
            out_ref[head, :, vdim : vdim + 64] = jnp.broadcast_to(top[chosen], (half, 64))
            out_ref[head, :, vdim + 64 :] = jnp.broadcast_to(total[chosen], (half, 64))


def share_kernel(state_ref, arrived_ref, out_w_ref, out_ref):
    heads = state_ref.shape[0]
    vdim = out_w_ref.shape[1] // heads
    attended = []
    for head in range(heads):
        mine = state_ref[head]
        other = arrived_ref[heads - 1 - head]
        m0, m1 = mine[:, vdim : vdim + 1], other[:, vdim : vdim + 1]
        top = jnp.maximum(m0, m1)
        f0, f1 = jnp.exp(m0 - top), jnp.exp(m1 - top)
        total = mine[:, vdim + 64 : vdim + 65] * f0 + other[:, vdim + 64 : vdim + 65] * f1
        attended.append((mine[:, :vdim] * f0 + other[:, :vdim] * f1) / total)
    left = split(jnp.concatenate(attended, axis=1), 2)
    out_ref[...] = three(left, [out_w_ref[part] for part in range(2)], nn)


def key_value_kernel(key_ref, far_key_ref, value_ref, far_value_ref, keys_ref, values_ref):
    nope, vdim = key_ref.shape[1], value_ref.shape[1]
    for number, ref in enumerate((key_ref, far_key_ref)):
        for part, value in enumerate(split(ref[...], 3)):
            keys_ref[part, :, number * nope : (number + 1) * nope] = value
    for number, ref in enumerate((value_ref, far_value_ref)):
        for part, value in enumerate(split(ref[...], 2)):
            values_ref[part, :, number * vdim : (number + 1) * vdim] = value


def partner(array):
    size = lax.axis_size("head")
    return lax.ppermute(array, "head", [(h, h ^ 1) for h in range(size)])


def from_behind(array, step):
    size = lax.axis_size("ctx")
    return lax.ppermute(array, "ctx", [(c, (c + step) % size) for c in range(size)])


def exchange(pieces):
    size = lax.axis_size("head")
    groups = [list(range(core, size, 2)) for core in range(2)]
    return lax.all_to_all(
        pieces, "head", split_axis=0, concat_axis=0, tiled=True, axis_index_groups=groups
    )


def spread_kernel(*refs):
    out_ref = refs[-1]
    for number, ref in enumerate(refs[:-1]):
        for copy in range(out_ref.shape[0]):
            out_ref[copy, number] = ref[...]


def spread(array, places):
    return exchange(jnp.broadcast_to(array[None], (places, *array.shape)))


def on_device(hidden, w_query, w_down, latent_gain, w_key_up, w_value_up, w_out):
    rows, depth = hidden.shape
    blocks = lax.axis_size("ctx")
    places = lax.axis_size("head") // 2
    half = places * rows
    rank, nope = w_key_up.shape
    vdim = w_value_up.shape[1]
    width = w_down.shape[1]
    place = jnp.stack([lax.axis_index("ctx"), lax.axis_index("head") & 1]).astype(jnp.int32)
    gain = latent_gain[None]

    mine = spread(hidden, places).reshape(half, depth)
    far_query, far_key, far_value, far_out = (
        partner(weight) for weight in (w_query, w_key_up, w_value_up, w_out)
    )
    down_parts = call(
        functools.partial(split_kernel, 3),
        shape(3, width, depth, dtype=BF16),
        [w_down.T],
        "down_parts",
    )
    own = call(own_kernel, shape(rows, width), [hidden, down_parts, gain], "own_latent")
    far = [from_behind(own, step) for step in FAR]
    far_copies = call(spread_kernel, shape(places, len(FAR), rows, width), far, "far_copies")
    far_latent = exchange(far_copies).reshape(-1, width)

    latent = call(latent_kernel, shape(half, width), [mine, down_parts, gain], "latent")
    ring = [from_behind(latent, step) for step in RING]

    mine, far_query, _ = lax.optimization_barrier((mine, far_query, latent))
    queries = call(
        query_kernel,
        shape(2, half, w_query.shape[1]),
        [mine, w_query.T, far_query.T],
        "query",
    )
    other_queries = partner(queries)
    key_parts, value_parts = call(
        key_value_kernel,
        [shape(3, rank, 2 * nope, dtype=BF16), shape(2, rank, 2 * vdim, dtype=BF16)],
        [w_key_up, far_key, w_value_up, far_value],
        "key_value_parts",
    )
    out_parts = call(
        functools.partial(split_kernel, 2),
        shape(2, 2 * vdim, depth, dtype=BF16),
        [w_out, far_out],
        "out_parts",
    )

    state = call(
        functools.partial(attend_kernel, rows, w_query.shape[1] ** (-0.5), blocks),
        [shape(2, half, 2 * vdim)] * 2,
        [queries, other_queries, key_parts, value_parts, latent, *ring, far_latent],
        "attend",
        place,
    )
    arrived = partner(state[1])
    shares = call(share_kernel, shape(half, depth), [state[0], arrived, out_parts], "share")
    return exchange(shares.reshape(places, rows, depth)).sum(axis=0)


def solution(mesh):
    placed = (
        P(("ctx", "head"), None),
        P(None, "head"),
        P(),
        P(),
        P(None, "head"),
        P(None, "head"),
        P("head", None),
    )
    return jax.shard_map(
        on_device, mesh=mesh, in_specs=placed, out_specs=P(("ctx", "head"), None), check_vma=False
    )
```

time: 167 us -> 102 us (0.61)
  waiting for transfers between devices: 63.4 us -> 1.17 us
  blocking collectives: 63.9 us -> 21.2 us
  starting transfers between devices: 0.04 us -> 41.4 us
  Pallas kernels: 0 us -> 24.2 us
  matrix products: 21.9 us -> 0 us
  between operations: 13.5 us -> 0.16 us
  local copies, waits for them, and re-layouts: 0.19 us -> 12.9 us
  other arithmetic: 4.02 us -> 0.77 us
    all_gather x2 -> x0, waiting for transfers between devices: 62.7 us -> none  [the longest x1 36 us: on_device(): portion = lax.all_gather(projected, 'ctx', axis=0, tiled=True)]
    all_to_all x2 -> x1, blocking collectives: 63.9 us -> 21.2 us  [exchange(): lax.all_to_all(pieces, 'head', split_axis=0, concat_axis=0, tiled=True, a...]
    ppermute x0 -> x13, starting transfers between devices: none -> 27 us  [the longest x7 17.7 us: from_behind(): lax.ppermute(array, 'ctx', [(c, (c + step) % size) for c in range(size)])]
    pallas_call x0 -> x9, Pallas kernels: none -> 24.2 us  [call(): pl.pallas_call(kernel, out_shape=outs, in_specs=[pl.BlockSpec(memory_spac...]
    dot_general x8 -> x0, matrix products: 21.9 us -> none  [matmul(): jnp.dot(left, right, precision=EXACT, preferred_element_type=jnp.float32)]
    all_to_all x0 -> x2, starting transfers between devices: none -> 14.4 us  [exchange(): lax.all_to_all(pieces, 'head', split_axis=0, concat_axis=0, tiled=True, a...]
    unnamed x13 -> x24, local copies, waits for them, and re-layouts: 0.1 us -> 10.9 us
    reduce_sum x3 -> x1, other arithmetic: 3.16 us -> 0.69 us  [on_device(): return exchange(shares.reshape(places, rows, depth)).sum(axis=0)]
  transfers between devices with their start and end apart: 2 -> 15, of which waited for: 2 -> 1; matrix products, arithmetic and copies ran while one was open for 8% -> 0% of each run, Pallas kernels for 0% -> 23%
where the time goes in v2:
time: 102 us
  starting transfers between devices  41.4 us (41%)
  Pallas kernels  24.2 us (24%)
  blocking collectives  21.2 us (21%)
  local copies, waits for them, and re-layouts  12.9 us (13%)
  waiting for transfers between devices  1.17 us (1%)
    pallas_call x9, Pallas kernels, call(): pl.pallas_call(kernel, out_shape=outs, in_specs=[pl.BlockSpec(memory_spac...  24.2 us
    all_to_all x1, blocking collectives, exchange(): lax.all_to_all(pieces, 'head', split_axis=0, concat_axis=0, tiled=True, a...  21.2 us
    ppermute x7, starting transfers between devices, from_behind(): lax.ppermute(array, 'ctx', [(c, (c + step) % size) for c in range(size)])  17.7 us
    all_to_all x2, starting transfers between devices, exchange(): lax.all_to_all(pieces, 'head', split_axis=0, concat_axis=0, tiled=True, a...  14.4 us
    unnamed x24, local copies, waits for them, and re-layouts  10.9 us
    ppermute x6, starting transfers between devices, partner(): return lax.ppermute(array, 'head', [(h, h ^ 1) for h in range(size)])  9.26 us
  transfers between devices with their start and end apart: 15, of which 1 were waited for; matrix products, arithmetic and copies ran while one was open for 0% of the time, Pallas kernels for 23%

profile of v2, /device:TPU:1, one launch (start us, length us, event | category | flops | bytes accessed | tf_op | source)
XLA Modules:
  0.0 101.8 jit_solution(7146459593404428369)
XLA Ops:
  0.0 2.0 %broadcast_in_dim.4 = f32[16,8,2304]{2,1,0:T(8,128)} broadcast(f32[8,2304]{1,0:T(8,128)} %x_ref.1), dimensions={1,2} | broadcast | bytes 1253376 | tf_op jit(solution)/shard_map/broadcast_in_dim | solution.py:219
  2.0 7.6 %all-to-all-start = ((f32[16,8,2304]{2,1,0:T(8,128)}), f32[16,8,2304]{2,1,0:T(8,128)S(1)}, u32[]{:S(2)}, u32[]{:S(2)}) async-start(f32[16,8,2304]{2,1,0:T(8,128)} %broadcast_in_dim.4), calls=%async_computation | async-start | bytes 2359296 | tf_op jit(solution)/shard_map/all_to_all | solution.py:206
  9.6 1.0 %collective-permute-start = (f32[2304,192]{0,1:T(8,128)}, f32[2304,192]{0,1:T(8,128)}, u32[]{:S(2)}, u32[]{:S(2)}) collective-permute-start(f32[2304,192]{0,1:T(8,128)} %param.8), channel_id=1, source_target_pairs={{0,1},{1,0},{2,3},{3,2},{4,5},{5,4},{6,7},{7,6},{8,9},{9,8},{10,11... | collective-permute-start | bytes 5308424 | tf_op jit(solution)/shard_map/ppermute | solution.py:195
  10.6 2.5 %copy-done.3 = f32[2304,576]{0,1:T(8,128)S(1)} copy-done((f32[2304,576]{0,1:T(8,128)S(1)}, f32[2304,576]{0,1:T(8,128)}, u32[]{:S(2)}) %copy-start.3) | copy-done | bytes 5308440
  13.2 1.5 %down_parts.1.down_ref = bf16[3,576,2304]{2,1,0:T(8,128)(2,1)S(1)} custom-call(f32[576,2304]{1,0:T(8,128)S(1)} %bitcast.12), custom_call_target="tpu_custom_call" | custom-call | tf_op jit(solution)/shard_map/down_parts/pallas_call | solution.py:59
  14.7 2.6 %own_latent.1 = f32[8,576]{1,0:T(8,128)S(1)} custom-call(f32[8,2304]{1,0:T(8,128)S(1)} %copy-done.8, bf16[3,576,2304]{2,1,0:T(8,128)(2,1)S(1)} %down_parts.1.down_ref, f32[1,512]{1,0:T(1,128)S(1)} %bitcast.15), custom_call_target="tpu_custom_call" | custom-call | tf_op jit(solution)/shard_map/own_latent/pallas_call | solution.py:59
  17.8 3.0 %collective-permute-start.6 = (f32[8,576]{1,0:T(8,128)S(1)}, f32[8,576]{1,0:T(8,128)S(1)}, u32[]{:S(2)}, u32[]{:S(2)}) collective-permute-start(f32[8,576]{1,0:T(8,128)S(1)} %own_latent.1), channel_id=1, source_target_pairs={{0,64},{32,96},{64,128},{96,160},{128,192},{160,224},{192,0},{224,... | collective-permute-start | bytes 55304 | tf_op jit(solution)/shard_map/ppermute | solution.py:200
  20.7 4.7 %collective-permute-start.7 = (f32[8,576]{1,0:T(8,128)S(1)}, f32[8,576]{1,0:T(8,128)S(1)}, u32[]{:S(2)}, u32[]{:S(2)}) collective-permute-start(f32[8,576]{1,0:T(8,128)S(1)} %own_latent.1), channel_id=1, source_target_pairs={{0,96},{32,128},{64,160},{96,192},{128,224},{160,0},{192,32},{224,... | collective-permute-start | bytes 55304 | tf_op jit(solution)/shard_map/ppermute | solution.py:200
  26.3 4.0 %collective-permute-start.9 = (f32[8,576]{1,0:T(8,128)S(1)}, f32[8,576]{1,0:T(8,128)S(1)}, u32[]{:S(2)}, u32[]{:S(2)}) collective-permute-start(f32[8,576]{1,0:T(8,128)S(1)} %own_latent.1), channel_id=1, source_target_pairs={{0,160},{32,192},{64,224},{96,0},{128,32},{160,64},{192,96},{224,1... | collective-permute-start | bytes 55304 | tf_op jit(solution)/shard_map/ppermute | solution.py:200
  30.3 2.4 %collective-permute-start.10 = (f32[8,576]{1,0:T(8,128)S(1)}, f32[8,576]{1,0:T(8,128)S(1)}, u32[]{:S(2)}, u32[]{:S(2)}) collective-permute-start(f32[8,576]{1,0:T(8,128)S(1)} %own_latent.1), channel_id=1, source_target_pairs={{0,192},{32,224},{64,0},{96,32},{128,64},{160,96},{192,128},{224,1... | collective-permute-start | bytes 55304 | tf_op jit(solution)/shard_map/ppermute | solution.py:200
  32.7 1.1 %collective-permute-done.10.refs_4_ = f32[8,576]{1,0:T(8,128)S(1)} collective-permute-done((f32[8,576]{1,0:T(8,128)S(1)}, f32[8,576]{1,0:T(8,128)S(1)}, u32[]{:S(2)}, u32[]{:S(2)}) %collective-permute-start.10) | collective-permute-done | bytes 18464 | tf_op jit(solution)/shard_map/ppermute | solution.py:200
  34.0 1.2 %copy-done.2 = f32[16,5,8,576]{3,2,1,0:T(8,128)} copy-done((f32[16,5,8,576]{3,2,1,0:T(8,128)}, f32[16,5,8,576]{3,2,1,0:T(8,128)S(1)}, u32[]{:S(2)}) %copy-start.2) | copy-done | bytes 1474584
  35.2 6.9 %all-to-all-start.1 = ((f32[16,5,8,576]{3,2,1,0:T(8,128)}), f32[16,5,8,576]{3,2,1,0:T(8,128)S(1)}, u32[]{:S(2)}, u32[]{:S(2)}) async-start(f32[16,5,8,576]{3,2,1,0:T(8,128)} %copy-done.2), calls=%async_computation.1 | async-start | bytes 3276800 | tf_op jit(solution)/shard_map/all_to_all | solution.py:206
  42.0 2.7 %collective-permute-start.12 = (f32[128,2304]{1,0:T(8,128)}, f32[128,2304]{1,0:T(8,128)}, u32[]{:S(2)}, u32[]{:S(2)}) collective-permute-start(f32[128,2304]{1,0:T(8,128)} %refs_0_.1), channel_id=1, source_target_pairs={{0,1},{1,0},{2,3},{3,2},{4,5},{5,4},{6,7},{7,6},{8,9},{9,8},{10,11... | collective-permute-start | bytes 3538952 | tf_op jit(solution)/shard_map/ppermute | solution.py:195
  44.8 3.3 %copy-done.1 = bf16[3,576,2304]{2,1,0:T(8,128)(2,1)S(1)} copy-done((bf16[3,576,2304]{2,1,0:T(8,128)(2,1)S(1)}, bf16[3,576,2304]{2,1,0:T(8,128)(2,1)}, u32[]{:S(2)}) %copy-start.1) | copy-done | bytes 7962648
  48.0 3.3 %latent.1.refs_4_ = f32[128,576]{1,0:T(8,128)S(1)} custom-call(f32[128,2304]{1,0:T(8,128)S(1)} %bitcast.9, bf16[3,576,2304]{2,1,0:T(8,128)(2,1)S(1)} %copy-done.1, f32[1,512]{1,0:T(1,128)S(1)} %bitcast.16), custom_call_target="tpu_custom_call" | custom-call | tf_op jit(solution)/shard_map/latent/pallas_call | solution.py:59
  52.2 1.9 %collective-permute-start.5 = (f32[128,576]{1,0:T(8,128)S(1)}, f32[128,576]{1,0:T(8,128)}, u32[]{:S(2)}, u32[]{:S(2)}) collective-permute-start(f32[128,576]{1,0:T(8,128)S(1)} %latent.1.refs_4_), channel_id=1, source_target_pairs={{0,224},{32,0},{64,32},{96,64},{128,96},{160,128},{192,160},{224,1... | collective-permute-start | bytes 884744 | tf_op jit(solution)/shard_map/ppermute | solution.py:200
  55.1 3.8 %query.1.refs_0_ = f32[2,128,192]{2,1,0:T(8,128)S(1)} custom-call(f32[128,2304]{1,0:T(8,128)S(1)} %bitcast.10, f32[192,2304]{1,0:T(8,128)S(1)} %bitcast.14, f32[192,2304]{1,0:T(8,128)} %bitcast.6.other_ref), custom_call_target="tpu_custom_call" | custom-call | tf_op jit(solution)/shard_map/query/pallas_call | solution.py:59
  60.6 1.4 %key_value_parts.1 = (bf16[3,512,256]{2,1,0:T(8,128)(2,1)S(1)}, bf16[2,512,256]{2,1,0:T(8,128)(2,1)S(1)}) custom-call(f32[512,128]{1,0:T(8,128)} %key_ref.1, f32[512,128]{1,0:T(8,128)S(1)} %copy-done.10, f32[512,128]{1,0:T(8,128)} %value_ref.1, f32[512,128]{1,0:T(8,128)} %collective-permute-done.3.far_value_ref), custom_call_target="tpu_custom_call" | custom-call | tf_op jit(solution)/shard_map/key_value_parts/pallas_call | solution.py:59
  62.8 1.0 %copy-done.7 = bf16[2,512,256]{2,1,0:T(8,128)(2,1)S(1)} copy-done((bf16[2,512,256]{2,1,0:T(8,128)(2,1)S(1)}, bf16[2,512,256]{2,1,0:T(8,128)(2,1)}, u32[]{:S(2)}) %copy-start.7) | copy-done | bytes 524312
  63.9 9.1 %attend.1 = (f32[2,128,256]{2,1,0:T(8,128)S(1)}, f32[2,128,256]{2,1,0:T(8,128)S(1)}) custom-call(s32[2]{0:T(128)S(1)} %pad_add_fusion.place_ref, f32[2,128,192]{2,1,0:T(8,128)S(1)} %query.1.refs_0_, f32[2,128,192]{2,1,0:T(8,128)} %collective-permute-done.1.refs_1_, bf16[3,512,256]{2,1,0:T(8,128)(2,1)S(1)} %get-tuple-element.13.refs_2_, ...), custom_call_target="tpu_custom_call" | custom-call | tf_op jit(solution)/shard_map/attend/pallas_call | solution.py:59
  73.0 4.5 %collective-permute-start.11 = (f32[2,128,256]{2,1,0:T(8,128)S(1)}, f32[2,128,256]{2,1,0:T(8,128)S(1)}, u32[]{:S(2)}, u32[]{:S(2)}) collective-permute-start(f32[2,128,256]{2,1,0:T(8,128)S(1)} %get-tuple-element.16), channel_id=1, source_target_pairs={{0,1},{1,0},{2,3},{3,2},{4,5},{5,4},{6,7},{7,6},{8,9},{9,8},{10,11... | collective-permute-start | bytes 786440 | tf_op jit(solution)/shard_map/ppermute | solution.py:195
  77.5 1.6 %out_parts.1.out_w_ref = bf16[2,256,2304]{2,1,0:T(8,128)(2,1)S(1)} custom-call(f32[128,2304]{1,0:T(8,128)S(1)} %copy-done.5, f32[128,2304]{1,0:T(8,128)} %collective-permute-done.12.refs_1_), custom_call_target="tpu_custom_call" | custom-call | tf_op jit(solution)/shard_map/out_parts/pallas_call | solution.py:59
  79.9 21.2 %all_to_all.15 = f32[16,8,2304]{2,1,0:T(8,128)S(1)} all-to-all(f32[16,8,2304]{2,1,0:T(8,128)S(1)} %bitcast.13), channel_id=1, replica_groups={{0,2,4,6,8,10,12,14,16,18,20,22,24,26,28,30},{1,3,5,7,9,11,13,15,17,19,..., dimensions={0} | all-to-all | bytes 2359296 | tf_op jit(solution)/shard_map/all_to_all | solution.py:206
  (43 shorter events, 7.5 us)
Async XLA Ops:
  2.0 33.1 %all-to-all-start = ((f32[16,8,2304]{2,1,0:T(8,128)}), f32[16,8,2304]{2,1,0:T(8,128)S(1)}, u32[]{:S(2)}, u32[]{:S(2)}) async-start(f32[16,8,2304]{2,1,0:T(8,128)} %broadcast_in_dim.4), calls=%async_computation | async-start | bytes 2359296 | tf_op jit(solution)/shard_map/all_to_all | solution.py:206
  9.6 44.5 %collective-permute-start = (f32[2304,192]{0,1:T(8,128)}, f32[2304,192]{0,1:T(8,128)}, u32[]{:S(2)}, u32[]{:S(2)}) collective-permute-start(f32[2304,192]{0,1:T(8,128)} %param.8), channel_id=1, source_target_pairs={{0,1},{1,0},{2,3},{3,2},{4,5},{5,4},{6,7},{7,6},{8,9},{9,8},{10,11... | collective-permute-start | bytes 5308424 | tf_op jit(solution)/shard_map/ppermute | solution.py:195
  10.6 2.5 %copy-start.3 = (f32[2304,576]{0,1:T(8,128)S(1)}, f32[2304,576]{0,1:T(8,128)}, u32[]{:S(2)}) copy-start(f32[2304,576]{0,1:T(8,128)} %param.9) | copy-start | bytes 15925252
  13.2 1.5 %copy-start.8 = (f32[8,2304]{1,0:T(8,128)S(1)}, f32[8,2304]{1,0:T(8,128)}, u32[]{:S(2)}) copy-start(f32[8,2304]{1,0:T(8,128)} %x_ref.1) | copy-start | bytes 221188
  13.2 1.5 %copy-start.11 = (f32[512]{0:T(512)S(1)}, f32[512]{0:T(512)}, u32[]{:S(2)}) copy-start(f32[512]{0:T(512)} %param.10) | copy-start | bytes 6148
  14.7 3.1 %copy-start = (bf16[3,576,2304]{2,1,0:T(8,128)(2,1)}, bf16[3,576,2304]{2,1,0:T(8,128)(2,1)S(1)}, u32[]{:S(2)}) copy-start(bf16[3,576,2304]{2,1,0:T(8,128)(2,1)S(1)} %down_parts.1.down_ref) | copy-start | bytes 23887876
  17.8 12.6 %collective-permute-start.6 = (f32[8,576]{1,0:T(8,128)S(1)}, f32[8,576]{1,0:T(8,128)S(1)}, u32[]{:S(2)}, u32[]{:S(2)}) collective-permute-start(f32[8,576]{1,0:T(8,128)S(1)} %own_latent.1), channel_id=1, source_target_pairs={{0,64},{32,96},{64,128},{96,160},{128,192},{160,224},{192,0},{224,... | collective-permute-start | bytes 55304 | tf_op jit(solution)/shard_map/ppermute | solution.py:200
  20.7 12.0 %collective-permute-start.7 = (f32[8,576]{1,0:T(8,128)S(1)}, f32[8,576]{1,0:T(8,128)S(1)}, u32[]{:S(2)}, u32[]{:S(2)}) collective-permute-start(f32[8,576]{1,0:T(8,128)S(1)} %own_latent.1), channel_id=1, source_target_pairs={{0,96},{32,128},{64,160},{96,192},{128,224},{160,0},{192,32},{224,... | collective-permute-start | bytes 55304 | tf_op jit(solution)/shard_map/ppermute | solution.py:200
  25.4 7.3 %collective-permute-start.8 = (f32[8,576]{1,0:T(8,128)S(1)}, f32[8,576]{1,0:T(8,128)S(1)}, u32[]{:S(2)}, u32[]{:S(2)}) collective-permute-start(f32[8,576]{1,0:T(8,128)S(1)} %own_latent.1), channel_id=1, source_target_pairs={{0,128},{32,160},{64,192},{96,224},{128,0},{160,32},{192,64},{224,... | collective-permute-start | bytes 55304 | tf_op jit(solution)/shard_map/ppermute | solution.py:200
  26.3 6.4 %collective-permute-start.9 = (f32[8,576]{1,0:T(8,128)S(1)}, f32[8,576]{1,0:T(8,128)S(1)}, u32[]{:S(2)}, u32[]{:S(2)}) collective-permute-start(f32[8,576]{1,0:T(8,128)S(1)} %own_latent.1), channel_id=1, source_target_pairs={{0,160},{32,192},{64,224},{96,0},{128,32},{160,64},{192,96},{224,1... | collective-permute-start | bytes 55304 | tf_op jit(solution)/shard_map/ppermute | solution.py:200
  30.3 3.5 %collective-permute-start.10 = (f32[8,576]{1,0:T(8,128)S(1)}, f32[8,576]{1,0:T(8,128)S(1)}, u32[]{:S(2)}, u32[]{:S(2)}) collective-permute-start(f32[8,576]{1,0:T(8,128)S(1)} %own_latent.1), channel_id=1, source_target_pairs={{0,192},{32,224},{64,0},{96,32},{128,64},{160,96},{192,128},{224,1... | collective-permute-start | bytes 55304 | tf_op jit(solution)/shard_map/ppermute | solution.py:200
  34.0 1.2 %copy-start.2 = (f32[16,5,8,576]{3,2,1,0:T(8,128)}, f32[16,5,8,576]{3,2,1,0:T(8,128)S(1)}, u32[]{:S(2)}) copy-start(f32[16,5,8,576]{3,2,1,0:T(8,128)S(1)} %far_copies.1) | copy-start | bytes 4423684
  35.2 27.7 %all-to-all-start.1 = ((f32[16,5,8,576]{3,2,1,0:T(8,128)}), f32[16,5,8,576]{3,2,1,0:T(8,128)S(1)}, u32[]{:S(2)}, u32[]{:S(2)}) async-start(f32[16,5,8,576]{3,2,1,0:T(8,128)} %copy-done.2), calls=%async_computation.1 | async-start | bytes 3276800 | tf_op jit(solution)/shard_map/all_to_all | solution.py:206
  42.0 35.4 %collective-permute-start.12 = (f32[128,2304]{1,0:T(8,128)}, f32[128,2304]{1,0:T(8,128)}, u32[]{:S(2)}, u32[]{:S(2)}) collective-permute-start(f32[128,2304]{1,0:T(8,128)} %refs_0_.1), channel_id=1, source_target_pairs={{0,1},{1,0},{2,3},{3,2},{4,5},{5,4},{6,7},{7,6},{8,9},{9,8},{10,11... | collective-permute-start | bytes 3538952 | tf_op jit(solution)/shard_map/ppermute | solution.py:195
  44.7 14.2 %collective-permute-start.2 = (f32[512,128]{1,0:T(8,128)}, f32[512,128]{1,0:T(8,128)S(1)}, u32[]{:S(2)}, u32[]{:S(2)}) collective-permute-start(f32[512,128]{1,0:T(8,128)} %key_ref.1), channel_id=1, source_target_pairs={{0,1},{1,0},{2,3},{3,2},{4,5},{5,4},{6,7},{7,6},{8,9},{9,8},{10,11... | collective-permute-start | bytes 786440 | tf_op jit(solution)/shard_map/ppermute | solution.py:195
  44.8 3.3 %copy-start.1 = (bf16[3,576,2304]{2,1,0:T(8,128)(2,1)S(1)}, bf16[3,576,2304]{2,1,0:T(8,128)(2,1)}, u32[]{:S(2)}) copy-start(bf16[3,576,2304]{2,1,0:T(8,128)(2,1)} %copy-done) | copy-start | bytes 23887876
  48.0 7.1 %copy-start.4 = (f32[2304,192]{0,1:T(8,128)S(1)}, f32[2304,192]{0,1:T(8,128)}, u32[]{:S(2)}) copy-start(f32[2304,192]{0,1:T(8,128)} %param.8) | copy-start | bytes 5308420
  51.4 11.4 %collective-permute-start.4 = (f32[128,576]{1,0:T(8,128)S(1)}, f32[128,576]{1,0:T(8,128)}, u32[]{:S(2)}, u32[]{:S(2)}) collective-permute-start(f32[128,576]{1,0:T(8,128)S(1)} %latent.1.refs_4_), channel_id=1, source_target_pairs={{0,32},{32,64},{64,96},{96,128},{128,160},{160,192},{192,224},{224... | collective-permute-start | bytes 884744 | tf_op jit(solution)/shard_map/ppermute | solution.py:200
  52.2 10.6 %collective-permute-start.5 = (f32[128,576]{1,0:T(8,128)S(1)}, f32[128,576]{1,0:T(8,128)}, u32[]{:S(2)}, u32[]{:S(2)}) collective-permute-start(f32[128,576]{1,0:T(8,128)S(1)} %latent.1.refs_4_), channel_id=1, source_target_pairs={{0,224},{32,0},{64,32},{96,64},{128,96},{160,128},{192,160},{224,1... | collective-permute-start | bytes 884744 | tf_op jit(solution)/shard_map/ppermute | solution.py:200
  54.1 5.5 %collective-permute-start.3 = (f32[512,128]{1,0:T(8,128)}, f32[512,128]{1,0:T(8,128)}, u32[]{:S(2)}, u32[]{:S(2)}) collective-permute-start(f32[512,128]{1,0:T(8,128)} %value_ref.1), channel_id=1, source_target_pairs={{0,1},{1,0},{2,3},{3,2},{4,5},{5,4},{6,7},{7,6},{8,9},{9,8},{10,11... | collective-permute-start | bytes 786440 | tf_op jit(solution)/shard_map/ppermute | solution.py:195
  59.6 3.3 %collective-permute-start.1 = (f32[2,128,192]{2,1,0:T(8,128)S(1)}, f32[2,128,192]{2,1,0:T(8,128)}, u32[]{:S(2)}, u32[]{:S(2)}) collective-permute-start(f32[2,128,192]{2,1,0:T(8,128)S(1)} %query.1.refs_0_), channel_id=1, source_target_pairs={{0,1},{1,0},{2,3},{3,2},{4,5},{5,4},{6,7},{7,6},{8,9},{9,8},{10,11... | collective-permute-start | bytes 589832 | tf_op jit(solution)/shard_map/ppermute | solution.py:195
  62.8 1.0 %copy-start.7 = (bf16[2,512,256]{2,1,0:T(8,128)(2,1)S(1)}, bf16[2,512,256]{2,1,0:T(8,128)(2,1)}, u32[]{:S(2)}) copy-start(bf16[2,512,256]{2,1,0:T(8,128)(2,1)} %copy-done.6) | copy-start | bytes 1572868
  63.9 13.6 %copy-start.5 = (f32[128,2304]{1,0:T(8,128)S(1)}, f32[128,2304]{1,0:T(8,128)}, u32[]{:S(2)}) copy-start(f32[128,2304]{1,0:T(8,128)} %refs_0_.1) | copy-start | bytes 3538948
  73.0 6.1 %collective-permute-start.11 = (f32[2,128,256]{2,1,0:T(8,128)S(1)}, f32[2,128,256]{2,1,0:T(8,128)S(1)}, u32[]{:S(2)}, u32[]{:S(2)}) collective-permute-start(f32[2,128,256]{2,1,0:T(8,128)S(1)} %get-tuple-element.16), channel_id=1, source_target_pairs={{0,1},{1,0},{2,3},{3,2},{4,5},{5,4},{6,7},{7,6},{8,9},{9,8},{10,11... | collective-permute-start | bytes 786440 | tf_op jit(solution)/shard_map/ppermute | solution.py:195
  (3 other events, 2.5 us)

commit v3 on v2

--- a/solution.py
+++ b/solution.py
@@ -9,6 +9,7 @@
 
 EPSILON = 1e-06
 FLOOR = -1e30
+LOG2E = 1.4426950408889634
 RING = (1, -1)
 FAR = (2, 3, 4, 5, 6)
 F32 = jnp.float32
@@ -48,10 +49,7 @@
 
 
 def three(left, right, dot):
-    high, low = left[:2]
-    rows = high.shape[0]
-    by_high = dot(jnp.concatenate([high, low], axis=0), right[0])
-    return by_high[:rows] + (by_high[rows:] + dot(high, right[1]))
+    return dot(left[1], right[0]) + dot(left[0], right[1]) + dot(left[0], right[0])
 
 
 def call(kernel, outs, operands, name, place=None):
@@ -92,7 +90,7 @@
 def own_kernel(x_ref, down_ref, gain_ref, out_ref):
     rows = x_ref.shape[0]
     x = jnp.concatenate([part.astype(F32) for part in split(x_ref[...], 3)], axis=0).astype(BF16)
-    high, middle, low = (nt(down_ref[part], x) for part in range(3))
+    high, middle, low = (nt(part, x) for part in split(down_ref[...], 3))
     total = high[:, :rows] + (
         (high[:, rows : 2 * rows] + middle[:, :rows])
         + (high[:, 2 * rows :] + middle[:, rows : 2 * rows] + low[:, :rows])
@@ -101,7 +99,7 @@
 
 
 def latent_kernel(x_ref, down_ref, gain_ref, out_ref):
-    down = six(split(x_ref[...], 3), [down_ref[part] for part in range(3)], nt)
+    down = six(split(x_ref[...], 3), split(down_ref[...], 3), nt)
     normed(down, gain_ref[...], out_ref)
 
 
@@ -116,15 +114,13 @@
 
 
 def attend_kernel(rows, scale, blocks, place_ref, *refs):
-    mine_ref, theirs_ref, key_ref, value_ref = refs[:4]
-    near_refs, far_ref = refs[4:-3], refs[-3]
+    mine_ref, theirs_ref, key_ref, far_key_ref, value_ref, far_value_ref = refs[:6]
+    near_refs, far_ref = refs[6:-3], refs[-3]
     out_refs = refs[-2:]
     ctx, core = place_ref[0], place_ref[1]
-    rank = key_ref.shape[1]
-    heads = mine_ref.shape[0]
-    half = mine_ref.shape[1]
-    nope = key_ref.shape[2] // heads
-    vdim = value_ref.shape[2] // heads
+    rank, nope = key_ref.shape
+    vdim = value_ref.shape[1]
+    heads, half, _ = mine_ref.shape
     count = 2 * half
 
     row = lax.broadcasted_iota(jnp.int32, (count, 1), 0)
@@ -145,15 +141,26 @@
     k_pos = block * count + block_offset(within // rows, lax.rem(within, rows), core, rows)
     causal = q_pos >= k_pos
 
-    compressed = split(latent[:, :rank], 3)
-    keys = six(compressed, [key_ref[part] for part in range(3)], nn)
-    values = three(compressed, [value_ref[part] for part in range(2)], nn)
+    compressed = split(latent[:, :rank], 2)
+    key_up = jnp.concatenate([key_ref[...], far_key_ref[...]], axis=1)
+    value_up = jnp.concatenate([value_ref[...], far_value_ref[...]], axis=1)
+    keys = three(compressed, split(key_up, 2), nn)
+    values = three(compressed, split(value_up, 2), nn)
+    high, middle, low = split(latent[:, rank:], 3)
+    shared_keys = [high, middle, low, high, middle, high]
     for head in range(heads):
-        key = jnp.concatenate([keys[:, head * nope : (head + 1) * nope], latent[:, rank:]], axis=1)
+        high, low = split(keys[:, head * nope : (head + 1) * nope], 2)
+        key = jnp.concatenate([high, low, high, *shared_keys], axis=1)
         query = jnp.concatenate([mine_ref[head], theirs_ref[heads - 1 - head]], axis=0)
-        scores = jnp.where(causal, six(split(query, 3), split(key, 3), nt) * scale, FLOOR)
+        query = query * (scale * LOG2E)
+        high, low = split(query[:, :nope], 2)
+        own_queries = [low, high, high]
+        high, middle, low = split(query[:, nope:], 3)
+        shared_queries = [low, middle, high, middle, high, high]
+        scores = nt(jnp.concatenate(own_queries + shared_queries, axis=1), key)
+        scores = jnp.where(causal, scores, FLOOR)
         top = jnp.max(scores, axis=1, keepdims=True)
-        weight = jnp.where(causal, jnp.exp(scores - top), 0.0)
+        weight = jnp.exp2(scores - top)
         total = jnp.sum(weight, axis=1, keepdims=True)
         value = split(values[:, head * vdim : (head + 1) * vdim], 2)
         acc = three(split(weight, 2), value, nn)
@@ -173,21 +180,11 @@
         other = arrived_ref[heads - 1 - head]
         m0, m1 = mine[:, vdim : vdim + 1], other[:, vdim : vdim + 1]
         top = jnp.maximum(m0, m1)
-        f0, f1 = jnp.exp(m0 - top), jnp.exp(m1 - top)
+        f0, f1 = jnp.exp2(m0 - top), jnp.exp2(m1 - top)
         total = mine[:, vdim + 64 : vdim + 65] * f0 + other[:, vdim + 64 : vdim + 65] * f1
         attended.append((mine[:, :vdim] * f0 + other[:, :vdim] * f1) / total)
     left = split(jnp.concatenate(attended, axis=1), 2)
     out_ref[...] = three(left, [out_w_ref[part] for part in range(2)], nn)
-
-
-def key_value_kernel(key_ref, far_key_ref, value_ref, far_value_ref, keys_ref, values_ref):
-    nope, vdim = key_ref.shape[1], value_ref.shape[1]
-    for number, ref in enumerate((key_ref, far_key_ref)):
-        for part, value in enumerate(split(ref[...], 3)):
-            keys_ref[part, :, number * nope : (number + 1) * nope] = value
-    for number, ref in enumerate((value_ref, far_value_ref)):
-        for part, value in enumerate(split(ref[...], 2)):
-            values_ref[part, :, number * vdim : (number + 1) * vdim] = value
 
 
 def partner(array):
@@ -224,7 +221,6 @@
     blocks = lax.axis_size("ctx")
     places = lax.axis_size("head") // 2
     half = places * rows
-    rank, nope = w_key_up.shape
     vdim = w_value_up.shape[1]
     width = w_down.shape[1]
     place = jnp.stack([lax.axis_index("ctx"), lax.axis_index("head") & 1]).astype(jnp.int32)
@@ -234,18 +230,12 @@
     far_query, far_key, far_value, far_out = (
         partner(weight) for weight in (w_query, w_key_up, w_value_up, w_out)
     )
-    down_parts = call(
-        functools.partial(split_kernel, 3),
-        shape(3, width, depth, dtype=BF16),
-        [w_down.T],
-        "down_parts",
-    )
-    own = call(own_kernel, shape(rows, width), [hidden, down_parts, gain], "own_latent")
+    own = call(own_kernel, shape(rows, width), [hidden, w_down.T, gain], "own_latent")
     far = [from_behind(own, step) for step in FAR]
     far_copies = call(spread_kernel, shape(places, len(FAR), rows, width), far, "far_copies")
     far_latent = exchange(far_copies).reshape(-1, width)
 
-    latent = call(latent_kernel, shape(half, width), [mine, down_parts, gain], "latent")
+    latent = call(latent_kernel, shape(half, width), [mine, w_down.T, gain], "latent")
     ring = [from_behind(latent, step) for step in RING]
 
     mine, far_query, _ = lax.optimization_barrier((mine, far_query, latent))
@@ -256,12 +246,6 @@
         "query",
     )
     other_queries = partner(queries)
-    key_parts, value_parts = call(
-        key_value_kernel,
-        [shape(3, rank, 2 * nope, dtype=BF16), shape(2, rank, 2 * vdim, dtype=BF16)],
-        [w_key_up, far_key, w_value_up, far_value],
-        "key_value_parts",
-    )
     out_parts = call(
         functools.partial(split_kernel, 2),
         shape(2, 2 * vdim, depth, dtype=BF16),
@@ -269,10 +253,21 @@
         "out_parts",
     )
 
+    latent, out_parts = lax.optimization_barrier((latent, out_parts))
     state = call(
         functools.partial(attend_kernel, rows, w_query.shape[1] ** (-0.5), blocks),
         [shape(2, half, 2 * vdim)] * 2,
-        [queries, other_queries, key_parts, value_parts, latent, *ring, far_latent],
+        [
+            queries,
+            other_queries,
+            w_key_up,
+            far_key,
+            w_value_up,
+            far_value,
+            latent,
+            *ring,
+            far_latent,
+        ],
         "attend",
         place,
     )

time: 102 us -> 96.2 us (0.943)
  Pallas kernels: 24.2 us -> 18.1 us
  waiting for transfers between devices: 1.17 us -> 3.57 us
  local copies, waits for them, and re-layouts: 12.9 us -> 10.7 us
    pallas_call x9 -> x7, Pallas kernels: 24.2 us -> 18.1 us  [call(): pl.pallas_call(kernel, out_shape=outs, in_specs=[pl.BlockSpec(memory_spac...]
    unnamed x24 -> x16, local copies, waits for them, and re-layouts: 10.9 us -> 8.58 us
    ppermute x6, starting transfers between devices: 9.26 us -> 7.99 us  [partner(): return lax.ppermute(array, 'head', [(h, h ^ 1) for h in range(size)])]
    ppermute x7, waiting for transfers between devices: 1.15 us -> 2.39 us  [from_behind(): lax.ppermute(array, 'ctx', [(c, (c + step) % size) for c in range(size)])]
    ppermute x6, waiting for transfers between devices: 0.02 us -> 1.18 us  [partner(): return lax.ppermute(array, 'head', [(h, h ^ 1) for h in range(size)])]
  transfers between devices with their start and end apart: 15 -> 15, of which waited for: 1 -> 3; matrix products, arithmetic and copies ran while one was open for 0% -> 0% of each run, Pallas kernels for 23% -> 12%
where the time goes in v3:
time: 96.2 us; the launch traced here: 95.7 us
  starting transfers between devices  41.1 us (43%)
  blocking collectives  21.3 us (22%)
  Pallas kernels  18.1 us (19%)
  local copies, waits for them, and re-layouts  10.7 us (11%)
  waiting for transfers between devices  3.57 us (4%)
    all_to_all x1, blocking collectives, exchange(): lax.all_to_all(pieces, 'head', split_axis=0, concat_axis=0, tiled=True, a...  21.3 us
    ppermute x7, starting transfers between devices, from_behind(): lax.ppermute(array, 'ctx', [(c, (c + step) % size) for c in range(size)])  18.5 us
    pallas_call x7, Pallas kernels, call(): pl.pallas_call(kernel, out_shape=outs, in_specs=[pl.BlockSpec(memory_spac...  18.1 us
    all_to_all x2, starting transfers between devices, exchange(): lax.all_to_all(pieces, 'head', split_axis=0, concat_axis=0, tiled=True, a...  14.6 us
    unnamed x16, local copies, waits for them, and re-layouts  8.58 us
    ppermute x6, starting transfers between devices, partner(): return lax.ppermute(array, 'head', [(h, h ^ 1) for h in range(size)])  7.99 us
    ppermute x7, waiting for transfers between devices, from_behind(): lax.ppermute(array, 'ctx', [(c, (c + step) % size) for c in range(size)])  2.39 us
    broadcast_in_dim x1, local copies, waits for them, and re-layouts, spread(): return exchange(jnp.broadcast_to(array[None], (places, *array.shape)))  2.13 us
  transfers between devices with their start and end apart: 15, of which 3 were waited for; matrix products, arithmetic and copies ran while one was open for 0% of the time, Pallas kernels for 12%

profile of v3, /device:TPU:1, one launch (start us, length us, event | category | flops | bytes accessed | tf_op | source)
XLA Modules:
  0.0 95.7 jit_solution(15869477719768538994)
XLA Ops:
  0.0 2.1 %broadcast_in_dim.4 = f32[16,8,2304]{2,1,0:T(8,128)} broadcast(f32[8,2304]{1,0:T(8,128)} %x_ref.1), dimensions={1,2} | broadcast | bytes 1253376 | tf_op jit(solution)/shard_map/broadcast_in_dim | solution.py:216
  2.1 7.6 %all-to-all-start = ((f32[16,8,2304]{2,1,0:T(8,128)}), f32[16,8,2304]{2,1,0:T(8,128)S(1)}, u32[]{:S(2)}, u32[]{:S(2)}) async-start(f32[16,8,2304]{2,1,0:T(8,128)} %broadcast_in_dim.4), calls=%async_computation | async-start | bytes 2359296 | tf_op jit(solution)/shard_map/all_to_all | solution.py:203
  9.7 1.0 %collective-permute-start = (f32[2304,192]{0,1:T(8,128)S(1)}, f32[2304,192]{0,1:T(8,128)}, u32[]{:S(2)}, u32[]{:S(2)}) collective-permute-start(f32[2304,192]{0,1:T(8,128)S(1)} %copy-done.2), channel_id=1, source_target_pairs={{0,1},{1,0},{2,3},{3,2},{4,5},{5,4},{6,7},{7,6},{8,9},{9,8},{10,11... | collective-permute-start | bytes 5308424 | tf_op jit(solution)/shard_map/ppermute | solution.py:192
  10.8 2.5 %copy-done = f32[2304,576]{0,1:T(8,128)S(1)} copy-done((f32[2304,576]{0,1:T(8,128)S(1)}, f32[2304,576]{0,1:T(8,128)}, u32[]{:S(2)}) %copy-start) | copy-done | bytes 5308440
  13.3 2.6 %own_latent.1 = f32[8,576]{1,0:T(8,128)S(1)} custom-call(f32[8,2304]{1,0:T(8,128)S(1)} %copy-done.6, f32[576,2304]{1,0:T(8,128)S(1)} %bitcast.9, f32[1,512]{1,0:T(1,128)S(1)} %bitcast.15), custom_call_target="tpu_custom_call" | custom-call | tf_op jit(solution)/shard_map/own_latent/pallas_call | solution.py:57
  15.9 6.5 %collective-permute-start.10 = (f32[8,576]{1,0:T(8,128)S(1)}, f32[8,576]{1,0:T(8,128)S(1)}, u32[]{:S(2)}, u32[]{:S(2)}) collective-permute-start(f32[8,576]{1,0:T(8,128)S(1)} %own_latent.1), channel_id=1, source_target_pairs={{0,160},{32,192},{64,224},{96,0},{128,32},{160,64},{192,96},{224,1... | collective-permute-start | bytes 55304 | tf_op jit(solution)/shard_map/ppermute | solution.py:197
  22.6 2.1 %collective-permute-start.7 = (f32[8,576]{1,0:T(8,128)S(1)}, f32[8,576]{1,0:T(8,128)S(1)}, u32[]{:S(2)}, u32[]{:S(2)}) collective-permute-start(f32[8,576]{1,0:T(8,128)S(1)} %own_latent.1), channel_id=1, source_target_pairs={{0,64},{32,96},{64,128},{96,160},{128,192},{160,224},{192,0},{224,... | collective-permute-start | bytes 55304 | tf_op jit(solution)/shard_map/ppermute | solution.py:197
  25.2 4.5 %collective-permute-start.9 = (f32[8,576]{1,0:T(8,128)S(1)}, f32[8,576]{1,0:T(8,128)S(1)}, u32[]{:S(2)}, u32[]{:S(2)}) collective-permute-start(f32[8,576]{1,0:T(8,128)S(1)} %own_latent.1), channel_id=1, source_target_pairs={{0,128},{32,160},{64,192},{96,224},{128,0},{160,32},{192,64},{224,... | collective-permute-start | bytes 55304 | tf_op jit(solution)/shard_map/ppermute | solution.py:197
  30.4 1.7 %collective-permute-done.9.refs_2_ = f32[8,576]{1,0:T(8,128)S(1)} collective-permute-done((f32[8,576]{1,0:T(8,128)S(1)}, f32[8,576]{1,0:T(8,128)S(1)}, u32[]{:S(2)}, u32[]{:S(2)}) %collective-permute-start.9) | collective-permute-done | bytes 18464 | tf_op jit(solution)/shard_map/ppermute | solution.py:197
  32.1 1.3 %far_copies.1 = f32[16,5,8,576]{3,2,1,0:T(8,128)} custom-call(f32[8,576]{1,0:T(8,128)S(1)} %collective-permute-done.7.refs_0_, f32[8,576]{1,0:T(8,128)S(1)} %collective-permute-done.8.refs_1_, f32[8,576]{1,0:T(8,128)S(1)} %collective-permute-done.9.refs_2_, f32[8,576]{1,0:T(8,128)S(1)} %collective-permute-done.10.refs_3_, ...), custom_call_target="tpu_custom_call" | custom-call | tf_op jit(solution)/shard_map/far_copies/pallas_call | solution.py:57
  33.3 7.0 %all-to-all-start.1 = ((f32[16,5,8,576]{3,2,1,0:T(8,128)}), f32[16,5,8,576]{3,2,1,0:T(8,128)}, u32[]{:S(2)}, u32[]{:S(2)}) async-start(f32[16,5,8,576]{3,2,1,0:T(8,128)} %far_copies.1), calls=%async_computation.1 | async-start | bytes 3276800 | tf_op jit(solution)/shard_map/all_to_all | solution.py:203
  40.3 2.3 %collective-permute-start.4 = (f32[128,2304]{1,0:T(8,128)}, f32[128,2304]{1,0:T(8,128)S(1)}, u32[]{:S(2)}, u32[]{:S(2)}) collective-permute-start(f32[128,2304]{1,0:T(8,128)} %refs_0_.1), channel_id=1, source_target_pairs={{0,1},{1,0},{2,3},{3,2},{4,5},{5,4},{6,7},{7,6},{8,9},{9,8},{10,11... | collective-permute-start | bytes 3538952 | tf_op jit(solution)/shard_map/ppermute | solution.py:192
  42.6 2.5 %copy-done.1 = f32[2304,576]{0,1:T(8,128)S(1)} copy-done((f32[2304,576]{0,1:T(8,128)S(1)}, f32[2304,576]{0,1:T(8,128)}, u32[]{:S(2)}) %copy-start.1) | copy-done | bytes 5308440
  45.1 3.3 %latent.1.refs_6_ = f32[128,576]{1,0:T(8,128)S(1)} custom-call(f32[128,2304]{1,0:T(8,128)S(1)} %bitcast.11, f32[576,2304]{1,0:T(8,128)S(1)} %bitcast.10, f32[1,512]{1,0:T(1,128)S(1)} %bitcast.16), custom_call_target="tpu_custom_call" | custom-call | tf_op jit(solution)/shard_map/latent/pallas_call | solution.py:57
  48.5 1.9 %collective-permute-start.5 = (f32[128,576]{1,0:T(8,128)S(1)}, f32[128,576]{1,0:T(8,128)}, u32[]{:S(2)}, u32[]{:S(2)}) collective-permute-start(f32[128,576]{1,0:T(8,128)S(1)} %latent.1.refs_6_), channel_id=1, source_target_pairs={{0,32},{32,64},{64,96},{96,128},{128,160},{160,192},{192,224},{224... | collective-permute-start | bytes 884744 | tf_op jit(solution)/shard_map/ppermute | solution.py:197
  50.3 2.9 %collective-permute-start.6 = (f32[128,576]{1,0:T(8,128)S(1)}, f32[128,576]{1,0:T(8,128)}, u32[]{:S(2)}, u32[]{:S(2)}) collective-permute-start(f32[128,576]{1,0:T(8,128)S(1)} %latent.1.refs_6_), channel_id=1, source_target_pairs={{0,224},{32,0},{64,32},{96,64},{128,96},{160,128},{192,160},{224,1... | collective-permute-start | bytes 884744 | tf_op jit(solution)/shard_map/ppermute | solution.py:197
  53.7 3.8 %query.1.refs_0_ = f32[2,128,192]{2,1,0:T(8,128)S(1)} custom-call(f32[128,2304]{1,0:T(8,128)S(1)} %bitcast.12, f32[192,2304]{1,0:T(8,128)S(1)} %bitcast.14, f32[192,2304]{1,0:T(8,128)} %bitcast.6.other_ref), custom_call_target="tpu_custom_call" | custom-call | tf_op jit(solution)/shard_map/query/pallas_call | solution.py:57
  57.5 1.0 %copy-done.4 = f32[128,2304]{1,0:T(8,128)} copy-done((f32[128,2304]{1,0:T(8,128)}, f32[128,2304]{1,0:T(8,128)S(1)}, u32[]{:S(2)}) %copy-start.4) | copy-done | bytes 1179672
  58.9 1.3 %copy-done.3 = f32[128,2304]{1,0:T(8,128)S(1)} copy-done((f32[128,2304]{1,0:T(8,128)S(1)}, f32[128,2304]{1,0:T(8,128)}, u32[]{:S(2)}) %copy-start.3) | copy-done | bytes 1179672
  60.2 1.3 %copy-done.5 = f32[128,2304]{1,0:T(8,128)S(1)} copy-done((f32[128,2304]{1,0:T(8,128)S(1)}, f32[128,2304]{1,0:T(8,128)}, u32[]{:S(2)}) %copy-start.5) | copy-done | bytes 1179672
  61.8 5.9 %attend.1 = (f32[2,128,256]{2,1,0:T(8,128)S(1)}, f32[2,128,256]{2,1,0:T(8,128)S(1)}) custom-call(s32[2]{0:T(128)S(1)} %pad_add_fusion.place_ref, f32[2,128,192]{2,1,0:T(8,128)S(1)} %query.1.refs_0_, f32[2,128,192]{2,1,0:T(8,128)S(1)} %collective-permute-done.1.refs_1_, f32[512,128]{1,0:T(8,128)} %refs_2_.1, f32[512,128]{1,0:T(8,128)} %collective-permute-done.2.refs_3_, ...), custom_call_target="tpu_custom_call" | custom-call | tf_op jit(solution)/shard_map/attend/pallas_call | solution.py:57
  67.8 3.9 %collective-permute-start.12 = (f32[2,128,256]{2,1,0:T(8,128)S(1)}, f32[2,128,256]{2,1,0:T(8,128)S(1)}, u32[]{:S(2)}, u32[]{:S(2)}) collective-permute-start(f32[2,128,256]{2,1,0:T(8,128)S(1)} %get-tuple-element.15), channel_id=1, source_target_pairs={{0,1},{1,0},{2,3},{3,2},{4,5},{5,4},{6,7},{7,6},{8,9},{9,8},{10,11... | collective-permute-start | bytes 786440 | tf_op jit(solution)/shard_map/ppermute | solution.py:192
  71.7 1.2 %collective-permute-done.12.arrived_ref = f32[2,128,256]{2,1,0:T(8,128)S(1)} collective-permute-done((f32[2,128,256]{2,1,0:T(8,128)S(1)}, f32[2,128,256]{2,1,0:T(8,128)S(1)}, u32[]{:S(2)}, u32[]{:S(2)}) %collective-permute-start.12) | collective-permute-done | bytes 262176 | tf_op jit(solution)/shard_map/ppermute | solution.py:192
  73.7 21.3 %all_to_all.15 = f32[16,8,2304]{2,1,0:T(8,128)S(1)} all-to-all(f32[16,8,2304]{2,1,0:T(8,128)S(1)} %bitcast.13), channel_id=1, replica_groups={{0,2,4,6,8,10,12,14,16,18,20,22,24,26,28,30},{1,3,5,7,9,11,13,15,17,19,..., dimensions={0} | all-to-all | bytes 2359296 | tf_op jit(solution)/shard_map/all_to_all | solution.py:203
  (33 shorter events, 4.2 us)
Async XLA Ops:
  0.0 10.8 %copy-start.6 = (f32[8,2304]{1,0:T(8,128)S(1)}, f32[8,2304]{1,0:T(8,128)}, u32[]{:S(2)}) copy-start(f32[8,2304]{1,0:T(8,128)} %x_ref.1) | copy-start | bytes 221188
  0.0 9.7 %copy-start.2 = (f32[2304,192]{0,1:T(8,128)S(1)}, f32[2304,192]{0,1:T(8,128)}, u32[]{:S(2)}) copy-start(f32[2304,192]{0,1:T(8,128)} %param.8) | copy-start | bytes 5308420
  0.0 10.8 %copy-start.7 = (f32[512]{0:T(512)S(1)}, f32[512]{0:T(512)}, u32[]{:S(2)}) copy-start(f32[512]{0:T(512)} %param.10) | copy-start | bytes 6148
  2.1 31.2 %all-to-all-start = ((f32[16,8,2304]{2,1,0:T(8,128)}), f32[16,8,2304]{2,1,0:T(8,128)S(1)}, u32[]{:S(2)}, u32[]{:S(2)}) async-start(f32[16,8,2304]{2,1,0:T(8,128)} %broadcast_in_dim.4), calls=%async_computation | async-start | bytes 2359296 | tf_op jit(solution)/shard_map/all_to_all | solution.py:203
  9.7 43.8 %collective-permute-start = (f32[2304,192]{0,1:T(8,128)S(1)}, f32[2304,192]{0,1:T(8,128)}, u32[]{:S(2)}, u32[]{:S(2)}) collective-permute-start(f32[2304,192]{0,1:T(8,128)S(1)} %copy-done.2), channel_id=1, source_target_pairs={{0,1},{1,0},{2,3},{3,2},{4,5},{5,4},{6,7},{7,6},{8,9},{9,8},{10,11... | collective-permute-start | bytes 5308424 | tf_op jit(solution)/shard_map/ppermute | solution.py:192
  10.8 2.5 %copy-start = (f32[2304,576]{0,1:T(8,128)S(1)}, f32[2304,576]{0,1:T(8,128)}, u32[]{:S(2)}) copy-start(f32[2304,576]{0,1:T(8,128)} %param.9) | copy-start | bytes 15925252
  15.9 9.3 %collective-permute-start.10 = (f32[8,576]{1,0:T(8,128)S(1)}, f32[8,576]{1,0:T(8,128)S(1)}, u32[]{:S(2)}, u32[]{:S(2)}) collective-permute-start(f32[8,576]{1,0:T(8,128)S(1)} %own_latent.1), channel_id=1, source_target_pairs={{0,160},{32,192},{64,224},{96,0},{128,32},{160,64},{192,96},{224,1... | collective-permute-start | bytes 55304 | tf_op jit(solution)/shard_map/ppermute | solution.py:197
  22.4 7.3 %collective-permute-start.11 = (f32[8,576]{1,0:T(8,128)S(1)}, f32[8,576]{1,0:T(8,128)S(1)}, u32[]{:S(2)}, u32[]{:S(2)}) collective-permute-start(f32[8,576]{1,0:T(8,128)S(1)} %own_latent.1), channel_id=1, source_target_pairs={{0,192},{32,224},{64,0},{96,32},{128,64},{160,96},{192,128},{224,1... | collective-permute-start | bytes 55304 | tf_op jit(solution)/shard_map/ppermute | solution.py:197
  22.6 7.0 %collective-permute-start.7 = (f32[8,576]{1,0:T(8,128)S(1)}, f32[8,576]{1,0:T(8,128)S(1)}, u32[]{:S(2)}, u32[]{:S(2)}) collective-permute-start(f32[8,576]{1,0:T(8,128)S(1)} %own_latent.1), channel_id=1, source_target_pairs={{0,64},{32,96},{64,128},{96,160},{128,192},{160,224},{192,0},{224,... | collective-permute-start | bytes 55304 | tf_op jit(solution)/shard_map/ppermute | solution.py:197
  24.7 5.6 %collective-permute-start.8 = (f32[8,576]{1,0:T(8,128)S(1)}, f32[8,576]{1,0:T(8,128)S(1)}, u32[]{:S(2)}, u32[]{:S(2)}) collective-permute-start(f32[8,576]{1,0:T(8,128)S(1)} %own_latent.1), channel_id=1, source_target_pairs={{0,96},{32,128},{64,160},{96,192},{128,224},{160,0},{192,32},{224,... | collective-permute-start | bytes 55304 | tf_op jit(solution)/shard_map/ppermute | solution.py:197
  25.2 6.9 %collective-permute-start.9 = (f32[8,576]{1,0:T(8,128)S(1)}, f32[8,576]{1,0:T(8,128)S(1)}, u32[]{:S(2)}, u32[]{:S(2)}) collective-permute-start(f32[8,576]{1,0:T(8,128)S(1)} %own_latent.1), channel_id=1, source_target_pairs={{0,128},{32,160},{64,192},{96,224},{128,0},{160,32},{192,64},{224,... | collective-permute-start | bytes 55304 | tf_op jit(solution)/shard_map/ppermute | solution.py:197
  33.3 28.5 %all-to-all-start.1 = ((f32[16,5,8,576]{3,2,1,0:T(8,128)}), f32[16,5,8,576]{3,2,1,0:T(8,128)}, u32[]{:S(2)}, u32[]{:S(2)}) async-start(f32[16,5,8,576]{3,2,1,0:T(8,128)} %far_copies.1), calls=%async_computation.1 | async-start | bytes 3276800 | tf_op jit(solution)/shard_map/all_to_all | solution.py:203
  40.3 17.2 %collective-permute-start.4 = (f32[128,2304]{1,0:T(8,128)}, f32[128,2304]{1,0:T(8,128)S(1)}, u32[]{:S(2)}, u32[]{:S(2)}) collective-permute-start(f32[128,2304]{1,0:T(8,128)} %refs_0_.1), channel_id=1, source_target_pairs={{0,1},{1,0},{2,3},{3,2},{4,5},{5,4},{6,7},{7,6},{8,9},{9,8},{10,11... | collective-permute-start | bytes 3538952 | tf_op jit(solution)/shard_map/ppermute | solution.py:192
  42.6 2.5 %copy-start.1 = (f32[2304,576]{0,1:T(8,128)S(1)}, f32[2304,576]{0,1:T(8,128)}, u32[]{:S(2)}) copy-start(f32[2304,576]{0,1:T(8,128)} %param.9) | copy-start | bytes 15925252
  48.5 13.4 %collective-permute-start.5 = (f32[128,576]{1,0:T(8,128)S(1)}, f32[128,576]{1,0:T(8,128)}, u32[]{:S(2)}, u32[]{:S(2)}) collective-permute-start(f32[128,576]{1,0:T(8,128)S(1)} %latent.1.refs_6_), channel_id=1, source_target_pairs={{0,32},{32,64},{64,96},{96,128},{128,160},{160,192},{192,224},{224... | collective-permute-start | bytes 884744 | tf_op jit(solution)/shard_map/ppermute | solution.py:197
  50.3 11.5 %collective-permute-start.6 = (f32[128,576]{1,0:T(8,128)S(1)}, f32[128,576]{1,0:T(8,128)}, u32[]{:S(2)}, u32[]{:S(2)}) collective-permute-start(f32[128,576]{1,0:T(8,128)S(1)} %latent.1.refs_6_), channel_id=1, source_target_pairs={{0,224},{32,0},{64,32},{96,64},{128,96},{160,128},{192,160},{224,1... | collective-permute-start | bytes 884744 | tf_op jit(solution)/shard_map/ppermute | solution.py:197
  53.2 8.6 %collective-permute-start.2 = (f32[512,128]{1,0:T(8,128)}, f32[512,128]{1,0:T(8,128)}, u32[]{:S(2)}, u32[]{:S(2)}) collective-permute-start(f32[512,128]{1,0:T(8,128)} %refs_2_.1), channel_id=1, source_target_pairs={{0,1},{1,0},{2,3},{3,2},{4,5},{5,4},{6,7},{7,6},{8,9},{9,8},{10,11... | collective-permute-start | bytes 786440 | tf_op jit(solution)/shard_map/ppermute | solution.py:192
  53.5 8.3 %collective-permute-start.3 = (f32[512,128]{1,0:T(8,128)}, f32[512,128]{1,0:T(8,128)}, u32[]{:S(2)}, u32[]{:S(2)}) collective-permute-start(f32[512,128]{1,0:T(8,128)} %refs_4_.1), channel_id=1, source_target_pairs={{0,1},{1,0},{2,3},{3,2},{4,5},{5,4},{6,7},{7,6},{8,9},{9,8},{10,11... | collective-permute-start | bytes 786440 | tf_op jit(solution)/shard_map/ppermute | solution.py:192
  57.5 1.0 %copy-start.4 = (f32[128,2304]{1,0:T(8,128)}, f32[128,2304]{1,0:T(8,128)S(1)}, u32[]{:S(2)}) copy-start(f32[128,2304]{1,0:T(8,128)S(1)} %collective-permute-done.4.refs_1_) | copy-start | bytes 3538948
  58.5 3.3 %collective-permute-start.1 = (f32[2,128,192]{2,1,0:T(8,128)S(1)}, f32[2,128,192]{2,1,0:T(8,128)S(1)}, u32[]{:S(2)}, u32[]{:S(2)}) collective-permute-start(f32[2,128,192]{2,1,0:T(8,128)S(1)} %query.1.refs_0_), channel_id=1, source_target_pairs={{0,1},{1,0},{2,3},{3,2},{4,5},{5,4},{6,7},{7,6},{8,9},{9,8},{10,11... | collective-permute-start | bytes 589832 | tf_op jit(solution)/shard_map/ppermute | solution.py:192
  58.9 1.3 %copy-start.3 = (f32[128,2304]{1,0:T(8,128)S(1)}, f32[128,2304]{1,0:T(8,128)}, u32[]{:S(2)}) copy-start(f32[128,2304]{1,0:T(8,128)} %refs_0_.1) | copy-start | bytes 3538948
  60.2 1.3 %copy-start.5 = (f32[128,2304]{1,0:T(8,128)S(1)}, f32[128,2304]{1,0:T(8,128)}, u32[]{:S(2)}) copy-start(f32[128,2304]{1,0:T(8,128)} %copy-done.4) | copy-start | bytes 3538948
  67.8 5.0 %collective-permute-start.12 = (f32[2,128,256]{2,1,0:T(8,128)S(1)}, f32[2,128,256]{2,1,0:T(8,128)S(1)}, u32[]{:S(2)}, u32[]{:S(2)}) collective-permute-start(f32[2,128,256]{2,1,0:T(8,128)S(1)} %get-tuple-element.15), channel_id=1, source_target_pairs={{0,1},{1,0},{2,3},{3,2},{4,5},{5,4},{6,7},{7,6},{8,9},{9,8},{10,11... | collective-permute-start | bytes 786440 | tf_op jit(solution)/shard_map/ppermute | solution.py:192

commit v4 on v3

--- a/solution.py
+++ b/solution.py
@@ -26,30 +26,19 @@
     return lax.dot_general(left, right, (((1,), (1,)), ((), ())), preferred_element_type=F32)
 
 
-def split(array, count):
-    parts = []
-    for _ in range(count - 1):
-        part = array.astype(BF16)
-        parts.append(part)
-        array = array - part.astype(F32)
-    parts.append(array.astype(BF16))
-    return parts
-
-
-def six(left, right, dot):
-    high, middle, low = left
-    rows = high.shape[0]
-    by_high = dot(jnp.concatenate([high, middle, low], axis=0), right[0])
-    by_middle = dot(jnp.concatenate([high, middle], axis=0), right[1])
-    by_low = dot(high, right[2])
-    return by_high[:rows] + (
-        (by_high[rows : 2 * rows] + by_middle[:rows])
-        + (by_high[2 * rows :] + by_middle[rows:] + by_low)
-    )
-
-
-def three(left, right, dot):
+def split(array):
+    high = array.astype(BF16)
+    return high, (array - high.astype(F32)).astype(BF16)
+
+
+def product(left, right, dot):
     return dot(left[1], right[0]) + dot(left[0], right[1]) + dot(left[0], right[0])
+
+
+def stacked(left, right, dot):
+    rows = left[0].shape[0]
+    by_high = dot(jnp.concatenate(left, axis=0), right[0])
+    return by_high[:rows] + (by_high[rows:] + dot(left[0], right[1]))
 
 
 def call(kernel, outs, operands, name, place=None):
@@ -69,13 +58,12 @@
     return jax.ShapeDtypeStruct(dims, dtype)
 
 
-def split_kernel(count, *refs):
+def split_kernel(*refs):
     sources, outs = refs[:-1], refs[-1]
     start = 0
     for ref in sources:
         stop = start + ref.shape[0]
-        for part, value in enumerate(split(ref[...], count)):
-            outs[part, start:stop] = value
+        outs[0, start:stop], outs[1, start:stop] = split(ref[...])
         start = stop
 
 
@@ -89,24 +77,21 @@
 
 def own_kernel(x_ref, down_ref, gain_ref, out_ref):
     rows = x_ref.shape[0]
-    x = jnp.concatenate([part.astype(F32) for part in split(x_ref[...], 3)], axis=0).astype(BF16)
-    high, middle, low = (nt(part, x) for part in split(down_ref[...], 3))
-    total = high[:, :rows] + (
-        (high[:, rows : 2 * rows] + middle[:, :rows])
-        + (high[:, 2 * rows :] + middle[:, rows : 2 * rows] + low[:, :rows])
-    )
+    x = jnp.concatenate([part.astype(F32) for part in split(x_ref[...])], axis=0).astype(BF16)
+    high, low = (nt(part, x) for part in split(down_ref[...]))
+    total = high[:, :rows] + (high[:, rows:] + low[:, :rows])
     normed(total.T, gain_ref[...], out_ref)
 
 
 def latent_kernel(x_ref, down_ref, gain_ref, out_ref):
-    down = six(split(x_ref[...], 3), split(down_ref[...], 3), nt)
+    down = stacked(split(x_ref[...]), split(down_ref[...]), nt)
     normed(down, gain_ref[...], out_ref)
 
 
 def query_kernel(x_ref, own_ref, other_ref, out_ref):
-    x = split(x_ref[...], 3)
-    out_ref[0] = six(x, split(own_ref[...], 3), nt)
-    out_ref[1] = six(x, split(other_ref[...], 3), nt)
+    x = split(x_ref[...])
+    out_ref[0] = stacked(x, split(own_ref[...]), nt)
+    out_ref[1] = stacked(x, split(other_ref[...]), nt)
 
 
 def block_offset(place, row, cls, rows):
@@ -141,29 +126,29 @@
     k_pos = block * count + block_offset(within // rows, lax.rem(within, rows), core, rows)
     causal = q_pos >= k_pos
 
-    compressed = split(latent[:, :rank], 2)
+    high, low = split(latent)
+    compressed = high[:, :rank], low[:, :rank]
     key_up = jnp.concatenate([key_ref[...], far_key_ref[...]], axis=1)
     value_up = jnp.concatenate([value_ref[...], far_value_ref[...]], axis=1)
-    keys = three(compressed, split(key_up, 2), nn)
-    values = three(compressed, split(value_up, 2), nn)
-    high, middle, low = split(latent[:, rank:], 3)
-    shared_keys = [high, middle, low, high, middle, high]
+    keys = split(product(compressed, split(key_up), nn))
+    values = split(product(compressed, split(value_up), nn))
+    shared = high[:, rank:], low[:, rank:]
     for head in range(heads):
-        high, low = split(keys[:, head * nope : (head + 1) * nope], 2)
-        key = jnp.concatenate([high, low, high, *shared_keys], axis=1)
+        high, low = (
+            jnp.concatenate([own[:, head * nope : (head + 1) * nope], other], axis=1)
+            for own, other in zip(keys, shared)
+        )
+        key = jnp.concatenate([high, low, high], axis=1)
         query = jnp.concatenate([mine_ref[head], theirs_ref[heads - 1 - head]], axis=0)
-        query = query * (scale * LOG2E)
-        high, low = split(query[:, :nope], 2)
-        own_queries = [low, high, high]
-        high, middle, low = split(query[:, nope:], 3)
-        shared_queries = [low, middle, high, middle, high, high]
-        scores = nt(jnp.concatenate(own_queries + shared_queries, axis=1), key)
+        high, low = split(query * (scale * LOG2E))
+        scores = nt(jnp.concatenate([low, high, high], axis=1), key)
         scores = jnp.where(causal, scores, FLOOR)
         top = jnp.max(scores, axis=1, keepdims=True)
         weight = jnp.exp2(scores - top)
         total = jnp.sum(weight, axis=1, keepdims=True)
-        value = split(values[:, head * vdim : (head + 1) * vdim], 2)
-        acc = three(split(weight, 2), value, nn)
+        acc = product(
+            split(weight), [part[:, head * vdim : (head + 1) * vdim] for part in values], nn
+        )
         for number, out_ref in enumerate(out_refs):
             chosen = slice(number * half, (number + 1) * half)
             out_ref[head, :, :vdim] = acc[chosen]
@@ -183,8 +168,8 @@
         f0, f1 = jnp.exp2(m0 - top), jnp.exp2(m1 - top)
         total = mine[:, vdim + 64 : vdim + 65] * f0 + other[:, vdim + 64 : vdim + 65] * f1
         attended.append((mine[:, :vdim] * f0 + other[:, :vdim] * f1) / total)
-    left = split(jnp.concatenate(attended, axis=1), 2)
-    out_ref[...] = three(left, [out_w_ref[part] for part in range(2)], nn)
+    left = split(jnp.concatenate(attended, axis=1))
+    out_ref[...] = stacked(left, [out_w_ref[part] for part in range(2)], nn)
 
 
 def partner(array):
@@ -232,6 +217,7 @@
     )
     own = call(own_kernel, shape(rows, width), [hidden, w_down.T, gain], "own_latent")
     far = [from_behind(own, step) for step in FAR]
+    far, far_out = lax.optimization_barrier((far, far_out))
     far_copies = call(spread_kernel, shape(places, len(FAR), rows, width), far, "far_copies")
     far_latent = exchange(far_copies).reshape(-1, width)
 
@@ -247,7 +233,7 @@
     )
     other_queries = partner(queries)
     out_parts = call(
-        functools.partial(split_kernel, 2),
+        split_kernel,
         shape(2, 2 * vdim, depth, dtype=BF16),
         [w_out, far_out],
         "out_parts",

time: 96.2 us -> 94.8 us (0.985)
  waiting for transfers between devices: 3.57 us -> 6.19 us
  local copies, waits for them, and re-layouts: 10.7 us -> 8.27 us
  Pallas kernels: 18.1 us -> 16.4 us
    ppermute x6, starting transfers between devices: 7.99 us -> 12.1 us  [partner(): return lax.ppermute(array, 'head', [(h, h ^ 1) for h in range(size)])]
    all_to_all x2, waiting for transfers between devices: 0.01 us -> 3.86 us  [exchange(): lax.all_to_all(pieces, 'head', split_axis=0, concat_axis=0, tiled=True, a...]
    all_to_all x2, starting transfers between devices: 14.6 us -> 12.1 us  [exchange(): lax.all_to_all(pieces, 'head', split_axis=0, concat_axis=0, tiled=True, a...]
    unnamed x16 -> x12, local copies, waits for them, and re-layouts: 8.58 us -> 6.29 us
    pallas_call x7, Pallas kernels: 18.1 us -> 16.4 us  [call(): pl.pallas_call(kernel, out_shape=outs, in_specs=[pl.BlockSpec(memory_spac...]
    ppermute x7, waiting for transfers between devices: 2.39 us -> 1.16 us  [from_behind(): lax.ppermute(array, 'ctx', [(c, (c + step) % size) for c in range(size)])]
  transfers between devices with their start and end apart: 15 -> 15, of which waited for: 3 -> 3; matrix products, arithmetic and copies ran while one was open for 0% -> 2% of each run, Pallas kernels for 12% -> 10%
where the time goes in v4:
time: 94.8 us; the launch traced here: 94.3 us
  starting transfers between devices  41.9 us (44%)
  blocking collectives  20.7 us (22%)
  Pallas kernels  16.4 us (17%)
  local copies, waits for them, and re-layouts  8.27 us (9%)
  waiting for transfers between devices  6.19 us (7%)
    all_to_all x1, blocking collectives, exchange(): lax.all_to_all(pieces, 'head', split_axis=0, concat_axis=0, tiled=True, a...  20.7 us
    ppermute x7, starting transfers between devices, from_behind(): lax.ppermute(array, 'ctx', [(c, (c + step) % size) for c in range(size)])  17.8 us
    pallas_call x7, Pallas kernels, call(): pl.pallas_call(kernel, out_shape=outs, in_specs=[pl.BlockSpec(memory_spac...  16.4 us
    ppermute x6, starting transfers between devices, partner(): return lax.ppermute(array, 'head', [(h, h ^ 1) for h in range(size)])  12.1 us
    all_to_all x2, starting transfers between devices, exchange(): lax.all_to_all(pieces, 'head', split_axis=0, concat_axis=0, tiled=True, a...  12.1 us
    unnamed x12, local copies, waits for them, and re-layouts  6.29 us
    all_to_all x2, waiting for transfers between devices, exchange(): lax.all_to_all(pieces, 'head', split_axis=0, concat_axis=0, tiled=True, a...  3.86 us
    broadcast_in_dim x1, local copies, waits for them, and re-layouts, spread(): return exchange(jnp.broadcast_to(array[None], (places, *array.shape)))  1.98 us
  transfers between devices with their start and end apart: 15, of which 3 were waited for; matrix products, arithmetic and copies ran while one was open for 2% of the time, Pallas kernels for 10%

profile of v4, /device:TPU:1, one launch (start us, length us, event | category | flops | bytes accessed | tf_op | source)
XLA Modules:
  0.0 94.3 jit_solution(8497746701460676990)
XLA Ops:
  0.0 3.2 %collective-permute-start.9 = (f32[128,2304]{1,0:T(8,128)}, f32[128,2304]{1,0:T(8,128)}, u32[]{:S(2)}, u32[]{:S(2)}) collective-permute-start(f32[128,2304]{1,0:T(8,128)} %refs_0_.1), channel_id=1, source_target_pairs={{0,1},{1,0},{2,3},{3,2},{4,5},{5,4},{6,7},{7,6},{8,9},{9,8},{10,11... | collective-permute-start | bytes 3538952 | tf_op jit(solution)/shard_map/ppermute | solution.py:177
  3.2 2.0 %broadcast_in_dim.4 = f32[16,8,2304]{2,1,0:T(8,128)} broadcast(f32[8,2304]{1,0:T(8,128)} %x_ref.1), dimensions={1,2} | broadcast | bytes 1253376 | tf_op jit(solution)/shard_map/broadcast_in_dim | solution.py:201
  5.2 5.1 %all-to-all-start = ((f32[16,8,2304]{2,1,0:T(8,128)}), f32[16,8,2304]{2,1,0:T(8,128)S(1)}, u32[]{:S(2)}, u32[]{:S(2)}) async-start(f32[16,8,2304]{2,1,0:T(8,128)} %broadcast_in_dim.4), calls=%async_computation | async-start | bytes 2359296 | tf_op jit(solution)/shard_map/all_to_all | solution.py:188
  10.9 2.5 %copy-done = f32[2304,576]{0,1:T(8,128)S(1)} copy-done((f32[2304,576]{0,1:T(8,128)S(1)}, f32[2304,576]{0,1:T(8,128)}, u32[]{:S(2)}) %copy-start) | copy-done | bytes 5308440
  13.4 1.8 %own_latent.1 = f32[8,576]{1,0:T(8,128)S(1)} custom-call(f32[8,2304]{1,0:T(8,128)S(1)} %copy-done.4, f32[576,2304]{1,0:T(8,128)S(1)} %bitcast.9, f32[1,512]{1,0:T(1,128)S(1)} %bitcast.15), custom_call_target="tpu_custom_call" | custom-call | tf_op jit(solution)/shard_map/own_latent/pallas_call | solution.py:46
  15.2 3.0 %collective-permute-start.4 = (f32[8,576]{1,0:T(8,128)S(1)}, f32[8,576]{1,0:T(8,128)S(1)}, u32[]{:S(2)}, u32[]{:S(2)}) collective-permute-start(f32[8,576]{1,0:T(8,128)S(1)} %own_latent.1), channel_id=1, source_target_pairs={{0,64},{32,96},{64,128},{96,160},{128,192},{160,224},{192,0},{224,... | collective-permute-start | bytes 55304 | tf_op jit(solution)/shard_map/ppermute | solution.py:182
  18.2 4.7 %collective-permute-start.5 = (f32[8,576]{1,0:T(8,128)S(1)}, f32[8,576]{1,0:T(8,128)S(1)}, u32[]{:S(2)}, u32[]{:S(2)}) collective-permute-start(f32[8,576]{1,0:T(8,128)S(1)} %own_latent.1), channel_id=1, source_target_pairs={{0,96},{32,128},{64,160},{96,192},{128,224},{160,0},{192,32},{224,... | collective-permute-start | bytes 55304 | tf_op jit(solution)/shard_map/ppermute | solution.py:182
  23.9 4.0 %collective-permute-start.7 = (f32[8,576]{1,0:T(8,128)S(1)}, f32[8,576]{1,0:T(8,128)S(1)}, u32[]{:S(2)}, u32[]{:S(2)}) collective-permute-start(f32[8,576]{1,0:T(8,128)S(1)} %own_latent.1), channel_id=1, source_target_pairs={{0,160},{32,192},{64,224},{96,0},{128,32},{160,64},{192,96},{224,1... | collective-permute-start | bytes 55304 | tf_op jit(solution)/shard_map/ppermute | solution.py:182
  27.8 2.4 %collective-permute-start.8 = (f32[8,576]{1,0:T(8,128)S(1)}, f32[8,576]{1,0:T(8,128)S(1)}, u32[]{:S(2)}, u32[]{:S(2)}) collective-permute-start(f32[8,576]{1,0:T(8,128)S(1)} %own_latent.1), channel_id=1, source_target_pairs={{0,192},{32,224},{64,0},{96,32},{128,64},{160,96},{192,128},{224,1... | collective-permute-start | bytes 55304 | tf_op jit(solution)/shard_map/ppermute | solution.py:182
  30.2 1.1 %collective-permute-done.8.refs_4_ = f32[8,576]{1,0:T(8,128)S(1)} collective-permute-done((f32[8,576]{1,0:T(8,128)S(1)}, f32[8,576]{1,0:T(8,128)S(1)}, u32[]{:S(2)}, u32[]{:S(2)}) %collective-permute-start.8) | collective-permute-done | bytes 18464 | tf_op jit(solution)/shard_map/ppermute | solution.py:182
  31.3 1.3 %far_copies.1 = f32[16,5,8,576]{3,2,1,0:T(8,128)} custom-call(f32[8,576]{1,0:T(8,128)S(1)} %collective-permute-done.4.refs_0_, f32[8,576]{1,0:T(8,128)S(1)} %collective-permute-done.5.refs_1_, f32[8,576]{1,0:T(8,128)S(1)} %collective-permute-done.6.refs_2_, f32[8,576]{1,0:T(8,128)S(1)} %collective-permute-done.7.refs_3_, ...), custom_call_target="tpu_custom_call" | custom-call | tf_op jit(solution)/shard_map/far_copies/pallas_call | solution.py:46
  32.6 7.0 %all-to-all-start.1 = ((f32[16,5,8,576]{3,2,1,0:T(8,128)}), f32[16,5,8,576]{3,2,1,0:T(8,128)}, u32[]{:S(2)}, u32[]{:S(2)}) async-start(f32[16,5,8,576]{3,2,1,0:T(8,128)} %far_copies.1), calls=%async_computation.1 | async-start | bytes 3276800 | tf_op jit(solution)/shard_map/all_to_all | solution.py:188
  39.6 2.5 %copy-done.1 = f32[2304,576]{0,1:T(8,128)S(1)} copy-done((f32[2304,576]{0,1:T(8,128)S(1)}, f32[2304,576]{0,1:T(8,128)}, u32[]{:S(2)}) %copy-start.1) | copy-done | bytes 5308440
  42.1 2.0 %latent.1.refs_6_ = f32[128,576]{1,0:T(8,128)S(1)} custom-call(f32[128,2304]{1,0:T(8,128)S(1)} %bitcast.11, f32[576,2304]{1,0:T(8,128)S(1)} %bitcast.10, f32[1,512]{1,0:T(1,128)S(1)} %bitcast.16), custom_call_target="tpu_custom_call" | custom-call | tf_op jit(solution)/shard_map/latent/pallas_call | solution.py:46
  45.0 1.9 %collective-permute-start.11 = (f32[128,576]{1,0:T(8,128)S(1)}, f32[128,576]{1,0:T(8,128)}, u32[]{:S(2)}, u32[]{:S(2)}) collective-permute-start(f32[128,576]{1,0:T(8,128)S(1)} %latent.1.refs_6_), channel_id=1, source_target_pairs={{0,224},{32,0},{64,32},{96,64},{128,96},{160,128},{192,160},{224,1... | collective-permute-start | bytes 884744 | tf_op jit(solution)/shard_map/ppermute | solution.py:182
  46.9 3.1 %collective-permute-start.2 = (f32[512,128]{1,0:T(8,128)}, f32[512,128]{1,0:T(8,128)}, u32[]{:S(2)}, u32[]{:S(2)}) collective-permute-start(f32[512,128]{1,0:T(8,128)} %refs_2_.1), channel_id=1, source_target_pairs={{0,1},{1,0},{2,3},{3,2},{4,5},{5,4},{6,7},{7,6},{8,9},{9,8},{10,11... | collective-permute-start | bytes 786440 | tf_op jit(solution)/shard_map/ppermute | solution.py:177
  50.1 2.8 %query.1.refs_0_ = f32[2,128,192]{2,1,0:T(8,128)S(1)} custom-call(f32[128,2304]{1,0:T(8,128)S(1)} %bitcast.12, f32[192,2304]{1,0:T(8,128)S(1)} %bitcast.14, f32[192,2304]{1,0:T(8,128)} %bitcast.6.other_ref), custom_call_target="tpu_custom_call" | custom-call | tf_op jit(solution)/shard_map/query/pallas_call | solution.py:46
  53.6 1.3 %copy-done.3 = f32[128,2304]{1,0:T(8,128)S(1)} copy-done((f32[128,2304]{1,0:T(8,128)S(1)}, f32[128,2304]{1,0:T(8,128)}, u32[]{:S(2)}) %copy-start.3) | copy-done | bytes 1179672
  54.8 1.6 %out_parts.1.out_w_ref = bf16[2,256,2304]{2,1,0:T(8,128)(2,1)S(1)} custom-call(f32[128,2304]{1,0:T(8,128)S(1)} %copy-done.3, f32[128,2304]{1,0:T(8,128)} %collective-permute-done.9.refs_1_), custom_call_target="tpu_custom_call" | custom-call | tf_op jit(solution)/shard_map/out_parts/pallas_call | solution.py:46
  56.5 3.9 %all-to-all-done.1 = f32[16,5,8,576]{3,2,1,0:T(8,128)} async-done(((f32[16,5,8,576]{3,2,1,0:T(8,128)}), f32[16,5,8,576]{3,2,1,0:T(8,128)}, u32[]{:S(2)}, u32[]{:S(2)}) %all-to-all-start.1) | async-done | bytes 1474592 | tf_op jit(solution)/shard_map/all_to_all | solution.py:188
  60.3 6.0 %attend.1 = (f32[2,128,256]{2,1,0:T(8,128)S(1)}, f32[2,128,256]{2,1,0:T(8,128)S(1)}) custom-call(s32[2]{0:T(128)S(1)} %pad_add_fusion.place_ref, f32[2,128,192]{2,1,0:T(8,128)S(1)} %query.1.refs_0_, f32[2,128,192]{2,1,0:T(8,128)S(1)} %collective-permute-done.1.refs_1_, f32[512,128]{1,0:T(8,128)} %refs_2_.1, f32[512,128]{1,0:T(8,128)} %collective-permute-done.2.refs_3_, ...), custom_call_target="tpu_custom_call" | custom-call | tf_op jit(solution)/shard_map/attend/pallas_call | solution.py:46
  66.3 4.6 %collective-permute-start.12 = (f32[2,128,256]{2,1,0:T(8,128)S(1)}, f32[2,128,256]{2,1,0:T(8,128)S(1)}, u32[]{:S(2)}, u32[]{:S(2)}) collective-permute-start(f32[2,128,256]{2,1,0:T(8,128)S(1)} %get-tuple-element.27), channel_id=1, source_target_pairs={{0,1},{1,0},{2,3},{3,2},{4,5},{5,4},{6,7},{7,6},{8,9},{9,8},{10,11... | collective-permute-start | bytes 786440 | tf_op jit(solution)/shard_map/ppermute | solution.py:177
  71.0 1.2 %collective-permute-done.12.arrived_ref = f32[2,128,256]{2,1,0:T(8,128)S(1)} collective-permute-done((f32[2,128,256]{2,1,0:T(8,128)S(1)}, f32[2,128,256]{2,1,0:T(8,128)S(1)}, u32[]{:S(2)}, u32[]{:S(2)}) %collective-permute-start.12) | collective-permute-done | bytes 262176 | tf_op jit(solution)/shard_map/ppermute | solution.py:177
  73.0 20.7 %all_to_all.15 = f32[16,8,2304]{2,1,0:T(8,128)S(1)} all-to-all(f32[16,8,2304]{2,1,0:T(8,128)S(1)} %bitcast.13), channel_id=1, replica_groups={{0,2,4,6,8,10,12,14,16,18,20,22,24,26,28,30},{1,3,5,7,9,11,13,15,17,19,..., dimensions={0} | all-to-all | bytes 2359296 | tf_op jit(solution)/shard_map/all_to_all | solution.py:188
  (29 shorter events, 4.6 us)
Async XLA Ops:
  0.0 10.9 %copy-start.4 = (f32[8,2304]{1,0:T(8,128)S(1)}, f32[8,2304]{1,0:T(8,128)}, u32[]{:S(2)}) copy-start(f32[8,2304]{1,0:T(8,128)} %x_ref.1) | copy-start | bytes 221188
  0.0 10.3 %copy-start.2 = (f32[2304,192]{0,1:T(8,128)S(1)}, f32[2304,192]{0,1:T(8,128)}, u32[]{:S(2)}) copy-start(f32[2304,192]{0,1:T(8,128)} %param.8) | copy-start | bytes 5308420
  0.0 10.9 %copy-start.5 = (f32[512]{0:T(512)S(1)}, f32[512]{0:T(512)}, u32[]{:S(2)}) copy-start(f32[512]{0:T(512)} %param.10) | copy-start | bytes 6148
  0.0 31.3 %collective-permute-start.9 = (f32[128,2304]{1,0:T(8,128)}, f32[128,2304]{1,0:T(8,128)}, u32[]{:S(2)}, u32[]{:S(2)}) collective-permute-start(f32[128,2304]{1,0:T(8,128)} %refs_0_.1), channel_id=1, source_target_pairs={{0,1},{1,0},{2,3},{3,2},{4,5},{5,4},{6,7},{7,6},{8,9},{9,8},{10,11... | collective-permute-start | bytes 3538952 | tf_op jit(solution)/shard_map/ppermute | solution.py:177
  5.2 27.4 %all-to-all-start = ((f32[16,8,2304]{2,1,0:T(8,128)}), f32[16,8,2304]{2,1,0:T(8,128)S(1)}, u32[]{:S(2)}, u32[]{:S(2)}) async-start(f32[16,8,2304]{2,1,0:T(8,128)} %broadcast_in_dim.4), calls=%async_computation | async-start | bytes 2359296 | tf_op jit(solution)/shard_map/all_to_all | solution.py:188
  10.4 39.7 %collective-permute-start = (f32[2304,192]{0,1:T(8,128)S(1)}, f32[2304,192]{0,1:T(8,128)}, u32[]{:S(2)}, u32[]{:S(2)}) collective-permute-start(f32[2304,192]{0,1:T(8,128)S(1)} %copy-done.2), channel_id=1, source_target_pairs={{0,1},{1,0},{2,3},{3,2},{4,5},{5,4},{6,7},{7,6},{8,9},{9,8},{10,11... | collective-permute-start | bytes 5308424 | tf_op jit(solution)/shard_map/ppermute | solution.py:177
  10.9 2.5 %copy-start = (f32[2304,576]{0,1:T(8,128)S(1)}, f32[2304,576]{0,1:T(8,128)}, u32[]{:S(2)}) copy-start(f32[2304,576]{0,1:T(8,128)} %param.9) | copy-start | bytes 15925252
  15.2 8.7 %collective-permute-start.4 = (f32[8,576]{1,0:T(8,128)S(1)}, f32[8,576]{1,0:T(8,128)S(1)}, u32[]{:S(2)}, u32[]{:S(2)}) collective-permute-start(f32[8,576]{1,0:T(8,128)S(1)} %own_latent.1), channel_id=1, source_target_pairs={{0,64},{32,96},{64,128},{96,160},{128,192},{160,224},{192,0},{224,... | collective-permute-start | bytes 55304 | tf_op jit(solution)/shard_map/ppermute | solution.py:182
  18.2 9.6 %collective-permute-start.5 = (f32[8,576]{1,0:T(8,128)S(1)}, f32[8,576]{1,0:T(8,128)S(1)}, u32[]{:S(2)}, u32[]{:S(2)}) collective-permute-start(f32[8,576]{1,0:T(8,128)S(1)} %own_latent.1), channel_id=1, source_target_pairs={{0,96},{32,128},{64,160},{96,192},{128,224},{160,0},{192,32},{224,... | collective-permute-start | bytes 55304 | tf_op jit(solution)/shard_map/ppermute | solution.py:182
  22.9 7.3 %collective-permute-start.6 = (f32[8,576]{1,0:T(8,128)S(1)}, f32[8,576]{1,0:T(8,128)S(1)}, u32[]{:S(2)}, u32[]{:S(2)}) collective-permute-start(f32[8,576]{1,0:T(8,128)S(1)} %own_latent.1), channel_id=1, source_target_pairs={{0,128},{32,160},{64,192},{96,224},{128,0},{160,32},{192,64},{224,... | collective-permute-start | bytes 55304 | tf_op jit(solution)/shard_map/ppermute | solution.py:182
  23.9 6.3 %collective-permute-start.7 = (f32[8,576]{1,0:T(8,128)S(1)}, f32[8,576]{1,0:T(8,128)S(1)}, u32[]{:S(2)}, u32[]{:S(2)}) collective-permute-start(f32[8,576]{1,0:T(8,128)S(1)} %own_latent.1), channel_id=1, source_target_pairs={{0,160},{32,192},{64,224},{96,0},{128,32},{160,64},{192,96},{224,1... | collective-permute-start | bytes 55304 | tf_op jit(solution)/shard_map/ppermute | solution.py:182
  27.8 3.5 %collective-permute-start.8 = (f32[8,576]{1,0:T(8,128)S(1)}, f32[8,576]{1,0:T(8,128)S(1)}, u32[]{:S(2)}, u32[]{:S(2)}) collective-permute-start(f32[8,576]{1,0:T(8,128)S(1)} %own_latent.1), channel_id=1, source_target_pairs={{0,192},{32,224},{64,0},{96,32},{128,64},{160,96},{192,128},{224,1... | collective-permute-start | bytes 55304 | tf_op jit(solution)/shard_map/ppermute | solution.py:182
  32.6 27.7 %all-to-all-start.1 = ((f32[16,5,8,576]{3,2,1,0:T(8,128)}), f32[16,5,8,576]{3,2,1,0:T(8,128)}, u32[]{:S(2)}, u32[]{:S(2)}) async-start(f32[16,5,8,576]{3,2,1,0:T(8,128)} %far_copies.1), calls=%async_computation.1 | async-start | bytes 3276800 | tf_op jit(solution)/shard_map/all_to_all | solution.py:188
  39.6 2.5 %copy-start.1 = (f32[2304,576]{0,1:T(8,128)S(1)}, f32[2304,576]{0,1:T(8,128)}, u32[]{:S(2)}) copy-start(f32[2304,576]{0,1:T(8,128)} %param.9) | copy-start | bytes 15925252
  44.2 12.3 %collective-permute-start.10 = (f32[128,576]{1,0:T(8,128)S(1)}, f32[128,576]{1,0:T(8,128)}, u32[]{:S(2)}, u32[]{:S(2)}) collective-permute-start(f32[128,576]{1,0:T(8,128)S(1)} %latent.1.refs_6_), channel_id=1, source_target_pairs={{0,32},{32,64},{64,96},{96,128},{128,160},{160,192},{192,224},{224... | collective-permute-start | bytes 884744 | tf_op jit(solution)/shard_map/ppermute | solution.py:182
  45.0 11.5 %collective-permute-start.11 = (f32[128,576]{1,0:T(8,128)S(1)}, f32[128,576]{1,0:T(8,128)}, u32[]{:S(2)}, u32[]{:S(2)}) collective-permute-start(f32[128,576]{1,0:T(8,128)S(1)} %latent.1.refs_6_), channel_id=1, source_target_pairs={{0,224},{32,0},{64,32},{96,64},{128,96},{160,128},{192,160},{224,1... | collective-permute-start | bytes 884744 | tf_op jit(solution)/shard_map/ppermute | solution.py:182
  46.9 9.5 %collective-permute-start.2 = (f32[512,128]{1,0:T(8,128)}, f32[512,128]{1,0:T(8,128)}, u32[]{:S(2)}, u32[]{:S(2)}) collective-permute-start(f32[512,128]{1,0:T(8,128)} %refs_2_.1), channel_id=1, source_target_pairs={{0,1},{1,0},{2,3},{3,2},{4,5},{5,4},{6,7},{7,6},{8,9},{9,8},{10,11... | collective-permute-start | bytes 786440 | tf_op jit(solution)/shard_map/ppermute | solution.py:177
  50.1 6.4 %collective-permute-start.3 = (f32[512,128]{1,0:T(8,128)}, f32[512,128]{1,0:T(8,128)}, u32[]{:S(2)}, u32[]{:S(2)}) collective-permute-start(f32[512,128]{1,0:T(8,128)} %refs_4_.1), channel_id=1, source_target_pairs={{0,1},{1,0},{2,3},{3,2},{4,5},{5,4},{6,7},{7,6},{8,9},{9,8},{10,11... | collective-permute-start | bytes 786440 | tf_op jit(solution)/shard_map/ppermute | solution.py:177
  52.9 3.6 %collective-permute-start.1 = (f32[2,128,192]{2,1,0:T(8,128)S(1)}, f32[2,128,192]{2,1,0:T(8,128)S(1)}, u32[]{:S(2)}, u32[]{:S(2)}) collective-permute-start(f32[2,128,192]{2,1,0:T(8,128)S(1)} %query.1.refs_0_), channel_id=1, source_target_pairs={{0,1},{1,0},{2,3},{3,2},{4,5},{5,4},{6,7},{7,6},{8,9},{9,8},{10,11... | collective-permute-start | bytes 589832 | tf_op jit(solution)/shard_map/ppermute | solution.py:177
  53.6 1.3 %copy-start.3 = (f32[128,2304]{1,0:T(8,128)S(1)}, f32[128,2304]{1,0:T(8,128)}, u32[]{:S(2)}) copy-start(f32[128,2304]{1,0:T(8,128)} %refs_0_.1) | copy-start | bytes 3538948
  66.3 5.8 %collective-permute-start.12 = (f32[2,128,256]{2,1,0:T(8,128)S(1)}, f32[2,128,256]{2,1,0:T(8,128)S(1)}, u32[]{:S(2)}, u32[]{:S(2)}) collective-permute-start(f32[2,128,256]{2,1,0:T(8,128)S(1)} %get-tuple-element.27), channel_id=1, source_target_pairs={{0,1},{1,0},{2,3},{3,2},{4,5},{5,4},{6,7},{7,6},{8,9},{9,8},{10,11... | collective-permute-start | bytes 786440 | tf_op jit(solution)/shard_map/ppermute | solution.py:177

commit v5 on v3

--- a/solution.py
+++ b/solution.py
@@ -90,17 +90,26 @@
 def own_kernel(x_ref, down_ref, gain_ref, out_ref):
     rows = x_ref.shape[0]
     x = jnp.concatenate([part.astype(F32) for part in split(x_ref[...], 3)], axis=0).astype(BF16)
-    high, middle, low = (nt(part, x) for part in split(down_ref[...], 3))
-    total = high[:, :rows] + (
+    rank = gain_ref.shape[1]
+    high, low = (nt(part, x) for part in split(down_ref[:rank], 2))
+    raw = high[:, :rows] + (high[:, rows : 2 * rows] + low[:, :rows])
+    high, middle, low = (nt(part, x) for part in split(down_ref[rank:], 3))
+    shared = high[:, :rows] + (
         (high[:, rows : 2 * rows] + middle[:, :rows])
         + (high[:, 2 * rows :] + middle[:, rows : 2 * rows] + low[:, :rows])
     )
-    normed(total.T, gain_ref[...], out_ref)
+    normed(jnp.concatenate([raw, shared], axis=0).T, gain_ref[...], out_ref)
 
 
 def latent_kernel(x_ref, down_ref, gain_ref, out_ref):
-    down = six(split(x_ref[...], 3), split(down_ref[...], 3), nt)
-    normed(down, gain_ref[...], out_ref)
+    rank = gain_ref.shape[1]
+    x = split(x_ref[...], 3)
+    rows = x_ref.shape[0]
+    high, low = split(down_ref[:rank], 2)
+    by_high = nt(jnp.concatenate(x[:2], axis=0), high)
+    raw = by_high[:rows] + (by_high[rows:] + nt(x[0], low))
+    shared = six(x, split(down_ref[rank:], 3), nt)
+    normed(jnp.concatenate([raw, shared], axis=1), gain_ref[...], out_ref)
 
 
 def query_kernel(x_ref, own_ref, other_ref, out_ref):
@@ -232,6 +241,7 @@
     )
     own = call(own_kernel, shape(rows, width), [hidden, w_down.T, gain], "own_latent")
     far = [from_behind(own, step) for step in FAR]
+    far, far_out = lax.optimization_barrier((far, far_out))
     far_copies = call(spread_kernel, shape(places, len(FAR), rows, width), far, "far_copies")
     far_latent = exchange(far_copies).reshape(-1, width)
 

time: 96.2 us -> 94.8 us (0.985)
  local copies, waits for them, and re-layouts: 10.7 us -> 8.27 us
  waiting for transfers between devices: 3.57 us -> 4.86 us
    ppermute x6, starting transfers between devices: 7.99 us -> 12.1 us  [partner(): return lax.ppermute(array, 'head', [(h, h ^ 1) for h in range(size)])]
    all_to_all x2, waiting for transfers between devices: 0.01 us -> 2.52 us  [exchange(): lax.all_to_all(pieces, 'head', split_axis=0, concat_axis=0, tiled=True, a...]
    all_to_all x2, starting transfers between devices: 14.6 us -> 12.1 us  [exchange(): lax.all_to_all(pieces, 'head', split_axis=0, concat_axis=0, tiled=True, a...]
    unnamed x16 -> x12, local copies, waits for them, and re-layouts: 8.58 us -> 6.29 us
    ppermute x7, waiting for transfers between devices: 2.39 us -> 1.17 us  [from_behind(): lax.ppermute(array, 'ctx', [(c, (c + step) % size) for c in range(size)])]
  transfers between devices with their start and end apart: 15 -> 15, of which waited for: 3 -> 3; matrix products, arithmetic and copies ran while one was open for 0% -> 2% of each run, Pallas kernels for 12% -> 12%
where the time goes in v5:
time: 94.8 us; the launch traced here: 94.4 us
  starting transfers between devices  42 us (44%)
  blocking collectives  20.7 us (22%)
  Pallas kernels  17.7 us (19%)
  local copies, waits for them, and re-layouts  8.27 us (9%)
  waiting for transfers between devices  4.86 us (5%)
    all_to_all x1, blocking collectives, exchange(): lax.all_to_all(pieces, 'head', split_axis=0, concat_axis=0, tiled=True, a...  20.7 us
    ppermute x7, starting transfers between devices, from_behind(): lax.ppermute(array, 'ctx', [(c, (c + step) % size) for c in range(size)])  17.8 us
    pallas_call x7, Pallas kernels, call(): pl.pallas_call(kernel, out_shape=outs, in_specs=[pl.BlockSpec(memory_spac...  17.7 us
    ppermute x6, starting transfers between devices, partner(): return lax.ppermute(array, 'head', [(h, h ^ 1) for h in range(size)])  12.1 us
    all_to_all x2, starting transfers between devices, exchange(): lax.all_to_all(pieces, 'head', split_axis=0, concat_axis=0, tiled=True, a...  12.1 us
    unnamed x12, local copies, waits for them, and re-layouts  6.29 us
    all_to_all x2, waiting for transfers between devices, exchange(): lax.all_to_all(pieces, 'head', split_axis=0, concat_axis=0, tiled=True, a...  2.52 us
    broadcast_in_dim x1, local copies, waits for them, and re-layouts, spread(): return exchange(jnp.broadcast_to(array[None], (places, *array.shape)))  1.98 us
  transfers between devices with their start and end apart: 15, of which 3 were waited for; matrix products, arithmetic and copies ran while one was open for 2% of the time, Pallas kernels for 12%

profile of v5, /device:TPU:1, one launch (start us, length us, event | category | flops | bytes accessed | tf_op | source)
XLA Modules:
  0.0 94.4 jit_solution(8724036572482065042)
XLA Ops:
  0.0 3.2 %collective-permute-start.9 = (f32[128,2304]{1,0:T(8,128)}, f32[128,2304]{1,0:T(8,128)}, u32[]{:S(2)}, u32[]{:S(2)}) collective-permute-start(f32[128,2304]{1,0:T(8,128)} %refs_0_.1), channel_id=1, source_target_pairs={{0,1},{1,0},{2,3},{3,2},{4,5},{5,4},{6,7},{7,6},{8,9},{9,8},{10,11... | collective-permute-start | bytes 3538952 | tf_op jit(solution)/shard_map/ppermute | solution.py:201
  3.2 2.0 %broadcast_in_dim.4 = f32[16,8,2304]{2,1,0:T(8,128)} broadcast(f32[8,2304]{1,0:T(8,128)} %x_ref.1), dimensions={1,2} | broadcast | bytes 1253376 | tf_op jit(solution)/shard_map/broadcast_in_dim | solution.py:225
  5.2 5.1 %all-to-all-start = ((f32[16,8,2304]{2,1,0:T(8,128)}), f32[16,8,2304]{2,1,0:T(8,128)S(1)}, u32[]{:S(2)}, u32[]{:S(2)}) async-start(f32[16,8,2304]{2,1,0:T(8,128)} %broadcast_in_dim.4), calls=%async_computation | async-start | bytes 2359296 | tf_op jit(solution)/shard_map/all_to_all | solution.py:212
  10.9 2.5 %copy-done = f32[2304,576]{0,1:T(8,128)S(1)} copy-done((f32[2304,576]{0,1:T(8,128)S(1)}, f32[2304,576]{0,1:T(8,128)}, u32[]{:S(2)}) %copy-start) | copy-done | bytes 5308440
  13.4 1.8 %own_latent.1 = f32[8,576]{1,0:T(8,128)S(1)} custom-call(f32[8,2304]{1,0:T(8,128)S(1)} %copy-done.4, f32[576,2304]{1,0:T(8,128)S(1)} %bitcast.9, f32[1,512]{1,0:T(1,128)S(1)} %bitcast.15), custom_call_target="tpu_custom_call" | custom-call | tf_op jit(solution)/shard_map/own_latent/pallas_call | solution.py:57
  15.2 3.1 %collective-permute-start.4 = (f32[8,576]{1,0:T(8,128)S(1)}, f32[8,576]{1,0:T(8,128)S(1)}, u32[]{:S(2)}, u32[]{:S(2)}) collective-permute-start(f32[8,576]{1,0:T(8,128)S(1)} %own_latent.1), channel_id=1, source_target_pairs={{0,64},{32,96},{64,128},{96,160},{128,192},{160,224},{192,0},{224,... | collective-permute-start | bytes 55304 | tf_op jit(solution)/shard_map/ppermute | solution.py:206
  18.3 4.7 %collective-permute-start.5 = (f32[8,576]{1,0:T(8,128)S(1)}, f32[8,576]{1,0:T(8,128)S(1)}, u32[]{:S(2)}, u32[]{:S(2)}) collective-permute-start(f32[8,576]{1,0:T(8,128)S(1)} %own_latent.1), channel_id=1, source_target_pairs={{0,96},{32,128},{64,160},{96,192},{128,224},{160,0},{192,32},{224,... | collective-permute-start | bytes 55304 | tf_op jit(solution)/shard_map/ppermute | solution.py:206
  23.9 3.9 %collective-permute-start.7 = (f32[8,576]{1,0:T(8,128)S(1)}, f32[8,576]{1,0:T(8,128)S(1)}, u32[]{:S(2)}, u32[]{:S(2)}) collective-permute-start(f32[8,576]{1,0:T(8,128)S(1)} %own_latent.1), channel_id=1, source_target_pairs={{0,160},{32,192},{64,224},{96,0},{128,32},{160,64},{192,96},{224,1... | collective-permute-start | bytes 55304 | tf_op jit(solution)/shard_map/ppermute | solution.py:206
  27.9 2.4 %collective-permute-start.8 = (f32[8,576]{1,0:T(8,128)S(1)}, f32[8,576]{1,0:T(8,128)S(1)}, u32[]{:S(2)}, u32[]{:S(2)}) collective-permute-start(f32[8,576]{1,0:T(8,128)S(1)} %own_latent.1), channel_id=1, source_target_pairs={{0,192},{32,224},{64,0},{96,32},{128,64},{160,96},{192,128},{224,1... | collective-permute-start | bytes 55304 | tf_op jit(solution)/shard_map/ppermute | solution.py:206
  30.3 1.2 %collective-permute-done.8.refs_4_ = f32[8,576]{1,0:T(8,128)S(1)} collective-permute-done((f32[8,576]{1,0:T(8,128)S(1)}, f32[8,576]{1,0:T(8,128)S(1)}, u32[]{:S(2)}, u32[]{:S(2)}) %collective-permute-start.8) | collective-permute-done | bytes 18464 | tf_op jit(solution)/shard_map/ppermute | solution.py:206
  31.4 1.3 %far_copies.1 = f32[16,5,8,576]{3,2,1,0:T(8,128)} custom-call(f32[8,576]{1,0:T(8,128)S(1)} %collective-permute-done.4.refs_0_, f32[8,576]{1,0:T(8,128)S(1)} %collective-permute-done.5.refs_1_, f32[8,576]{1,0:T(8,128)S(1)} %collective-permute-done.6.refs_2_, f32[8,576]{1,0:T(8,128)S(1)} %collective-permute-done.7.refs_3_, ...), custom_call_target="tpu_custom_call" | custom-call | tf_op jit(solution)/shard_map/far_copies/pallas_call | solution.py:57
  32.7 7.0 %all-to-all-start.1 = ((f32[16,5,8,576]{3,2,1,0:T(8,128)}), f32[16,5,8,576]{3,2,1,0:T(8,128)}, u32[]{:S(2)}, u32[]{:S(2)}) async-start(f32[16,5,8,576]{3,2,1,0:T(8,128)} %far_copies.1), calls=%async_computation.1 | async-start | bytes 3276800 | tf_op jit(solution)/shard_map/all_to_all | solution.py:212
  39.7 2.5 %copy-done.1 = f32[2304,576]{0,1:T(8,128)S(1)} copy-done((f32[2304,576]{0,1:T(8,128)S(1)}, f32[2304,576]{0,1:T(8,128)}, u32[]{:S(2)}) %copy-start.1) | copy-done | bytes 5308440
  42.2 2.5 %latent.1.refs_6_ = f32[128,576]{1,0:T(8,128)S(1)} custom-call(f32[128,2304]{1,0:T(8,128)S(1)} %bitcast.11, f32[576,2304]{1,0:T(8,128)S(1)} %bitcast.10, f32[1,512]{1,0:T(1,128)S(1)} %bitcast.16), custom_call_target="tpu_custom_call" | custom-call | tf_op jit(solution)/shard_map/latent/pallas_call | solution.py:57
  45.5 1.9 %collective-permute-start.11 = (f32[128,576]{1,0:T(8,128)S(1)}, f32[128,576]{1,0:T(8,128)}, u32[]{:S(2)}, u32[]{:S(2)}) collective-permute-start(f32[128,576]{1,0:T(8,128)S(1)} %latent.1.refs_6_), channel_id=1, source_target_pairs={{0,224},{32,0},{64,32},{96,64},{128,96},{160,128},{192,160},{224,1... | collective-permute-start | bytes 884744 | tf_op jit(solution)/shard_map/ppermute | solution.py:206
  47.4 3.1 %collective-permute-start.2 = (f32[512,128]{1,0:T(8,128)}, f32[512,128]{1,0:T(8,128)}, u32[]{:S(2)}, u32[]{:S(2)}) collective-permute-start(f32[512,128]{1,0:T(8,128)} %refs_2_.1), channel_id=1, source_target_pairs={{0,1},{1,0},{2,3},{3,2},{4,5},{5,4},{6,7},{7,6},{8,9},{9,8},{10,11... | collective-permute-start | bytes 786440 | tf_op jit(solution)/shard_map/ppermute | solution.py:201
  50.6 3.7 %query.1.refs_0_ = f32[2,128,192]{2,1,0:T(8,128)S(1)} custom-call(f32[128,2304]{1,0:T(8,128)S(1)} %bitcast.12, f32[192,2304]{1,0:T(8,128)S(1)} %bitcast.14, f32[192,2304]{1,0:T(8,128)} %bitcast.6.other_ref), custom_call_target="tpu_custom_call" | custom-call | tf_op jit(solution)/shard_map/query/pallas_call | solution.py:57
  55.0 1.3 %copy-done.3 = f32[128,2304]{1,0:T(8,128)S(1)} copy-done((f32[128,2304]{1,0:T(8,128)S(1)}, f32[128,2304]{1,0:T(8,128)}, u32[]{:S(2)}) %copy-start.3) | copy-done | bytes 1179672
  56.3 1.6 %out_parts.1.out_w_ref = bf16[2,256,2304]{2,1,0:T(8,128)(2,1)S(1)} custom-call(f32[128,2304]{1,0:T(8,128)S(1)} %copy-done.3, f32[128,2304]{1,0:T(8,128)} %collective-permute-done.9.refs_1_), custom_call_target="tpu_custom_call" | custom-call | tf_op jit(solution)/shard_map/out_parts/pallas_call | solution.py:57
  57.9 2.5 %all-to-all-done.1 = f32[16,5,8,576]{3,2,1,0:T(8,128)} async-done(((f32[16,5,8,576]{3,2,1,0:T(8,128)}), f32[16,5,8,576]{3,2,1,0:T(8,128)}, u32[]{:S(2)}, u32[]{:S(2)}) %all-to-all-start.1) | async-done | bytes 1474592 | tf_op jit(solution)/shard_map/all_to_all | solution.py:212
  60.4 5.9 %attend.1 = (f32[2,128,256]{2,1,0:T(8,128)S(1)}, f32[2,128,256]{2,1,0:T(8,128)S(1)}) custom-call(s32[2]{0:T(128)S(1)} %pad_add_fusion.place_ref, f32[2,128,192]{2,1,0:T(8,128)S(1)} %query.1.refs_0_, f32[2,128,192]{2,1,0:T(8,128)S(1)} %collective-permute-done.1.refs_1_, f32[512,128]{1,0:T(8,128)} %refs_2_.1, f32[512,128]{1,0:T(8,128)} %collective-permute-done.2.refs_3_, ...), custom_call_target="tpu_custom_call" | custom-call | tf_op jit(solution)/shard_map/attend/pallas_call | solution.py:57
  66.4 4.6 %collective-permute-start.12 = (f32[2,128,256]{2,1,0:T(8,128)S(1)}, f32[2,128,256]{2,1,0:T(8,128)S(1)}, u32[]{:S(2)}, u32[]{:S(2)}) collective-permute-start(f32[2,128,256]{2,1,0:T(8,128)S(1)} %get-tuple-element.27), channel_id=1, source_target_pairs={{0,1},{1,0},{2,3},{3,2},{4,5},{5,4},{6,7},{7,6},{8,9},{9,8},{10,11... | collective-permute-start | bytes 786440 | tf_op jit(solution)/shard_map/ppermute | solution.py:201
  71.0 1.2 %collective-permute-done.12.arrived_ref = f32[2,128,256]{2,1,0:T(8,128)S(1)} collective-permute-done((f32[2,128,256]{2,1,0:T(8,128)S(1)}, f32[2,128,256]{2,1,0:T(8,128)S(1)}, u32[]{:S(2)}, u32[]{:S(2)}) %collective-permute-start.12) | collective-permute-done | bytes 262176 | tf_op jit(solution)/shard_map/ppermute | solution.py:201
  73.0 20.7 %all_to_all.15 = f32[16,8,2304]{2,1,0:T(8,128)S(1)} all-to-all(f32[16,8,2304]{2,1,0:T(8,128)S(1)} %bitcast.13), channel_id=1, replica_groups={{0,2,4,6,8,10,12,14,16,18,20,22,24,26,28,30},{1,3,5,7,9,11,13,15,17,19,..., dimensions={0} | all-to-all | bytes 2359296 | tf_op jit(solution)/shard_map/all_to_all | solution.py:212
  (29 shorter events, 4.6 us)
Async XLA Ops:
  0.0 10.9 %copy-start.4 = (f32[8,2304]{1,0:T(8,128)S(1)}, f32[8,2304]{1,0:T(8,128)}, u32[]{:S(2)}) copy-start(f32[8,2304]{1,0:T(8,128)} %x_ref.1) | copy-start | bytes 221188
  0.0 10.3 %copy-start.2 = (f32[2304,192]{0,1:T(8,128)S(1)}, f32[2304,192]{0,1:T(8,128)}, u32[]{:S(2)}) copy-start(f32[2304,192]{0,1:T(8,128)} %param.8) | copy-start | bytes 5308420
  0.0 10.9 %copy-start.5 = (f32[512]{0:T(512)S(1)}, f32[512]{0:T(512)}, u32[]{:S(2)}) copy-start(f32[512]{0:T(512)} %param.10) | copy-start | bytes 6148
  0.0 31.4 %collective-permute-start.9 = (f32[128,2304]{1,0:T(8,128)}, f32[128,2304]{1,0:T(8,128)}, u32[]{:S(2)}, u32[]{:S(2)}) collective-permute-start(f32[128,2304]{1,0:T(8,128)} %refs_0_.1), channel_id=1, source_target_pairs={{0,1},{1,0},{2,3},{3,2},{4,5},{5,4},{6,7},{7,6},{8,9},{9,8},{10,11... | collective-permute-start | bytes 3538952 | tf_op jit(solution)/shard_map/ppermute | solution.py:201
  5.2 27.5 %all-to-all-start = ((f32[16,8,2304]{2,1,0:T(8,128)}), f32[16,8,2304]{2,1,0:T(8,128)S(1)}, u32[]{:S(2)}, u32[]{:S(2)}) async-start(f32[16,8,2304]{2,1,0:T(8,128)} %broadcast_in_dim.4), calls=%async_computation | async-start | bytes 2359296 | tf_op jit(solution)/shard_map/all_to_all | solution.py:212
  10.4 40.2 %collective-permute-start = (f32[2304,192]{0,1:T(8,128)S(1)}, f32[2304,192]{0,1:T(8,128)}, u32[]{:S(2)}, u32[]{:S(2)}) collective-permute-start(f32[2304,192]{0,1:T(8,128)S(1)} %copy-done.2), channel_id=1, source_target_pairs={{0,1},{1,0},{2,3},{3,2},{4,5},{5,4},{6,7},{7,6},{8,9},{9,8},{10,11... | collective-permute-start | bytes 5308424 | tf_op jit(solution)/shard_map/ppermute | solution.py:201
  10.9 2.5 %copy-start = (f32[2304,576]{0,1:T(8,128)S(1)}, f32[2304,576]{0,1:T(8,128)}, u32[]{:S(2)}) copy-start(f32[2304,576]{0,1:T(8,128)} %param.9) | copy-start | bytes 15925252
  15.2 8.7 %collective-permute-start.4 = (f32[8,576]{1,0:T(8,128)S(1)}, f32[8,576]{1,0:T(8,128)S(1)}, u32[]{:S(2)}, u32[]{:S(2)}) collective-permute-start(f32[8,576]{1,0:T(8,128)S(1)} %own_latent.1), channel_id=1, source_target_pairs={{0,64},{32,96},{64,128},{96,160},{128,192},{160,224},{192,0},{224,... | collective-permute-start | bytes 55304 | tf_op jit(solution)/shard_map/ppermute | solution.py:206
  18.3 9.6 %collective-permute-start.5 = (f32[8,576]{1,0:T(8,128)S(1)}, f32[8,576]{1,0:T(8,128)S(1)}, u32[]{:S(2)}, u32[]{:S(2)}) collective-permute-start(f32[8,576]{1,0:T(8,128)S(1)} %own_latent.1), channel_id=1, source_target_pairs={{0,96},{32,128},{64,160},{96,192},{128,224},{160,0},{192,32},{224,... | collective-permute-start | bytes 55304 | tf_op jit(solution)/shard_map/ppermute | solution.py:206
  22.9 7.3 %collective-permute-start.6 = (f32[8,576]{1,0:T(8,128)S(1)}, f32[8,576]{1,0:T(8,128)S(1)}, u32[]{:S(2)}, u32[]{:S(2)}) collective-permute-start(f32[8,576]{1,0:T(8,128)S(1)} %own_latent.1), channel_id=1, source_target_pairs={{0,128},{32,160},{64,192},{96,224},{128,0},{160,32},{192,64},{224,... | collective-permute-start | bytes 55304 | tf_op jit(solution)/shard_map/ppermute | solution.py:206
  23.9 6.3 %collective-permute-start.7 = (f32[8,576]{1,0:T(8,128)S(1)}, f32[8,576]{1,0:T(8,128)S(1)}, u32[]{:S(2)}, u32[]{:S(2)}) collective-permute-start(f32[8,576]{1,0:T(8,128)S(1)} %own_latent.1), channel_id=1, source_target_pairs={{0,160},{32,192},{64,224},{96,0},{128,32},{160,64},{192,96},{224,1... | collective-permute-start | bytes 55304 | tf_op jit(solution)/shard_map/ppermute | solution.py:206
  27.9 3.6 %collective-permute-start.8 = (f32[8,576]{1,0:T(8,128)S(1)}, f32[8,576]{1,0:T(8,128)S(1)}, u32[]{:S(2)}, u32[]{:S(2)}) collective-permute-start(f32[8,576]{1,0:T(8,128)S(1)} %own_latent.1), channel_id=1, source_target_pairs={{0,192},{32,224},{64,0},{96,32},{128,64},{160,96},{192,128},{224,1... | collective-permute-start | bytes 55304 | tf_op jit(solution)/shard_map/ppermute | solution.py:206
  32.7 27.7 %all-to-all-start.1 = ((f32[16,5,8,576]{3,2,1,0:T(8,128)}), f32[16,5,8,576]{3,2,1,0:T(8,128)}, u32[]{:S(2)}, u32[]{:S(2)}) async-start(f32[16,5,8,576]{3,2,1,0:T(8,128)} %far_copies.1), calls=%async_computation.1 | async-start | bytes 3276800 | tf_op jit(solution)/shard_map/all_to_all | solution.py:212
  39.7 2.5 %copy-start.1 = (f32[2304,576]{0,1:T(8,128)S(1)}, f32[2304,576]{0,1:T(8,128)}, u32[]{:S(2)}) copy-start(f32[2304,576]{0,1:T(8,128)} %param.9) | copy-start | bytes 15925252
  44.7 13.2 %collective-permute-start.10 = (f32[128,576]{1,0:T(8,128)S(1)}, f32[128,576]{1,0:T(8,128)}, u32[]{:S(2)}, u32[]{:S(2)}) collective-permute-start(f32[128,576]{1,0:T(8,128)S(1)} %latent.1.refs_6_), channel_id=1, source_target_pairs={{0,32},{32,64},{64,96},{96,128},{128,160},{160,192},{192,224},{224... | collective-permute-start | bytes 884744 | tf_op jit(solution)/shard_map/ppermute | solution.py:206
  45.5 12.4 %collective-permute-start.11 = (f32[128,576]{1,0:T(8,128)S(1)}, f32[128,576]{1,0:T(8,128)}, u32[]{:S(2)}, u32[]{:S(2)}) collective-permute-start(f32[128,576]{1,0:T(8,128)S(1)} %latent.1.refs_6_), channel_id=1, source_target_pairs={{0,224},{32,0},{64,32},{96,64},{128,96},{160,128},{192,160},{224,1... | collective-permute-start | bytes 884744 | tf_op jit(solution)/shard_map/ppermute | solution.py:206
  47.4 10.4 %collective-permute-start.2 = (f32[512,128]{1,0:T(8,128)}, f32[512,128]{1,0:T(8,128)}, u32[]{:S(2)}, u32[]{:S(2)}) collective-permute-start(f32[512,128]{1,0:T(8,128)} %refs_2_.1), channel_id=1, source_target_pairs={{0,1},{1,0},{2,3},{3,2},{4,5},{5,4},{6,7},{7,6},{8,9},{9,8},{10,11... | collective-permute-start | bytes 786440 | tf_op jit(solution)/shard_map/ppermute | solution.py:201
  50.5 7.3 %collective-permute-start.3 = (f32[512,128]{1,0:T(8,128)}, f32[512,128]{1,0:T(8,128)}, u32[]{:S(2)}, u32[]{:S(2)}) collective-permute-start(f32[512,128]{1,0:T(8,128)} %refs_4_.1), channel_id=1, source_target_pairs={{0,1},{1,0},{2,3},{3,2},{4,5},{5,4},{6,7},{7,6},{8,9},{9,8},{10,11... | collective-permute-start | bytes 786440 | tf_op jit(solution)/shard_map/ppermute | solution.py:201
  54.3 3.6 %collective-permute-start.1 = (f32[2,128,192]{2,1,0:T(8,128)S(1)}, f32[2,128,192]{2,1,0:T(8,128)S(1)}, u32[]{:S(2)}, u32[]{:S(2)}) collective-permute-start(f32[2,128,192]{2,1,0:T(8,128)S(1)} %query.1.refs_0_), channel_id=1, source_target_pairs={{0,1},{1,0},{2,3},{3,2},{4,5},{5,4},{6,7},{7,6},{8,9},{9,8},{10,11... | collective-permute-start | bytes 589832 | tf_op jit(solution)/shard_map/ppermute | solution.py:201
  55.0 1.3 %copy-start.3 = (f32[128,2304]{1,0:T(8,128)S(1)}, f32[128,2304]{1,0:T(8,128)}, u32[]{:S(2)}) copy-start(f32[128,2304]{1,0:T(8,128)} %refs_0_.1) | copy-start | bytes 3538948
  66.4 5.8 %collective-permute-start.12 = (f32[2,128,256]{2,1,0:T(8,128)S(1)}, f32[2,128,256]{2,1,0:T(8,128)S(1)}, u32[]{:S(2)}, u32[]{:S(2)}) collective-permute-start(f32[2,128,256]{2,1,0:T(8,128)S(1)} %get-tuple-element.27), channel_id=1, source_target_pairs={{0,1},{1,0},{2,3},{3,2},{4,5},{5,4},{6,7},{7,6},{8,9},{9,8},{10,11... | collective-permute-start | bytes 786440 | tf_op jit(solution)/shard_map/ppermute | solution.py:201

commit v6 on v5

--- a/solution.py
+++ b/solution.py
@@ -221,10 +221,6 @@
             out_ref[copy, number] = ref[...]
 
 
-def spread(array, places):
-    return exchange(jnp.broadcast_to(array[None], (places, *array.shape)))
-
-
 def on_device(hidden, w_query, w_down, latent_gain, w_key_up, w_value_up, w_out):
     rows, depth = hidden.shape
     blocks = lax.axis_size("ctx")
@@ -235,7 +231,8 @@
     place = jnp.stack([lax.axis_index("ctx"), lax.axis_index("head") & 1]).astype(jnp.int32)
     gain = latent_gain[None]
 
-    mine = spread(hidden, places).reshape(half, depth)
+    copies = call(spread_kernel, shape(places, 1, rows, depth), [hidden], "copies")
+    mine = exchange(copies).reshape(half, depth)
     far_query, far_key, far_value, far_out = (
         partner(weight) for weight in (w_query, w_key_up, w_value_up, w_out)
     )

time: 94.8 us -> 94.8 us (level)
  Pallas kernels: 17.7 us -> 18.9 us
  local copies, waits for them, and re-layouts: 8.27 us -> 7.17 us
    broadcast_in_dim x1 -> x0, local copies, waits for them, and re-layouts: 1.98 us -> none  [spread(): return exchange(jnp.broadcast_to(array[None], (places, *array.shape)))]
    pallas_call x7 -> x8, Pallas kernels: 17.7 us -> 18.9 us  [call(): pl.pallas_call(kernel, out_shape=outs, in_specs=[pl.BlockSpec(memory_spac...]
    unnamed x12 -> x14, local copies, waits for them, and re-layouts: 6.29 us -> 7.17 us
  transfers between devices with their start and end apart: 15 -> 15, of which waited for: 3 -> 3; matrix products, arithmetic and copies ran while one was open for 2% -> 0% of each run, Pallas kernels for 12% -> 13%
where the time goes in v6:
time: 94.8 us; the launch traced here: 94.3 us
  starting transfers between devices  41.9 us (44%)
  blocking collectives  20.7 us (22%)
  Pallas kernels  18.9 us (20%)
  local copies, waits for them, and re-layouts  7.17 us (8%)
  waiting for transfers between devices  4.85 us (5%)
    all_to_all x1, blocking collectives, exchange(): lax.all_to_all(pieces, 'head', split_axis=0, concat_axis=0, tiled=True, a...  20.7 us
    pallas_call x8, Pallas kernels, call(): pl.pallas_call(kernel, out_shape=outs, in_specs=[pl.BlockSpec(memory_spac...  18.9 us
    ppermute x7, starting transfers between devices, from_behind(): lax.ppermute(array, 'ctx', [(c, (c + step) % size) for c in range(size)])  17.8 us
    ppermute x6, starting transfers between devices, partner(): return lax.ppermute(array, 'head', [(h, h ^ 1) for h in range(size)])  12.1 us
    all_to_all x2, starting transfers between devices, exchange(): lax.all_to_all(pieces, 'head', split_axis=0, concat_axis=0, tiled=True, a...  12 us
    unnamed x14, local copies, waits for them, and re-layouts  7.17 us
    all_to_all x2, waiting for transfers between devices, exchange(): lax.all_to_all(pieces, 'head', split_axis=0, concat_axis=0, tiled=True, a...  2.5 us
  transfers between devices with their start and end apart: 15, of which 3 were waited for; matrix products, arithmetic and copies ran while one was open for 0% of the time, Pallas kernels for 13%

profile of v6, /device:TPU:1, one launch (start us, length us, event | category | flops | bytes accessed | tf_op | source)
XLA Modules:
  0.0 94.3 jit_solution(5369636502664706295)
XLA Ops:
  0.0 3.2 %collective-permute-start.9 = (f32[128,2304]{1,0:T(8,128)}, f32[128,2304]{1,0:T(8,128)}, u32[]{:S(2)}, u32[]{:S(2)}) collective-permute-start(f32[128,2304]{1,0:T(8,128)} %refs_0_.3), channel_id=1, source_target_pairs={{0,1},{1,0},{2,3},{3,2},{4,5},{5,4},{6,7},{7,6},{8,9},{9,8},{10,11... | collective-permute-start | bytes 3538952 | tf_op jit(solution)/shard_map/ppermute | solution.py:201
  4.1 1.1 %copies.1 = f32[16,1,8,2304]{3,2,1,0:T(8,128)} custom-call(f32[8,2304]{1,0:T(8,128)S(1)} %copy-done.4), custom_call_target="tpu_custom_call" | custom-call | tf_op jit(solution)/shard_map/copies/pallas_call | solution.py:57
  5.2 5.0 %all-to-all-start = ((f32[16,1,8,2304]{3,2,1,0:T(8,128)}), f32[16,1,8,2304]{3,2,1,0:T(8,128)S(1)}, u32[]{:S(2)}, u32[]{:S(2)}) async-start(f32[16,1,8,2304]{3,2,1,0:T(8,128)} %copies.1), calls=%async_computation | async-start | bytes 2359296 | tf_op jit(solution)/shard_map/all_to_all | solution.py:212
  10.8 2.5 %copy-done = f32[2304,576]{0,1:T(8,128)S(1)} copy-done((f32[2304,576]{0,1:T(8,128)S(1)}, f32[2304,576]{0,1:T(8,128)}, u32[]{:S(2)}) %copy-start) | copy-done | bytes 5308440
  13.3 1.9 %own_latent.1 = f32[8,576]{1,0:T(8,128)S(1)} custom-call(f32[8,2304]{1,0:T(8,128)S(1)} %copy-done.5, f32[576,2304]{1,0:T(8,128)S(1)} %bitcast.9, f32[1,512]{1,0:T(1,128)S(1)} %bitcast.15), custom_call_target="tpu_custom_call" | custom-call | tf_op jit(solution)/shard_map/own_latent/pallas_call | solution.py:57
  15.2 3.1 %collective-permute-start.4 = (f32[8,576]{1,0:T(8,128)S(1)}, f32[8,576]{1,0:T(8,128)S(1)}, u32[]{:S(2)}, u32[]{:S(2)}) collective-permute-start(f32[8,576]{1,0:T(8,128)S(1)} %own_latent.1), channel_id=1, source_target_pairs={{0,64},{32,96},{64,128},{96,160},{128,192},{160,224},{192,0},{224,... | collective-permute-start | bytes 55304 | tf_op jit(solution)/shard_map/ppermute | solution.py:206
  18.2 4.6 %collective-permute-start.5 = (f32[8,576]{1,0:T(8,128)S(1)}, f32[8,576]{1,0:T(8,128)S(1)}, u32[]{:S(2)}, u32[]{:S(2)}) collective-permute-start(f32[8,576]{1,0:T(8,128)S(1)} %own_latent.1), channel_id=1, source_target_pairs={{0,96},{32,128},{64,160},{96,192},{128,224},{160,0},{192,32},{224,... | collective-permute-start | bytes 55304 | tf_op jit(solution)/shard_map/ppermute | solution.py:206
  23.9 3.9 %collective-permute-start.7 = (f32[8,576]{1,0:T(8,128)S(1)}, f32[8,576]{1,0:T(8,128)S(1)}, u32[]{:S(2)}, u32[]{:S(2)}) collective-permute-start(f32[8,576]{1,0:T(8,128)S(1)} %own_latent.1), channel_id=1, source_target_pairs={{0,160},{32,192},{64,224},{96,0},{128,32},{160,64},{192,96},{224,1... | collective-permute-start | bytes 55304 | tf_op jit(solution)/shard_map/ppermute | solution.py:206
  27.8 2.4 %collective-permute-start.8 = (f32[8,576]{1,0:T(8,128)S(1)}, f32[8,576]{1,0:T(8,128)S(1)}, u32[]{:S(2)}, u32[]{:S(2)}) collective-permute-start(f32[8,576]{1,0:T(8,128)S(1)} %own_latent.1), channel_id=1, source_target_pairs={{0,192},{32,224},{64,0},{96,32},{128,64},{160,96},{192,128},{224,1... | collective-permute-start | bytes 55304 | tf_op jit(solution)/shard_map/ppermute | solution.py:206
  30.2 1.2 %collective-permute-done.8.refs_4_ = f32[8,576]{1,0:T(8,128)S(1)} collective-permute-done((f32[8,576]{1,0:T(8,128)S(1)}, f32[8,576]{1,0:T(8,128)S(1)}, u32[]{:S(2)}, u32[]{:S(2)}) %collective-permute-start.8) | collective-permute-done | bytes 18464 | tf_op jit(solution)/shard_map/ppermute | solution.py:206
  31.4 1.3 %far_copies.1 = f32[16,5,8,576]{3,2,1,0:T(8,128)} custom-call(f32[8,576]{1,0:T(8,128)S(1)} %collective-permute-done.4.refs_0_, f32[8,576]{1,0:T(8,128)S(1)} %collective-permute-done.5.refs_1_, f32[8,576]{1,0:T(8,128)S(1)} %collective-permute-done.6.refs_2_, f32[8,576]{1,0:T(8,128)S(1)} %collective-permute-done.7.refs_3_, ...), custom_call_target="tpu_custom_call" | custom-call | tf_op jit(solution)/shard_map/far_copies/pallas_call | solution.py:57
  32.7 6.9 %all-to-all-start.1 = ((f32[16,5,8,576]{3,2,1,0:T(8,128)}), f32[16,5,8,576]{3,2,1,0:T(8,128)}, u32[]{:S(2)}, u32[]{:S(2)}) async-start(f32[16,5,8,576]{3,2,1,0:T(8,128)} %far_copies.1), calls=%async_computation.1 | async-start | bytes 3276800 | tf_op jit(solution)/shard_map/all_to_all | solution.py:212
  39.6 2.5 %copy-done.1 = f32[2304,576]{0,1:T(8,128)S(1)} copy-done((f32[2304,576]{0,1:T(8,128)S(1)}, f32[2304,576]{0,1:T(8,128)}, u32[]{:S(2)}) %copy-start.1) | copy-done | bytes 5308440
  42.1 2.5 %latent.1.refs_6_ = f32[128,576]{1,0:T(8,128)S(1)} custom-call(f32[128,2304]{1,0:T(8,128)S(1)} %bitcast.11, f32[576,2304]{1,0:T(8,128)S(1)} %bitcast.10, f32[1,512]{1,0:T(1,128)S(1)} %bitcast.16), custom_call_target="tpu_custom_call" | custom-call | tf_op jit(solution)/shard_map/latent/pallas_call | solution.py:57
  45.4 1.9 %collective-permute-start.11 = (f32[128,576]{1,0:T(8,128)S(1)}, f32[128,576]{1,0:T(8,128)}, u32[]{:S(2)}, u32[]{:S(2)}) collective-permute-start(f32[128,576]{1,0:T(8,128)S(1)} %latent.1.refs_6_), channel_id=1, source_target_pairs={{0,224},{32,0},{64,32},{96,64},{128,96},{160,128},{192,160},{224,1... | collective-permute-start | bytes 884744 | tf_op jit(solution)/shard_map/ppermute | solution.py:206
  47.4 3.1 %collective-permute-start.2 = (f32[512,128]{1,0:T(8,128)}, f32[512,128]{1,0:T(8,128)}, u32[]{:S(2)}, u32[]{:S(2)}) collective-permute-start(f32[512,128]{1,0:T(8,128)} %refs_2_.1), channel_id=1, source_target_pairs={{0,1},{1,0},{2,3},{3,2},{4,5},{5,4},{6,7},{7,6},{8,9},{9,8},{10,11... | collective-permute-start | bytes 786440 | tf_op jit(solution)/shard_map/ppermute | solution.py:201
  50.5 3.7 %query.1.refs_0_ = f32[2,128,192]{2,1,0:T(8,128)S(1)} custom-call(f32[128,2304]{1,0:T(8,128)S(1)} %bitcast.12, f32[192,2304]{1,0:T(8,128)S(1)} %bitcast.14, f32[192,2304]{1,0:T(8,128)} %bitcast.6.other_ref), custom_call_target="tpu_custom_call" | custom-call | tf_op jit(solution)/shard_map/query/pallas_call | solution.py:57
  54.9 1.3 %copy-done.3 = f32[128,2304]{1,0:T(8,128)S(1)} copy-done((f32[128,2304]{1,0:T(8,128)S(1)}, f32[128,2304]{1,0:T(8,128)}, u32[]{:S(2)}) %copy-start.3) | copy-done | bytes 1179672
  56.2 1.6 %out_parts.1.out_w_ref = bf16[2,256,2304]{2,1,0:T(8,128)(2,1)S(1)} custom-call(f32[128,2304]{1,0:T(8,128)S(1)} %copy-done.3, f32[128,2304]{1,0:T(8,128)} %collective-permute-done.9.refs_1_), custom_call_target="tpu_custom_call" | custom-call | tf_op jit(solution)/shard_map/out_parts/pallas_call | solution.py:57
  57.9 2.5 %all-to-all-done.1 = f32[16,5,8,576]{3,2,1,0:T(8,128)} async-done(((f32[16,5,8,576]{3,2,1,0:T(8,128)}), f32[16,5,8,576]{3,2,1,0:T(8,128)}, u32[]{:S(2)}, u32[]{:S(2)}) %all-to-all-start.1) | async-done | bytes 1474592 | tf_op jit(solution)/shard_map/all_to_all | solution.py:212
  60.4 5.9 %attend.1 = (f32[2,128,256]{2,1,0:T(8,128)S(1)}, f32[2,128,256]{2,1,0:T(8,128)S(1)}) custom-call(s32[2]{0:T(128)S(1)} %pad_add_fusion.place_ref, f32[2,128,192]{2,1,0:T(8,128)S(1)} %query.1.refs_0_, f32[2,128,192]{2,1,0:T(8,128)S(1)} %collective-permute-done.1.refs_1_, f32[512,128]{1,0:T(8,128)} %refs_2_.1, f32[512,128]{1,0:T(8,128)} %collective-permute-done.2.refs_3_, ...), custom_call_target="tpu_custom_call" | custom-call | tf_op jit(solution)/shard_map/attend/pallas_call | solution.py:57
  66.3 4.6 %collective-permute-start.12 = (f32[2,128,256]{2,1,0:T(8,128)S(1)}, f32[2,128,256]{2,1,0:T(8,128)S(1)}, u32[]{:S(2)}, u32[]{:S(2)}) collective-permute-start(f32[2,128,256]{2,1,0:T(8,128)S(1)} %get-tuple-element.27), channel_id=1, source_target_pairs={{0,1},{1,0},{2,3},{3,2},{4,5},{5,4},{6,7},{7,6},{8,9},{9,8},{10,11... | collective-permute-start | bytes 786440 | tf_op jit(solution)/shard_map/ppermute | solution.py:201
  70.9 1.2 %collective-permute-done.12.arrived_ref = f32[2,128,256]{2,1,0:T(8,128)S(1)} collective-permute-done((f32[2,128,256]{2,1,0:T(8,128)S(1)}, f32[2,128,256]{2,1,0:T(8,128)S(1)}, u32[]{:S(2)}, u32[]{:S(2)}) %collective-permute-start.12) | collective-permute-done | bytes 262176 | tf_op jit(solution)/shard_map/ppermute | solution.py:201
  72.9 20.7 %all_to_all.15 = f32[16,8,2304]{2,1,0:T(8,128)S(1)} all-to-all(f32[16,8,2304]{2,1,0:T(8,128)S(1)} %bitcast.13), channel_id=1, replica_groups={{0,2,4,6,8,10,12,14,16,18,20,22,24,26,28,30},{1,3,5,7,9,11,13,15,17,19,..., dimensions={0} | all-to-all | bytes 2359296 | tf_op jit(solution)/shard_map/all_to_all | solution.py:212
  (31 shorter events, 5.5 us)
Async XLA Ops:
  0.0 10.3 %copy-start.2 = (f32[2304,192]{0,1:T(8,128)S(1)}, f32[2304,192]{0,1:T(8,128)}, u32[]{:S(2)}) copy-start(f32[2304,192]{0,1:T(8,128)} %param.8) | copy-start | bytes 5308420
  0.0 31.4 %collective-permute-start.9 = (f32[128,2304]{1,0:T(8,128)}, f32[128,2304]{1,0:T(8,128)}, u32[]{:S(2)}, u32[]{:S(2)}) collective-permute-start(f32[128,2304]{1,0:T(8,128)} %refs_0_.3), channel_id=1, source_target_pairs={{0,1},{1,0},{2,3},{3,2},{4,5},{5,4},{6,7},{7,6},{8,9},{9,8},{10,11... | collective-permute-start | bytes 3538952 | tf_op jit(solution)/shard_map/ppermute | solution.py:201
  3.2 0.9 copy-start.4
  4.1 6.7 %copy-start.5 = (f32[8,2304]{1,0:T(8,128)S(1)}, f32[8,2304]{1,0:T(8,128)}, u32[]{:S(2)}) copy-start(f32[8,2304]{1,0:T(8,128)} %x_ref.1) | copy-start | bytes 221188
  4.1 6.7 %copy-start.6 = (f32[512]{0:T(512)S(1)}, f32[512]{0:T(512)}, u32[]{:S(2)}) copy-start(f32[512]{0:T(512)} %param.10) | copy-start | bytes 6148
  5.2 27.4 %all-to-all-start = ((f32[16,1,8,2304]{3,2,1,0:T(8,128)}), f32[16,1,8,2304]{3,2,1,0:T(8,128)S(1)}, u32[]{:S(2)}, u32[]{:S(2)}) async-start(f32[16,1,8,2304]{3,2,1,0:T(8,128)} %copies.1), calls=%async_computation | async-start | bytes 2359296 | tf_op jit(solution)/shard_map/all_to_all | solution.py:212
  10.3 40.2 %collective-permute-start = (f32[2304,192]{0,1:T(8,128)S(1)}, f32[2304,192]{0,1:T(8,128)}, u32[]{:S(2)}, u32[]{:S(2)}) collective-permute-start(f32[2304,192]{0,1:T(8,128)S(1)} %copy-done.2), channel_id=1, source_target_pairs={{0,1},{1,0},{2,3},{3,2},{4,5},{5,4},{6,7},{7,6},{8,9},{9,8},{10,11... | collective-permute-start | bytes 5308424 | tf_op jit(solution)/shard_map/ppermute | solution.py:201
  10.8 2.5 %copy-start = (f32[2304,576]{0,1:T(8,128)S(1)}, f32[2304,576]{0,1:T(8,128)}, u32[]{:S(2)}) copy-start(f32[2304,576]{0,1:T(8,128)} %param.9) | copy-start | bytes 15925252
  15.2 8.7 %collective-permute-start.4 = (f32[8,576]{1,0:T(8,128)S(1)}, f32[8,576]{1,0:T(8,128)S(1)}, u32[]{:S(2)}, u32[]{:S(2)}) collective-permute-start(f32[8,576]{1,0:T(8,128)S(1)} %own_latent.1), channel_id=1, source_target_pairs={{0,64},{32,96},{64,128},{96,160},{128,192},{160,224},{192,0},{224,... | collective-permute-start | bytes 55304 | tf_op jit(solution)/shard_map/ppermute | solution.py:206
  18.2 9.6 %collective-permute-start.5 = (f32[8,576]{1,0:T(8,128)S(1)}, f32[8,576]{1,0:T(8,128)S(1)}, u32[]{:S(2)}, u32[]{:S(2)}) collective-permute-start(f32[8,576]{1,0:T(8,128)S(1)} %own_latent.1), channel_id=1, source_target_pairs={{0,96},{32,128},{64,160},{96,192},{128,224},{160,0},{192,32},{224,... | collective-permute-start | bytes 55304 | tf_op jit(solution)/shard_map/ppermute | solution.py:206
  22.9 7.3 %collective-permute-start.6 = (f32[8,576]{1,0:T(8,128)S(1)}, f32[8,576]{1,0:T(8,128)S(1)}, u32[]{:S(2)}, u32[]{:S(2)}) collective-permute-start(f32[8,576]{1,0:T(8,128)S(1)} %own_latent.1), channel_id=1, source_target_pairs={{0,128},{32,160},{64,192},{96,224},{128,0},{160,32},{192,64},{224,... | collective-permute-start | bytes 55304 | tf_op jit(solution)/shard_map/ppermute | solution.py:206
  23.9 6.3 %collective-permute-start.7 = (f32[8,576]{1,0:T(8,128)S(1)}, f32[8,576]{1,0:T(8,128)S(1)}, u32[]{:S(2)}, u32[]{:S(2)}) collective-permute-start(f32[8,576]{1,0:T(8,128)S(1)} %own_latent.1), channel_id=1, source_target_pairs={{0,160},{32,192},{64,224},{96,0},{128,32},{160,64},{192,96},{224,1... | collective-permute-start | bytes 55304 | tf_op jit(solution)/shard_map/ppermute | solution.py:206
  27.8 3.6 %collective-permute-start.8 = (f32[8,576]{1,0:T(8,128)S(1)}, f32[8,576]{1,0:T(8,128)S(1)}, u32[]{:S(2)}, u32[]{:S(2)}) collective-permute-start(f32[8,576]{1,0:T(8,128)S(1)} %own_latent.1), channel_id=1, source_target_pairs={{0,192},{32,224},{64,0},{96,32},{128,64},{160,96},{192,128},{224,1... | collective-permute-start | bytes 55304 | tf_op jit(solution)/shard_map/ppermute | solution.py:206
  32.7 27.7 %all-to-all-start.1 = ((f32[16,5,8,576]{3,2,1,0:T(8,128)}), f32[16,5,8,576]{3,2,1,0:T(8,128)}, u32[]{:S(2)}, u32[]{:S(2)}) async-start(f32[16,5,8,576]{3,2,1,0:T(8,128)} %far_copies.1), calls=%async_computation.1 | async-start | bytes 3276800 | tf_op jit(solution)/shard_map/all_to_all | solution.py:212
  39.6 2.5 %copy-start.1 = (f32[2304,576]{0,1:T(8,128)S(1)}, f32[2304,576]{0,1:T(8,128)}, u32[]{:S(2)}) copy-start(f32[2304,576]{0,1:T(8,128)} %param.9) | copy-start | bytes 15925252
  44.6 13.2 %collective-permute-start.10 = (f32[128,576]{1,0:T(8,128)S(1)}, f32[128,576]{1,0:T(8,128)}, u32[]{:S(2)}, u32[]{:S(2)}) collective-permute-start(f32[128,576]{1,0:T(8,128)S(1)} %latent.1.refs_6_), channel_id=1, source_target_pairs={{0,32},{32,64},{64,96},{96,128},{128,160},{160,192},{192,224},{224... | collective-permute-start | bytes 884744 | tf_op jit(solution)/shard_map/ppermute | solution.py:206
  45.4 12.4 %collective-permute-start.11 = (f32[128,576]{1,0:T(8,128)S(1)}, f32[128,576]{1,0:T(8,128)}, u32[]{:S(2)}, u32[]{:S(2)}) collective-permute-start(f32[128,576]{1,0:T(8,128)S(1)} %latent.1.refs_6_), channel_id=1, source_target_pairs={{0,224},{32,0},{64,32},{96,64},{128,96},{160,128},{192,160},{224,1... | collective-permute-start | bytes 884744 | tf_op jit(solution)/shard_map/ppermute | solution.py:206
  47.4 10.5 %collective-permute-start.2 = (f32[512,128]{1,0:T(8,128)}, f32[512,128]{1,0:T(8,128)}, u32[]{:S(2)}, u32[]{:S(2)}) collective-permute-start(f32[512,128]{1,0:T(8,128)} %refs_2_.1), channel_id=1, source_target_pairs={{0,1},{1,0},{2,3},{3,2},{4,5},{5,4},{6,7},{7,6},{8,9},{9,8},{10,11... | collective-permute-start | bytes 786440 | tf_op jit(solution)/shard_map/ppermute | solution.py:201
  50.5 7.3 %collective-permute-start.3 = (f32[512,128]{1,0:T(8,128)}, f32[512,128]{1,0:T(8,128)}, u32[]{:S(2)}, u32[]{:S(2)}) collective-permute-start(f32[512,128]{1,0:T(8,128)} %refs_4_.1), channel_id=1, source_target_pairs={{0,1},{1,0},{2,3},{3,2},{4,5},{5,4},{6,7},{7,6},{8,9},{9,8},{10,11... | collective-permute-start | bytes 786440 | tf_op jit(solution)/shard_map/ppermute | solution.py:201
  54.3 3.6 %collective-permute-start.1 = (f32[2,128,192]{2,1,0:T(8,128)S(1)}, f32[2,128,192]{2,1,0:T(8,128)S(1)}, u32[]{:S(2)}, u32[]{:S(2)}) collective-permute-start(f32[2,128,192]{2,1,0:T(8,128)S(1)} %query.1.refs_0_), channel_id=1, source_target_pairs={{0,1},{1,0},{2,3},{3,2},{4,5},{5,4},{6,7},{7,6},{8,9},{9,8},{10,11... | collective-permute-start | bytes 589832 | tf_op jit(solution)/shard_map/ppermute | solution.py:201
  54.9 1.3 %copy-start.3 = (f32[128,2304]{1,0:T(8,128)S(1)}, f32[128,2304]{1,0:T(8,128)}, u32[]{:S(2)}) copy-start(f32[128,2304]{1,0:T(8,128)} %refs_0_.3) | copy-start | bytes 3538948
  66.3 5.8 %collective-permute-start.12 = (f32[2,128,256]{2,1,0:T(8,128)S(1)}, f32[2,128,256]{2,1,0:T(8,128)S(1)}, u32[]{:S(2)}, u32[]{:S(2)}) collective-permute-start(f32[2,128,256]{2,1,0:T(8,128)S(1)} %get-tuple-element.27), channel_id=1, source_target_pairs={{0,1},{1,0},{2,3},{3,2},{4,5},{5,4},{6,7},{7,6},{8,9},{9,8},{10,11... | collective-permute-start | bytes 786440 | tf_op jit(solution)/shard_map/ppermute | solution.py:201

commit v7 on v6

--- a/solution.py
+++ b/solution.py
@@ -243,7 +243,7 @@
     far_latent = exchange(far_copies).reshape(-1, width)
 
     latent = call(latent_kernel, shape(half, width), [mine, w_down.T, gain], "latent")
-    ring = [from_behind(latent, step) for step in RING]
+    ring = [from_behind(latent, 1), lax.ppermute(latent, "ctx", [(0, blocks - 1)])]
 
     mine, far_query, _ = lax.optimization_barrier((mine, far_query, latent))
     queries = call(

time: 94.8 us -> 95 us (level)
  waiting for transfers between devices: 4.85 us -> 2.36 us
  starting transfers between devices: 41.9 us -> 44.3 us
    ppermute x0 -> x1, starting transfers between devices: none -> 4.55 us  [on_device(): lax.ppermute(latent, 'ctx', [(0, blocks - 1)])]
    all_to_all x2, waiting for transfers between devices: 2.5 us -> 0.01 us  [exchange(): lax.all_to_all(pieces, 'head', split_axis=0, concat_axis=0, tiled=True, a...]
    ppermute x7 -> x6, starting transfers between devices: 17.8 us -> 15.9 us  [from_behind(): lax.ppermute(array, 'ctx', [(c, (c + step) % size) for c in range(size)])]
  transfers between devices with their start and end apart: 15 -> 15, of which waited for: 3 -> 2; matrix products, arithmetic and copies ran while one was open for 0% -> 0% of each run, Pallas kernels for 13% -> 13%
where the time goes in v7:
time: 95 us; the launch traced here: 94.5 us
  starting transfers between devices  44.3 us (47%)
  blocking collectives  20.8 us (22%)
  Pallas kernels  18.9 us (20%)
  local copies, waits for them, and re-layouts  7.17 us (8%)
  waiting for transfers between devices  2.36 us (2%)
    all_to_all x1, blocking collectives, exchange(): lax.all_to_all(pieces, 'head', split_axis=0, concat_axis=0, tiled=True, a...  20.8 us
    pallas_call x8, Pallas kernels, call(): pl.pallas_call(kernel, out_shape=outs, in_specs=[pl.BlockSpec(memory_spac...  18.9 us
    ppermute x6, starting transfers between devices, from_behind(): lax.ppermute(array, 'ctx', [(c, (c + step) % size) for c in range(size)])  15.9 us
    ppermute x6, starting transfers between devices, partner(): return lax.ppermute(array, 'head', [(h, h ^ 1) for h in range(size)])  12 us
    all_to_all x2, starting transfers between devices, exchange(): lax.all_to_all(pieces, 'head', split_axis=0, concat_axis=0, tiled=True, a...  12 us
    unnamed x14, local copies, waits for them, and re-layouts  7.17 us
    ppermute x1, starting transfers between devices, on_device(): lax.ppermute(latent, 'ctx', [(0, blocks - 1)])  4.55 us
  transfers between devices with their start and end apart: 15, of which 2 were waited for; matrix products, arithmetic and copies ran while one was open for 0% of the time, Pallas kernels for 13%

profile of v7, /device:TPU:1, one launch (start us, length us, event | category | flops | bytes accessed | tf_op | source)
XLA Modules:
  0.0 94.5 jit_solution(14044141046604053683)
XLA Ops:
  0.0 3.2 %collective-permute-start.9 = (f32[128,2304]{1,0:T(8,128)}, f32[128,2304]{1,0:T(8,128)}, u32[]{:S(2)}, u32[]{:S(2)}) collective-permute-start(f32[128,2304]{1,0:T(8,128)} %refs_0_.3), channel_id=1, source_target_pairs={{0,1},{1,0},{2,3},{3,2},{4,5},{5,4},{6,7},{7,6},{8,9},{9,8},{10,11... | collective-permute-start | bytes 3538952 | tf_op jit(solution)/shard_map/ppermute | solution.py:201
  4.1 1.1 %copies.1 = f32[16,1,8,2304]{3,2,1,0:T(8,128)} custom-call(f32[8,2304]{1,0:T(8,128)S(1)} %copy-done.4), custom_call_target="tpu_custom_call" | custom-call | tf_op jit(solution)/shard_map/copies/pallas_call | solution.py:57
  5.2 5.0 %all-to-all-start = ((f32[16,1,8,2304]{3,2,1,0:T(8,128)}), f32[16,1,8,2304]{3,2,1,0:T(8,128)S(1)}, u32[]{:S(2)}, u32[]{:S(2)}) async-start(f32[16,1,8,2304]{3,2,1,0:T(8,128)} %copies.1), calls=%async_computation | async-start | bytes 2359296 | tf_op jit(solution)/shard_map/all_to_all | solution.py:212
  10.8 2.5 %copy-done = f32[2304,576]{0,1:T(8,128)S(1)} copy-done((f32[2304,576]{0,1:T(8,128)S(1)}, f32[2304,576]{0,1:T(8,128)}, u32[]{:S(2)}) %copy-start) | copy-done | bytes 5308440
  13.3 1.9 %own_latent.1 = f32[8,576]{1,0:T(8,128)S(1)} custom-call(f32[8,2304]{1,0:T(8,128)S(1)} %copy-done.5, f32[576,2304]{1,0:T(8,128)S(1)} %bitcast.9, f32[1,512]{1,0:T(1,128)S(1)} %bitcast.15), custom_call_target="tpu_custom_call" | custom-call | tf_op jit(solution)/shard_map/own_latent/pallas_call | solution.py:57
  15.2 3.1 %collective-permute-start.4 = (f32[8,576]{1,0:T(8,128)S(1)}, f32[8,576]{1,0:T(8,128)S(1)}, u32[]{:S(2)}, u32[]{:S(2)}) collective-permute-start(f32[8,576]{1,0:T(8,128)S(1)} %own_latent.1), channel_id=1, source_target_pairs={{0,64},{32,96},{64,128},{96,160},{128,192},{160,224},{192,0},{224,... | collective-permute-start | bytes 55304 | tf_op jit(solution)/shard_map/ppermute | solution.py:206
  18.2 4.6 %collective-permute-start.5 = (f32[8,576]{1,0:T(8,128)S(1)}, f32[8,576]{1,0:T(8,128)S(1)}, u32[]{:S(2)}, u32[]{:S(2)}) collective-permute-start(f32[8,576]{1,0:T(8,128)S(1)} %own_latent.1), channel_id=1, source_target_pairs={{0,96},{32,128},{64,160},{96,192},{128,224},{160,0},{192,32},{224,... | collective-permute-start | bytes 55304 | tf_op jit(solution)/shard_map/ppermute | solution.py:206
  22.9 1.0 %collective-permute-start.6 = (f32[8,576]{1,0:T(8,128)S(1)}, f32[8,576]{1,0:T(8,128)S(1)}, u32[]{:S(2)}, u32[]{:S(2)}) collective-permute-start(f32[8,576]{1,0:T(8,128)S(1)} %own_latent.1), channel_id=1, source_target_pairs={{0,128},{32,160},{64,192},{96,224},{128,0},{160,32},{192,64},{224,... | collective-permute-start | bytes 55304 | tf_op jit(solution)/shard_map/ppermute | solution.py:206
  23.9 3.9 %collective-permute-start.7 = (f32[8,576]{1,0:T(8,128)S(1)}, f32[8,576]{1,0:T(8,128)S(1)}, u32[]{:S(2)}, u32[]{:S(2)}) collective-permute-start(f32[8,576]{1,0:T(8,128)S(1)} %own_latent.1), channel_id=1, source_target_pairs={{0,160},{32,192},{64,224},{96,0},{128,32},{160,64},{192,96},{224,1... | collective-permute-start | bytes 55304 | tf_op jit(solution)/shard_map/ppermute | solution.py:206
  27.8 2.4 %collective-permute-start.8 = (f32[8,576]{1,0:T(8,128)S(1)}, f32[8,576]{1,0:T(8,128)S(1)}, u32[]{:S(2)}, u32[]{:S(2)}) collective-permute-start(f32[8,576]{1,0:T(8,128)S(1)} %own_latent.1), channel_id=1, source_target_pairs={{0,192},{32,224},{64,0},{96,32},{128,64},{160,96},{192,128},{224,1... | collective-permute-start | bytes 55304 | tf_op jit(solution)/shard_map/ppermute | solution.py:206
  30.2 1.2 %collective-permute-done.8.refs_4_ = f32[8,576]{1,0:T(8,128)S(1)} collective-permute-done((f32[8,576]{1,0:T(8,128)S(1)}, f32[8,576]{1,0:T(8,128)S(1)}, u32[]{:S(2)}, u32[]{:S(2)}) %collective-permute-start.8) | collective-permute-done | bytes 18464 | tf_op jit(solution)/shard_map/ppermute | solution.py:206
  31.4 1.3 %far_copies.1 = f32[16,5,8,576]{3,2,1,0:T(8,128)} custom-call(f32[8,576]{1,0:T(8,128)S(1)} %collective-permute-done.4.refs_0_, f32[8,576]{1,0:T(8,128)S(1)} %collective-permute-done.5.refs_1_, f32[8,576]{1,0:T(8,128)S(1)} %collective-permute-done.6.refs_2_, f32[8,576]{1,0:T(8,128)S(1)} %collective-permute-done.7.refs_3_, ...), custom_call_target="tpu_custom_call" | custom-call | tf_op jit(solution)/shard_map/far_copies/pallas_call | solution.py:57
  32.7 6.9 %all-to-all-start.1 = ((f32[16,5,8,576]{3,2,1,0:T(8,128)}), f32[16,5,8,576]{3,2,1,0:T(8,128)}, u32[]{:S(2)}, u32[]{:S(2)}) async-start(f32[16,5,8,576]{3,2,1,0:T(8,128)} %far_copies.1), calls=%async_computation.1 | async-start | bytes 3276800 | tf_op jit(solution)/shard_map/all_to_all | solution.py:212
  39.6 2.5 %copy-done.1 = f32[2304,576]{0,1:T(8,128)S(1)} copy-done((f32[2304,576]{0,1:T(8,128)S(1)}, f32[2304,576]{0,1:T(8,128)}, u32[]{:S(2)}) %copy-start.1) | copy-done | bytes 5308440
  42.1 2.5 %latent.1.refs_6_ = f32[128,576]{1,0:T(8,128)S(1)} custom-call(f32[128,2304]{1,0:T(8,128)S(1)} %bitcast.11, f32[576,2304]{1,0:T(8,128)S(1)} %bitcast.10, f32[1,512]{1,0:T(1,128)S(1)} %bitcast.16), custom_call_target="tpu_custom_call" | custom-call | tf_op jit(solution)/shard_map/latent/pallas_call | solution.py:57
  45.4 4.5 %collective-permute-start.11 = (f32[128,576]{1,0:T(8,128)S(1)}, f32[128,576]{1,0:T(8,128)}, u32[]{:S(2)}, u32[]{:S(2)}) collective-permute-start(f32[128,576]{1,0:T(8,128)S(1)} %latent.1.refs_6_), channel_id=1, source_target_pairs={{0,224},{1,225},{2,226},{3,227},{4,228},{5,229},{6,230},{7,231},{8... | collective-permute-start | bytes 884744 | tf_op jit(solution)/shard_map/ppermute | solution.py:246
  50.0 3.1 %collective-permute-start.2 = (f32[512,128]{1,0:T(8,128)}, f32[512,128]{1,0:T(8,128)}, u32[]{:S(2)}, u32[]{:S(2)}) collective-permute-start(f32[512,128]{1,0:T(8,128)} %refs_2_.1), channel_id=1, source_target_pairs={{0,1},{1,0},{2,3},{3,2},{4,5},{5,4},{6,7},{7,6},{8,9},{9,8},{10,11... | collective-permute-start | bytes 786440 | tf_op jit(solution)/shard_map/ppermute | solution.py:201
  53.1 3.7 %query.1.refs_0_ = f32[2,128,192]{2,1,0:T(8,128)S(1)} custom-call(f32[128,2304]{1,0:T(8,128)S(1)} %bitcast.12, f32[192,2304]{1,0:T(8,128)S(1)} %bitcast.14, f32[192,2304]{1,0:T(8,128)} %bitcast.6.other_ref), custom_call_target="tpu_custom_call" | custom-call | tf_op jit(solution)/shard_map/query/pallas_call | solution.py:57
  57.6 1.3 %copy-done.3 = f32[128,2304]{1,0:T(8,128)S(1)} copy-done((f32[128,2304]{1,0:T(8,128)S(1)}, f32[128,2304]{1,0:T(8,128)}, u32[]{:S(2)}) %copy-start.3) | copy-done | bytes 1179672
  58.8 1.6 %out_parts.1.out_w_ref = bf16[2,256,2304]{2,1,0:T(8,128)(2,1)S(1)} custom-call(f32[128,2304]{1,0:T(8,128)S(1)} %copy-done.3, f32[128,2304]{1,0:T(8,128)} %collective-permute-done.9.refs_1_), custom_call_target="tpu_custom_call" | custom-call | tf_op jit(solution)/shard_map/out_parts/pallas_call | solution.py:57
  60.5 5.9 %attend.1 = (f32[2,128,256]{2,1,0:T(8,128)S(1)}, f32[2,128,256]{2,1,0:T(8,128)S(1)}) custom-call(s32[2]{0:T(128)S(1)} %pad_add_fusion.place_ref, f32[2,128,192]{2,1,0:T(8,128)S(1)} %query.1.refs_0_, f32[2,128,192]{2,1,0:T(8,128)S(1)} %collective-permute-done.1.refs_1_, f32[512,128]{1,0:T(8,128)} %refs_2_.1, f32[512,128]{1,0:T(8,128)} %collective-permute-done.2.refs_3_, ...), custom_call_target="tpu_custom_call" | custom-call | tf_op jit(solution)/shard_map/attend/pallas_call | solution.py:57
  66.4 4.5 %collective-permute-start.12 = (f32[2,128,256]{2,1,0:T(8,128)S(1)}, f32[2,128,256]{2,1,0:T(8,128)S(1)}, u32[]{:S(2)}, u32[]{:S(2)}) collective-permute-start(f32[2,128,256]{2,1,0:T(8,128)S(1)} %get-tuple-element.27), channel_id=1, source_target_pairs={{0,1},{1,0},{2,3},{3,2},{4,5},{5,4},{6,7},{7,6},{8,9},{9,8},{10,11... | collective-permute-start | bytes 786440 | tf_op jit(solution)/shard_map/ppermute | solution.py:201
  70.9 1.2 %collective-permute-done.12.arrived_ref = f32[2,128,256]{2,1,0:T(8,128)S(1)} collective-permute-done((f32[2,128,256]{2,1,0:T(8,128)S(1)}, f32[2,128,256]{2,1,0:T(8,128)S(1)}, u32[]{:S(2)}, u32[]{:S(2)}) %collective-permute-start.12) | collective-permute-done | bytes 262176 | tf_op jit(solution)/shard_map/ppermute | solution.py:201
  72.9 20.8 %all_to_all.15 = f32[16,8,2304]{2,1,0:T(8,128)S(1)} all-to-all(f32[16,8,2304]{2,1,0:T(8,128)S(1)} %bitcast.13), channel_id=1, replica_groups={{0,2,4,6,8,10,12,14,16,18,20,22,24,26,28,30},{1,3,5,7,9,11,13,15,17,19,..., dimensions={0} | all-to-all | bytes 2359296 | tf_op jit(solution)/shard_map/all_to_all | solution.py:212
  (31 shorter events, 4.5 us)
Async XLA Ops:
  0.0 10.3 %copy-start.2 = (f32[2304,192]{0,1:T(8,128)S(1)}, f32[2304,192]{0,1:T(8,128)}, u32[]{:S(2)}) copy-start(f32[2304,192]{0,1:T(8,128)} %param.8) | copy-start | bytes 5308420
  0.0 31.4 %collective-permute-start.9 = (f32[128,2304]{1,0:T(8,128)}, f32[128,2304]{1,0:T(8,128)}, u32[]{:S(2)}, u32[]{:S(2)}) collective-permute-start(f32[128,2304]{1,0:T(8,128)} %refs_0_.3), channel_id=1, source_target_pairs={{0,1},{1,0},{2,3},{3,2},{4,5},{5,4},{6,7},{7,6},{8,9},{9,8},{10,11... | collective-permute-start | bytes 3538952 | tf_op jit(solution)/shard_map/ppermute | solution.py:201
  3.2 0.9 copy-start.4
  4.1 6.7 %copy-start.5 = (f32[8,2304]{1,0:T(8,128)S(1)}, f32[8,2304]{1,0:T(8,128)}, u32[]{:S(2)}) copy-start(f32[8,2304]{1,0:T(8,128)} %x_ref.1) | copy-start | bytes 221188
  4.1 6.7 %copy-start.6 = (f32[512]{0:T(512)S(1)}, f32[512]{0:T(512)}, u32[]{:S(2)}) copy-start(f32[512]{0:T(512)} %param.10) | copy-start | bytes 6148
  5.2 27.4 %all-to-all-start = ((f32[16,1,8,2304]{3,2,1,0:T(8,128)}), f32[16,1,8,2304]{3,2,1,0:T(8,128)S(1)}, u32[]{:S(2)}, u32[]{:S(2)}) async-start(f32[16,1,8,2304]{3,2,1,0:T(8,128)} %copies.1), calls=%async_computation | async-start | bytes 2359296 | tf_op jit(solution)/shard_map/all_to_all | solution.py:212
  10.3 42.9 %collective-permute-start = (f32[2304,192]{0,1:T(8,128)S(1)}, f32[2304,192]{0,1:T(8,128)}, u32[]{:S(2)}, u32[]{:S(2)}) collective-permute-start(f32[2304,192]{0,1:T(8,128)S(1)} %copy-done.2), channel_id=1, source_target_pairs={{0,1},{1,0},{2,3},{3,2},{4,5},{5,4},{6,7},{7,6},{8,9},{9,8},{10,11... | collective-permute-start | bytes 5308424 | tf_op jit(solution)/shard_map/ppermute | solution.py:201
  10.8 2.5 %copy-start = (f32[2304,576]{0,1:T(8,128)S(1)}, f32[2304,576]{0,1:T(8,128)}, u32[]{:S(2)}) copy-start(f32[2304,576]{0,1:T(8,128)} %param.9) | copy-start | bytes 15925252
  15.2 8.7 %collective-permute-start.4 = (f32[8,576]{1,0:T(8,128)S(1)}, f32[8,576]{1,0:T(8,128)S(1)}, u32[]{:S(2)}, u32[]{:S(2)}) collective-permute-start(f32[8,576]{1,0:T(8,128)S(1)} %own_latent.1), channel_id=1, source_target_pairs={{0,64},{32,96},{64,128},{96,160},{128,192},{160,224},{192,0},{224,... | collective-permute-start | bytes 55304 | tf_op jit(solution)/shard_map/ppermute | solution.py:206
  18.2 9.6 %collective-permute-start.5 = (f32[8,576]{1,0:T(8,128)S(1)}, f32[8,576]{1,0:T(8,128)S(1)}, u32[]{:S(2)}, u32[]{:S(2)}) collective-permute-start(f32[8,576]{1,0:T(8,128)S(1)} %own_latent.1), channel_id=1, source_target_pairs={{0,96},{32,128},{64,160},{96,192},{128,224},{160,0},{192,32},{224,... | collective-permute-start | bytes 55304 | tf_op jit(solution)/shard_map/ppermute | solution.py:206
  22.9 7.3 %collective-permute-start.6 = (f32[8,576]{1,0:T(8,128)S(1)}, f32[8,576]{1,0:T(8,128)S(1)}, u32[]{:S(2)}, u32[]{:S(2)}) collective-permute-start(f32[8,576]{1,0:T(8,128)S(1)} %own_latent.1), channel_id=1, source_target_pairs={{0,128},{32,160},{64,192},{96,224},{128,0},{160,32},{192,64},{224,... | collective-permute-start | bytes 55304 | tf_op jit(solution)/shard_map/ppermute | solution.py:206
  23.9 6.3 %collective-permute-start.7 = (f32[8,576]{1,0:T(8,128)S(1)}, f32[8,576]{1,0:T(8,128)S(1)}, u32[]{:S(2)}, u32[]{:S(2)}) collective-permute-start(f32[8,576]{1,0:T(8,128)S(1)} %own_latent.1), channel_id=1, source_target_pairs={{0,160},{32,192},{64,224},{96,0},{128,32},{160,64},{192,96},{224,1... | collective-permute-start | bytes 55304 | tf_op jit(solution)/shard_map/ppermute | solution.py:206
  27.8 3.6 %collective-permute-start.8 = (f32[8,576]{1,0:T(8,128)S(1)}, f32[8,576]{1,0:T(8,128)S(1)}, u32[]{:S(2)}, u32[]{:S(2)}) collective-permute-start(f32[8,576]{1,0:T(8,128)S(1)} %own_latent.1), channel_id=1, source_target_pairs={{0,192},{32,224},{64,0},{96,32},{128,64},{160,96},{192,128},{224,1... | collective-permute-start | bytes 55304 | tf_op jit(solution)/shard_map/ppermute | solution.py:206
  32.7 27.8 %all-to-all-start.1 = ((f32[16,5,8,576]{3,2,1,0:T(8,128)}), f32[16,5,8,576]{3,2,1,0:T(8,128)}, u32[]{:S(2)}, u32[]{:S(2)}) async-start(f32[16,5,8,576]{3,2,1,0:T(8,128)} %far_copies.1), calls=%async_computation.1 | async-start | bytes 3276800 | tf_op jit(solution)/shard_map/all_to_all | solution.py:212
  39.6 2.5 %copy-start.1 = (f32[2304,576]{0,1:T(8,128)S(1)}, f32[2304,576]{0,1:T(8,128)}, u32[]{:S(2)}) copy-start(f32[2304,576]{0,1:T(8,128)} %param.9) | copy-start | bytes 15925252
  44.6 15.8 %collective-permute-start.10 = (f32[128,576]{1,0:T(8,128)S(1)}, f32[128,576]{1,0:T(8,128)}, u32[]{:S(2)}, u32[]{:S(2)}) collective-permute-start(f32[128,576]{1,0:T(8,128)S(1)} %latent.1.refs_6_), channel_id=1, source_target_pairs={{0,32},{32,64},{64,96},{96,128},{128,160},{160,192},{192,224},{224... | collective-permute-start | bytes 884744 | tf_op jit(solution)/shard_map/ppermute | solution.py:206
  45.4 15.0 %collective-permute-start.11 = (f32[128,576]{1,0:T(8,128)S(1)}, f32[128,576]{1,0:T(8,128)}, u32[]{:S(2)}, u32[]{:S(2)}) collective-permute-start(f32[128,576]{1,0:T(8,128)S(1)} %latent.1.refs_6_), channel_id=1, source_target_pairs={{0,224},{1,225},{2,226},{3,227},{4,228},{5,229},{6,230},{7,231},{8... | collective-permute-start | bytes 884744 | tf_op jit(solution)/shard_map/ppermute | solution.py:246
  50.0 10.4 %collective-permute-start.2 = (f32[512,128]{1,0:T(8,128)}, f32[512,128]{1,0:T(8,128)}, u32[]{:S(2)}, u32[]{:S(2)}) collective-permute-start(f32[512,128]{1,0:T(8,128)} %refs_2_.1), channel_id=1, source_target_pairs={{0,1},{1,0},{2,3},{3,2},{4,5},{5,4},{6,7},{7,6},{8,9},{9,8},{10,11... | collective-permute-start | bytes 786440 | tf_op jit(solution)/shard_map/ppermute | solution.py:201
  53.1 7.3 %collective-permute-start.3 = (f32[512,128]{1,0:T(8,128)}, f32[512,128]{1,0:T(8,128)}, u32[]{:S(2)}, u32[]{:S(2)}) collective-permute-start(f32[512,128]{1,0:T(8,128)} %refs_4_.1), channel_id=1, source_target_pairs={{0,1},{1,0},{2,3},{3,2},{4,5},{5,4},{6,7},{7,6},{8,9},{9,8},{10,11... | collective-permute-start | bytes 786440 | tf_op jit(solution)/shard_map/ppermute | solution.py:201
  56.9 3.6 %collective-permute-start.1 = (f32[2,128,192]{2,1,0:T(8,128)S(1)}, f32[2,128,192]{2,1,0:T(8,128)S(1)}, u32[]{:S(2)}, u32[]{:S(2)}) collective-permute-start(f32[2,128,192]{2,1,0:T(8,128)S(1)} %query.1.refs_0_), channel_id=1, source_target_pairs={{0,1},{1,0},{2,3},{3,2},{4,5},{5,4},{6,7},{7,6},{8,9},{9,8},{10,11... | collective-permute-start | bytes 589832 | tf_op jit(solution)/shard_map/ppermute | solution.py:201
  57.6 1.3 %copy-start.3 = (f32[128,2304]{1,0:T(8,128)S(1)}, f32[128,2304]{1,0:T(8,128)}, u32[]{:S(2)}) copy-start(f32[128,2304]{1,0:T(8,128)} %refs_0_.3) | copy-start | bytes 3538948
  66.4 5.6 %collective-permute-start.12 = (f32[2,128,256]{2,1,0:T(8,128)S(1)}, f32[2,128,256]{2,1,0:T(8,128)S(1)}, u32[]{:S(2)}, u32[]{:S(2)}) collective-permute-start(f32[2,128,256]{2,1,0:T(8,128)S(1)} %get-tuple-element.27), channel_id=1, source_target_pairs={{0,1},{1,0},{2,3},{3,2},{4,5},{5,4},{6,7},{7,6},{8,9},{9,8},{10,11... | collective-permute-start | bytes 786440 | tf_op jit(solution)/shard_map/ppermute | solution.py:201
